TPU v7x, 512 devices: a whole 4x4x16 slice. The times are simulated.
512 devices in a mesh: section: 8 (over z_lo), dp: 32 (over x, y, core), tensor: 2 (over z_hi).
Axes of the slice: x: 4, y: 4, z: 16 (z_hi: 2, z_lo: 8; z = z_hi * 8 + z_lo), core: 2. Of those that a mesh axis runs over, the one named last changes fastest.
Arguments:
- hidden_in: bfloat16 [8, 4096, 8192], P('section', ('dp', 'tensor')), may hold values from -600 to 600
- norm_gain: bfloat16 [8, 8192], P('section'), may hold values from 0.5 to 1.5
- value_weight: bfloat16 [8, 8192, 512], P('section', 'dp', 'tensor'), may hold values from -0.0625 to 0.0625
- query_vectors: bfloat16 [8, 4096, 4096], P('section', 'dp', 'tensor'), may hold values from -9 to 9
- key_vectors: bfloat16 [8, 4096, 512], P('section', 'dp', 'tensor'), may hold values from -9 to 9
- grad_attn: bfloat16 [8, 4096, 4096], P('section', 'dp', 'tensor'), may hold values from -250 to 250
- positions: int32 [8, 4096], P('section', 'dp'), may hold values from 0 to 65535, as said below
Outputs:
- value_weight_grad: float32 [8, 8192, 512], P('section', 'dp', 'tensor')
- norm_gain_grad: float32 [8, 8192], P('section')
- to_previous: bfloat16 [8, 4096, 8192], P('section', ('dp', 'tensor'))
Inputs may be any that keep to these rules, and one draw needn't show every extreme that they name: Within each micro-batch of 128 rows, positions rise by one from row to row except at one row between row 32 and row 95, where a new document starts at position 0.
All inputs are finite; a program needn't handle non-finite values.
Results may differ from a plain program's by a relative error of at most 0.014.
Values may be sent and summed in bfloat16 or wider, within the bound.
No kernel may reach another device: no remote copies, remote signals or barrier semaphores. Data moves between devices by JAX's collectives and lax.ppermute only.
A program may use at most 64 MiB of HBM per device.

v0:
```python
import math

import jax
import jax.numpy as jnp
from jax import lax
from jax.sharding import PartitionSpec as P

HD = 128
QPK = 8


def shifted(value, axis, steps):
    count = lax.axis_size(axis)
    first, last = (max(0, -steps), min(count, count - steps))
    return lax.ppermute(value, axis, [(source, source + steps) for source in range(first, last)])


def attend(query_rows, key_rows, grad_rows, position_rows):
    length = query_rows.shape[0]
    groups = key_rows.shape[1] // HD
    query_heads = query_rows.reshape(length, groups, QPK, HD)
    key_heads = key_rows.reshape(length, groups, HD)
    grad_heads = grad_rows.reshape(length, groups, QPK, HD)
    scores = jnp.einsum(
        "igpd,jgd->gpij", query_heads, key_heads, preferred_element_type=jnp.float32
    ) / math.sqrt(HD)
    places = jnp.arange(length, dtype=jnp.int32)
    visible = (places[:, None] >= places[None, :]) & (
        position_rows[:, None] - position_rows[None, :] == places[:, None] - places[None, :]
    )
    masked = jnp.where(visible, scores, jnp.float32(-1e30))
    largest = jnp.max(masked, axis=-1, keepdims=True)
    powers = jnp.where(visible, jnp.exp(masked - largest), jnp.float32(0.0))
    probabilities = powers / jnp.sum(powers, axis=-1, keepdims=True)
    weights = probabilities.astype(jnp.bfloat16)
    value_grad = jnp.einsum(
        "gpij,igpd->jgd", weights, grad_heads, preferred_element_type=jnp.float32
    )
    return value_grad.reshape(length, groups * HD).astype(jnp.bfloat16)


def shards(hidden_in, norm_gain, value_weight, query_vectors, key_vectors, grad_attn, positions):
    rows_float = hidden_in[0].astype(jnp.float32)
    root_mean = jnp.sqrt(jnp.mean(rows_float * rows_float, axis=1, keepdims=True) + 1e-05)
    normed = rows_float / root_mean
    gain_float = norm_gain[0].astype(jnp.float32)
    own_input = (normed * gain_float).astype(jnp.bfloat16)
    layer_input = lax.all_gather(own_input, "tensor", axis=0, tiled=True)
    value_grad = attend(query_vectors[0], key_vectors[0], grad_attn[0], positions[0])
    local_weight = value_weight[0]
    weight_grad = lax.psum_scatter(
        jnp.einsum("tc,tk->ck", layer_input, value_grad, preferred_element_type=jnp.float32).astype(
            jnp.bfloat16
        ),
        "dp",
        scatter_dimension=0,
        tiled=True,
    ).astype(jnp.float32)
    input_part = jnp.einsum(
        "tk,ck->tc",
        value_grad,
        lax.all_gather(local_weight, "dp", axis=0, tiled=True),
        preferred_element_type=jnp.float32,
    ).astype(jnp.bfloat16)
    own_rows = hidden_in.shape[1]
    grad_input = lax.psum(input_part, "tensor").astype(jnp.float32)
    own_grad = lax.dynamic_slice_in_dim(
        grad_input, lax.axis_index("tensor") * own_rows, own_rows, 0
    )
    grad_normed = own_grad * gain_float
    inner_mean = jnp.mean(grad_normed * normed, axis=1, keepdims=True)
    grad_hidden = ((grad_normed - normed * inner_mean) / root_mean).astype(jnp.bfloat16)
    gain_grad = lax.psum(jnp.sum(own_grad * normed, axis=0), ("dp", "tensor"))
    to_previous = shifted(grad_hidden, "section", -1)
    return (weight_grad[None], gain_grad[None], to_previous[None])


def solution(mesh):
    placed = (
        P("section", ("dp", "tensor"), None),
        P("section", None),
        P("section", "dp", "tensor"),
        P("section", "dp", "tensor"),
        P("section", "dp", "tensor"),
        P("section", "dp", "tensor"),
        P("section", "dp"),
    )
    return jax.shard_map(
        shards,
        mesh=mesh,
        in_specs=placed,
        out_specs=(
            P("section", "dp", "tensor"),
            P("section", None),
            P("section", ("dp", "tensor"), None),
        ),
        check_vma=False,
    )
```

profile of v0, /device:TPU:32, one launch (start us, length us, event | category | flops | bytes accessed | tf_op | source)
XLA Modules:
  0.0 1020.2 jit_solution(7451055335804669944)
XLA Ops:
  7.2 0.0 copy-start.3
  7.2 0.0 all-gather.6.cloned.1.call-start
  7.2 0.7 all-gather.6.cloned.1.call-update
  7.9 0.0 all-reduce.2.cloned.1.call-start
  8.0 0.9 reshape_squeeze.9
  8.8 1.1 copy.20
  10.0 1.3 copy.19
  11.3 0.0 copy-done.3
  11.3 0.1 fusion.17
  11.4 0.5 fusion.29
  11.9 0.3 fusion.14
  12.2 64.4 %all-gather.6.cloned.1.call-done = bf16[1,8192,256]{2,1,0:T(8,128)(2,1)} async-done(((bf16[1,256,256]{2,1,0:T(8,128)(2,1)}), bf16[1,8192,256]{2,1,0:T(8,128)(2,1)}) %all-gather.6.cloned.1.call-update) | async-done | bytes 4194320 | tf_op jit(solution)/shard_map/all_gather | solution.py:62
  76.6 5.0 convolution_convert_fusion.1
  81.6 0.0 copy-start.2
  81.6 0.0 copy-start
  81.6 0.0 all-reduce.2.cloned.1.call-update
  81.6 0.0 all-gather.4.cloned.1.call-start
  81.7 0.7 copy-done.2
  82.4 0.4 copy-done
  82.9 0.3 fusion.8
  83.2 215.1 %all-reduce.2.cloned.1.call-done = bf16[128,8192]{1,0:T(8,128)(2,1)} async-done(((bf16[128,8192]{1,0:T(8,128)(2,1)}), bf16[128,8192]{1,0:T(8,128)(2,1)}) %all-reduce.2.cloned.1.call-update) | async-done | bytes 2097168 | tf_op jit(solution)/shard_map/psum | solution.py:66
  298.3 0.0 copy-start.1
  298.3 2.1 fusion.4
  300.4 0.0 copy-done.1
  300.4 1.6 fusion.6
  302.1 0.0 all-gather.4.cloned.1.call-update
  302.1 0.0 reduce-scatter.2.cloned.1.call-start
  302.1 112.5 %all-gather.4.cloned.1.call-done = bf16[128,8192]{1,0:T(8,128)(2,1)} async-done(((bf16[64,8192]{1,0:T(8,128)(2,1)}), bf16[128,8192]{1,0:T(8,128)(2,1)}) %all-gather.4.cloned.1.call-update) | async-done | bytes 2097168 | tf_op jit(solution)/shard_map/all_gather | solution.py:48
  414.6 4.8 convolution_convert_fusion
  419.4 0.0 reduce-scatter.2.cloned.1.call-update
  419.4 15.7 %collective-permute-start = (bf16[64,8192]{1,0:T(8,128)(2,1)S(1)}, bf16[64,8192]{1,0:T(8,128)(2,1)S(1)}, u32[]{:S(2)}, u32[]{:S(2)}) collective-permute-start(bf16[64,8192]{1,0:T(8,128)(2,1)S(1)} %get-tuple-element.5), channel_id=1, source_target_pairs={{64,0},{128,64},{192,128},{256,192},{320,256},{384,320},{448,384},... | collective-permute-start | bytes 3145736 | tf_op jit(solution)/shard_map/ppermute | solution.py:15
  435.2 575.9 %psum.15 = f32[1,8192]{1,0:T(1,128)} all-reduce(f32[1,8192]{1,0:T(1,128)S(1)} %bitcast.58), channel_id=1, replica_groups=mesh['section'=8,'dp'=32,'tensor'=2] {'dp','tensor'}, use_global_device_ids=true, to_apply=%region_6.7 | all-reduce | flops 8192 | bytes 65536 | tf_op jit(solution)/shard_map/psum | solution.py:73
  1011.1 0.0 collective-permute-done
  1011.1 0.0 reduce-scatter.2.cloned.1.call-done
  1011.1 1.6 bitcast_convert_fusion
  1012.7 1.0 copy.39
  (3 shorter events, 0.0 us)
Async XLA Ops:
  7.2 4.1 copy-start.3
  7.2 69.4 %all-gather.6.cloned.1.call-start = ((), (), s32[]{:S(2)}) async-start(), calls=%async_computation.4 | async-start | bytes 4325376 | tf_op jit(solution)/shard_map/all_gather | solution.py:62
  7.9 290.4 %all-reduce.2.cloned.1.call-start = ((), (), s32[]{:S(2)}) async-start(), calls=%async_computation.3 | async-start | bytes 4194304 | tf_op jit(solution)/shard_map/psum | solution.py:66
  81.6 0.8 copy-start.2
  81.6 1.2 copy-start
  81.6 333.0 %all-gather.4.cloned.1.call-start = ((), (), s32[]{:S(2)}) async-start(), calls=%async_computation.1 | async-start | bytes 3145728 | tf_op jit(solution)/shard_map/all_gather | solution.py:48
  298.3 2.1 copy-start.1
  302.1 709.0 %reduce-scatter.2.cloned.1.call-start = ((), (), s32[]{:S(2)}) async-start(), calls=%async_computation.2 | async-start | bytes 4325376 | tf_op jit(solution)/shard_map/reduce_scatter | solution.py:51
  419.4 591.6 %collective-permute-start = (bf16[64,8192]{1,0:T(8,128)(2,1)S(1)}, bf16[64,8192]{1,0:T(8,128)(2,1)S(1)}, u32[]{:S(2)}, u32[]{:S(2)}) collective-permute-start(bf16[64,8192]{1,0:T(8,128)(2,1)S(1)} %get-tuple-element.5), channel_id=1, source_target_pairs={{64,0},{128,64},{192,128},{256,192},{320,256},{384,320},{448,384},... | collective-permute-start | bytes 3145736 | tf_op jit(solution)/shard_map/ppermute | solution.py:15
Sparse Core Ops, SparseCore 0:
  11.1 65.4 all-gather.5
  81.8 216.4 all-reduce.1
  302.2 112.3 all-gather.3
  419.5 110.5 reduce-scatter.1
where the time goes:
time: 1020 us
  blocking collectives  576 us (56%)
  waiting for transfers between devices  393 us (39%)
  starting transfers between devices  15.9 us (2%)
  between operations  13.8 us (1%)
  matrix products  10.7 us (1%)
    psum x1, blocking collectives, shards(): gain_grad = lax.psum(jnp.sum(own_grad * normed, axis=0), ('dp', 'tensor'))  576 us
    psum x1, waiting for transfers between devices, shards(): grad_input = lax.psum(input_part, 'tensor').astype(jnp.float32)  215 us
    all_gather x1, waiting for transfers between devices, shards(): layer_input = lax.all_gather(own_input, 'tensor', axis=0, tiled=True)  112 us
    all_gather x1, waiting for transfers between devices, shards(): lax.all_gather(local_weight, 'dp', axis=0, tiled=True)  64.4 us
  transfers between devices with their start and end apart: 5, of which 3 were waited for; matrix products, arithmetic and copies ran while one was open for 0% of the time, Pallas kernels for 0%

commit v1 on v0

--- a/solution.py
+++ b/solution.py
@@ -4,6 +4,7 @@
 import jax.numpy as jnp
 from jax import lax
 from jax.sharding import PartitionSpec as P
+
 
 HD = 128
 QPK = 8
@@ -13,6 +14,20 @@
     count = lax.axis_size(axis)
     first, last = (max(0, -steps), min(count, count - steps))
     return lax.ppermute(value, axis, [(source, source + steps) for source in range(first, last)])
+
+
+def swapped(value):
+    return lax.ppermute(value, "tensor", [(0, 1), (1, 0)])
+
+
+def exchanged(value, split, joined):
+    return lax.all_to_all(value, "dp", split, joined)
+
+
+def gathered(value):
+    count = lax.axis_size("dp")
+    copies = jnp.broadcast_to(value[None], (count,) + value.shape)
+    return exchanged(copies, 0, 0)
 
 
 def attend(query_rows, key_rows, grad_rows, position_rows):
@@ -39,38 +54,49 @@
     return value_grad.reshape(length, groups * HD).astype(jnp.bfloat16)
 
 
-def shards(hidden_in, norm_gain, value_weight, query_vectors, key_vectors, grad_attn, positions):
+def layer(hidden_in, norm_gain, value_weight, query_vectors, key_vectors, grad_attn, positions):
+    n_dp = lax.axis_size("dp")
+    here = lax.axis_index("dp")
+    half = lax.axis_index("tensor")
+    own_rows, width = hidden_in.shape[1:]
+    chunk = width // n_dp
+    local_weight = value_weight[0]
+    own_columns = local_weight.shape[1]
+    other_weight = swapped(local_weight)
     rows_float = hidden_in[0].astype(jnp.float32)
     root_mean = jnp.sqrt(jnp.mean(rows_float * rows_float, axis=1, keepdims=True) + 1e-05)
     normed = rows_float / root_mean
+    normed_columns = exchanged(
+        normed.astype(jnp.bfloat16).reshape(own_rows, n_dp, chunk), 1, 0
+    ).reshape(n_dp * own_rows, chunk)
+    value_grad = attend(query_vectors[0], key_vectors[0], grad_attn[0], positions[0])
+    kept = lax.dynamic_slice_in_dim(value_grad, half * own_rows, own_rows, 0)
+    given = lax.dynamic_slice_in_dim(value_grad, (1 - half) * own_rows, own_rows, 0)
+    own_value = jnp.concatenate([kept, swapped(given)], axis=1)
+    plane_value = gathered(own_value).reshape(n_dp * own_rows, 2 * own_columns)
+    full_weight = jnp.concatenate([local_weight, other_weight], axis=1)
+    grad_columns = jnp.einsum(
+        "tk,ck->tc", plane_value, full_weight, preferred_element_type=jnp.float32
+    ).astype(jnp.bfloat16)
+    own_grad = (
+        exchanged(grad_columns.reshape(n_dp, own_rows, chunk), 0, 1)
+        .reshape(own_rows, width)
+        .astype(jnp.float32)
+    )
+    normed_term = jnp.einsum(
+        "tc,tk->ck", normed_columns, plane_value, preferred_element_type=jnp.float32
+    )
     gain_float = norm_gain[0].astype(jnp.float32)
-    own_input = (normed * gain_float).astype(jnp.bfloat16)
-    layer_input = lax.all_gather(own_input, "tensor", axis=0, tiled=True)
-    value_grad = attend(query_vectors[0], key_vectors[0], grad_attn[0], positions[0])
-    local_weight = value_weight[0]
-    weight_grad = lax.psum_scatter(
-        jnp.einsum("tc,tk->ck", layer_input, value_grad, preferred_element_type=jnp.float32).astype(
-            jnp.bfloat16
-        ),
-        "dp",
-        scatter_dimension=0,
-        tiled=True,
+    own_gain = lax.dynamic_slice_in_dim(gain_float, here * chunk, chunk, 0)
+    term = normed_term * own_gain[:, None]
+    weight_grad = term[:, :own_columns] + swapped(
+        term[:, own_columns:].astype(jnp.bfloat16)
     ).astype(jnp.float32)
-    input_part = jnp.einsum(
-        "tk,ck->tc",
-        value_grad,
-        lax.all_gather(local_weight, "dp", axis=0, tiled=True),
-        preferred_element_type=jnp.float32,
-    ).astype(jnp.bfloat16)
-    own_rows = hidden_in.shape[1]
-    grad_input = lax.psum(input_part, "tensor").astype(jnp.float32)
-    own_grad = lax.dynamic_slice_in_dim(
-        grad_input, lax.axis_index("tensor") * own_rows, own_rows, 0
-    )
+    gain_term = jnp.sum(normed_term * full_weight.astype(jnp.float32), axis=1)
+    gain_grad = gathered(gain_term + swapped(gain_term)).reshape(width)
     grad_normed = own_grad * gain_float
     inner_mean = jnp.mean(grad_normed * normed, axis=1, keepdims=True)
     grad_hidden = ((grad_normed - normed * inner_mean) / root_mean).astype(jnp.bfloat16)
-    gain_grad = lax.psum(jnp.sum(own_grad * normed, axis=0), ("dp", "tensor"))
     to_previous = shifted(grad_hidden, "section", -1)
     return (weight_grad[None], gain_grad[None], to_previous[None])
 
@@ -86,7 +112,7 @@
         P("section", "dp"),
     )
     return jax.shard_map(
-        shards,
+        layer,
         mesh=mesh,
         in_specs=placed,
         out_specs=(

time: 1020 us -> 163 us (0.16)
  blocking collectives: 576 us -> 14.5 us
  waiting for transfers between devices: 393 us -> 61.8 us
  starting transfers between devices: 15.9 us -> 61.5 us
  between operations: 13.8 us -> 0.87 us
    psum x1 -> x0, blocking collectives: 576 us -> none  [shards(): gain_grad = lax.psum(jnp.sum(own_grad * normed, axis=0), ('dp', 'tensor'))]
    psum x1 -> x0, waiting for transfers between devices: 215 us -> none  [shards(): grad_input = lax.psum(input_part, 'tensor').astype(jnp.float32)]
    all_gather x2 -> x0, waiting for transfers between devices: 177 us -> none  [the longest x1 112 us: shards(): layer_input = lax.all_gather(own_input, 'tensor', axis=0, tiled=True)]
    ppermute x0 -> x4, starting transfers between devices: none -> 41.2 us  [swapped(): return lax.ppermute(value, 'tensor', [(0, 1), (1, 0)])]
    all_to_all x0 -> x3, waiting for transfers between devices: none -> 33.2 us  [exchanged(): return lax.all_to_all(value, 'dp', split, joined)]
    ppermute x0 -> x4, waiting for transfers between devices: none -> 28.6 us  [swapped(): return lax.ppermute(value, 'tensor', [(0, 1), (1, 0)])]
    all_to_all x0 -> x3, starting transfers between devices: none -> 16.9 us  [exchanged(): return lax.all_to_all(value, 'dp', split, joined)]
    all_to_all x0 -> x1, blocking collectives: none -> 14.5 us  [exchanged(): return lax.all_to_all(value, 'dp', split, joined)]
  transfers between devices with their start and end apart: 5 -> 8, of which waited for: 3 -> 6; matrix products, arithmetic and copies ran while one was open for 0% -> 8% of each run, Pallas kernels for 0% -> 0%
where the time goes in v1:
time: 163 us; the launch traced here: 162 us
  waiting for transfers between devices  61.8 us (38%)
  starting transfers between devices  61.5 us (38%)
  blocking collectives  14.5 us (9%)
  local copies, waits for them, and re-layouts  11.2 us (7%)
  other arithmetic  7.88 us (5%)
  matrix products  4.61 us (3%)
    ppermute x4, starting transfers between devices, swapped(): return lax.ppermute(value, 'tensor', [(0, 1), (1, 0)])  41.2 us
    all_to_all x3, waiting for transfers between devices, exchanged(): return lax.all_to_all(value, 'dp', split, joined)  33.2 us
    ppermute x4, waiting for transfers between devices, swapped(): return lax.ppermute(value, 'tensor', [(0, 1), (1, 0)])  28.6 us
    all_to_all x3, starting transfers between devices, exchanged(): return lax.all_to_all(value, 'dp', split, joined)  16.9 us
    all_to_all x1, blocking collectives, exchanged(): return lax.all_to_all(value, 'dp', split, joined)  14.5 us
    unnamed x15, local copies, waits for them, and re-layouts  5.57 us
    ppermute x1, starting transfers between devices, shifted(): lax.ppermute(value, axis, [(source, source + steps) for source in range(f...  3.38 us
  transfers between devices with their start and end apart: 8, of which 6 were waited for; matrix products, arithmetic and copies ran while one was open for 8% of the time, Pallas kernels for 0%

profile of v1, /device:TPU:32, one launch (start us, length us, event | category | flops | bytes accessed | tf_op | source)
XLA Modules:
  0.0 162.3 jit_solution(15938774233566594850)
XLA Ops:
  0.6 0.8 fusion.17
  1.5 0.9 reshape_squeeze.14
  2.3 1.1 copy.54
  3.5 1.3 copy.52
  4.8 0.5 fusion.30
  5.3 0.3 fusion.13
  5.6 0.1 constant_dynamic-slice_fusion.2
  5.8 14.8 %collective-permute-start = (bf16[64,256]{0,1:T(8,128)(2,1)S(1)}, bf16[64,256]{0,1:T(8,128)(2,1)S(1)}, u32[]{:S(2)}, u32[]{:S(2)}) collective-permute-start(bf16[64,256]{0,1:T(8,128)(2,1)S(1)} %get-tuple-element.6), channel_id=1, source_target_pairs={{0,1},{1,0},{2,3},{3,2},{4,5},{5,4},{6,7},{7,6},{8,9},{9,8},{10,11... | collective-permute-start | bytes 98312 | tf_op jit(solution)/shard_map/ppermute | solution.py:20
  20.6 3.7 %collective-permute-done = bf16[64,256]{0,1:T(8,128)(2,1)S(1)} collective-permute-done((bf16[64,256]{0,1:T(8,128)(2,1)S(1)}, bf16[64,256]{0,1:T(8,128)(2,1)S(1)}, u32[]{:S(2)}, u32[]{:S(2)}) %collective-permute-start) | collective-permute-done | bytes 32800 | tf_op jit(solution)/shard_map/ppermute | solution.py:20
  24.3 0.1 copy.44
  24.4 1.6 broadcast_in_dim.23
  26.0 0.0 copy-start.4
  26.0 7.5 %all-to-all-start.1 = ((bf16[32,64,512]{2,1,0:T(8,128)(2,1)}), bf16[32,64,512]{2,1,0:T(8,128)(2,1)S(1)}, u32[]{:S(2)}, u32[]{:S(2)}) async-start(bf16[32,64,512]{2,1,0:T(8,128)(2,1)} %broadcast_in_dim.23), calls=%async_computation.1 | async-start | bytes 4194304 | tf_op jit(solution)/shard_map/all_to_all | solution.py:24
  33.5 0.0 copy-done.4
  33.5 11.9 %collective-permute-start.2 = (bf16[256,256]{1,0:T(8,128)(2,1)S(1)}, bf16[256,256]{1,0:T(8,128)(2,1)S(1)}, u32[]{:S(2)}, u32[]{:S(2)}) collective-permute-start(bf16[256,256]{1,0:T(8,128)(2,1)S(1)} %bitcast.103), channel_id=1, source_target_pairs={{0,1},{1,0},{2,3},{3,2},{4,5},{5,4},{6,7},{7,6},{8,9},{9,8},{10,11... | collective-permute-start | bytes 393224 | tf_op jit(solution)/shard_map/ppermute | solution.py:20
  45.4 4.5 %collective-permute-done.2 = bf16[256,256]{1,0:T(8,128)(2,1)S(1)} collective-permute-done((bf16[256,256]{1,0:T(8,128)(2,1)S(1)}, bf16[256,256]{1,0:T(8,128)(2,1)S(1)}, u32[]{:S(2)}, u32[]{:S(2)}) %collective-permute-start.2) | collective-permute-done | bytes 131104 | tf_op jit(solution)/shard_map/ppermute | solution.py:20
  49.8 12.6 %all-to-all-done.1 = bf16[32,64,512]{2,1,0:T(8,128)(2,1)S(1)} async-done(((bf16[32,64,512]{2,1,0:T(8,128)(2,1)}), bf16[32,64,512]{2,1,0:T(8,128)(2,1)S(1)}, u32[]{:S(2)}, u32[]{:S(2)}) %all-to-all-start.1) | async-done | bytes 2097184 | tf_op jit(solution)/shard_map/all_to_all | solution.py:24
  62.4 0.0 copy-start.1
  62.4 1.3 copy-done.1
  63.8 1.7 %convolution_convert_fusion = bf16[2048,256]{1,0:T(8,128)(2,1)} fusion(bf16[2048,512]{1,0:T(8,128)(2,1)S(1)} %bitcast.91, bf16[256,256]{1,0:T(8,128)(2,1)S(1)} %collective-permute-done.2, bf16[256,256]{1,0:T(8,128)(2,1)S(1)} %bitcast.104), kind=kOutput, calls=%fused_computation.1 | convolution fusion | flops 537919488 | bytes 3407872 | tf_op jit(solution)/shard_map/tk,ck->tc/dot_general | solution.py:78
  65.5 4.8 %all-to-all-start.3 = ((bf16[32,64,1,256]{3,1,2,0:T(8,128)(2,1)}), bf16[32,64,1,256]{3,1,2,0:T(8,128)(2,1)}, u32[]{:S(2)}, u32[]{:S(2)}) async-start(bf16[32,64,1,256]{3,1,2,0:T(8,128)(2,1)} %bitcast.19), calls=%async_computation.3 | async-start | bytes 2097152 | tf_op jit(solution)/shard_map/all_to_all | solution.py:24
  70.3 0.0 copy-done.3
  70.3 0.1 convert_reduce_fusion
  70.5 0.0 copy-done
  70.5 0.3 copy.53
  70.8 0.3 fusion.3
  71.1 0.3 fusion.1
  71.4 1.6 copy.39
  72.9 14.1 %all-to-all-done.3 = bf16[32,64,1,256]{3,1,2,0:T(8,128)(2,1)} async-done(((bf16[32,64,1,256]{3,1,2,0:T(8,128)(2,1)}), bf16[32,64,1,256]{3,1,2,0:T(8,128)(2,1)}, u32[]{:S(2)}, u32[]{:S(2)}) %all-to-all-start.3) | async-done | bytes 1048608 | tf_op jit(solution)/shard_map/all_to_all | solution.py:24
  87.0 4.7 %all-to-all-start = ((bf16[1,64,32,256]{3,1,0,2:T(8,128)(2,1)}), bf16[1,64,32,256]{3,1,0,2:T(8,128)(2,1)}, u32[]{:S(2)}, u32[]{:S(2)}) async-start(bf16[1,64,32,256]{3,1,0,2:T(8,128)(2,1)} %copy.39), calls=%async_computation | async-start | bytes 2097152 | tf_op jit(solution)/shard_map/all_to_all | solution.py:24
  91.7 2.2 %fusion.2 = f32[64]{0:T(128)S(1)} fusion(f32[1,64,32,1,256]{4,2,1,3,0:T(8,128)S(1)} %bitcast.87, f32[64]{0:T(128)S(1)} %add_sqrt_fusion, f32[32,256]{1,0:T(8,128)S(1)} %mul.65, bf16[32,64,1,256]{3,1,2,0:T(8,128)(2,1)} %all-to-all-done.3), kind=kLoop, calls=%fused_computation.5 | loop fusion | flops 2621376 | bytes 3179008 | tf_op jit(solution)/shard_map/reduce_sum | solution.py:98
  94.0 1.8 %bitcast_convert_fusion = f32[32,1,64,1,256]{4,0,2,3,1:T(8,128)S(1)} fusion(bf16[32,64,1,256]{3,1,2,0:T(8,128)(2,1)} %all-to-all-done.3), kind=kLoop, calls=%fused_computation.21 | loop fusion | flops 524288 | bytes 3145728 | tf_op jit(solution)/shard_map/convert_element_type | solution.py:84
  95.8 1.2 copy.55
  97.0 0.0 copy-start.2
  97.0 1.5 fusion.7
  98.5 3.4 %collective-permute-start.4 = (bf16[64,8192]{1,0:T(8,128)(2,1)}, bf16[64,8192]{1,0:T(8,128)(2,1)S(1)}, u32[]{:S(2)}, u32[]{:S(2)}) collective-permute-start(bf16[64,8192]{1,0:T(8,128)(2,1)} %fusion.7), channel_id=1, source_target_pairs={{64,0},{128,64},{192,128},{256,192},{320,256},{384,320},{448,384},... | collective-permute-start | bytes 3145736 | tf_op jit(solution)/shard_map/ppermute | solution.py:16
  101.9 6.5 %all-to-all-done = bf16[1,64,32,256]{3,1,0,2:T(8,128)(2,1)} async-done(((bf16[1,64,32,256]{3,1,0,2:T(8,128)(2,1)}), bf16[1,64,32,256]{3,1,0,2:T(8,128)(2,1)}, u32[]{:S(2)}, u32[]{:S(2)}) %all-to-all-start) | async-done | bytes 1048608 | tf_op jit(solution)/shard_map/all_to_all | solution.py:24
  108.5 0.0 copy-done.2
  108.5 2.0 %multiply_reduce_fusion = (f32[256]{0:T(256)S(1)}, f32[256,512]{1,0:T(8,128)S(1)}) fusion(bf16[256,256]{1,0:T(8,128)(2,1)S(1)} %collective-permute-done.2, bf16[256,256]{1,0:T(8,128)(2,1)S(1)} %bitcast.105, f32[256]{0:T(256)S(1)} %bitcast.102, bf16[2048,256]{1,0:T(8,128)(2,1)} %bitcast.3, bf16[2048,512]{1,0:T(8,128)(2,1)S(1)} %bitcast.92), kind=kOutput, calls=%fused_computation.24 | convolution fusion | flops 537788160 | bytes 3934208 | tf_op jit(solution)/shard_map/tc,tk->ck/dot_general | solution.py:86
  110.5 11.9 %collective-permute-start.1 = (bf16[256,256]{1,0:T(8,128)(2,1)S(1)}, bf16[256,256]{1,0:T(8,128)(2,1)S(1)}, u32[]{:S(2)}, u32[]{:S(2)}) collective-permute-start(bf16[256,256]{1,0:T(8,128)(2,1)S(1)} %slice.15), channel_id=1, source_target_pairs={{0,1},{1,0},{2,3},{3,2},{4,5},{5,4},{6,7},{7,6},{8,9},{9,8},{10,11... | collective-permute-start | bytes 393224 | tf_op jit(solution)/shard_map/ppermute | solution.py:20
  122.4 2.7 %collective-permute-start.3 = (f32[256]{0:T(256)S(1)}, f32[256]{0:T(256)S(1)}, u32[]{:S(2)}, u32[]{:S(2)}) collective-permute-start(f32[256]{0:T(256)S(1)} %get-tuple-element.3), channel_id=1, source_target_pairs={{0,1},{1,0},{2,3},{3,2},{4,5},{5,4},{6,7},{7,6},{8,9},{9,8},{10,11... | collective-permute-start | bytes 3080 | tf_op jit(solution)/shard_map/ppermute | solution.py:20
  125.1 20.4 %collective-permute-done.3 = f32[256]{0:T(256)S(1)} collective-permute-done((f32[256]{0:T(256)S(1)}, f32[256]{0:T(256)S(1)}, u32[]{:S(2)}, u32[]{:S(2)}) %collective-permute-start.3) | collective-permute-done | bytes 1056 | tf_op jit(solution)/shard_map/ppermute | solution.py:20
  145.5 14.5 %all_to_all.35 = f32[32,1,256]{2,1,0:T(1,128)S(1)} all-to-all(f32[32,1,256]{2,1,0:T(1,128)S(1)} %broadcast_in_dim.45), channel_id=1, replica_groups=mesh['section'=8,'dp'=32,'tensor'=2] {'dp'}, dimensions={0} | all-to-all | bytes 65536 | tf_op jit(solution)/shard_map/all_to_all | solution.py:24
  160.0 0.0 collective-permute-done.1
  160.0 0.7 fusion.15
  160.7 0.0 collective-permute-done.4
  160.8 0.6 copy.78
  161.4 1.0 copy.79
  (11 shorter events, 0.1 us)
Async XLA Ops:
  5.8 18.6 %collective-permute-start = (bf16[64,256]{0,1:T(8,128)(2,1)S(1)}, bf16[64,256]{0,1:T(8,128)(2,1)S(1)}, u32[]{:S(2)}, u32[]{:S(2)}) collective-permute-start(bf16[64,256]{0,1:T(8,128)(2,1)S(1)} %get-tuple-element.6), channel_id=1, source_target_pairs={{0,1},{1,0},{2,3},{3,2},{4,5},{5,4},{6,7},{7,6},{8,9},{9,8},{10,11... | collective-permute-start | bytes 98312 | tf_op jit(solution)/shard_map/ppermute | solution.py:20
  26.0 7.5 %copy-start.4 = (bf16[1,256,256]{2,1,0:T(8,128)(2,1)S(1)}, bf16[1,256,256]{2,1,0:T(8,128)(2,1)}, u32[]{:S(2)}) copy-start(bf16[1,256,256]{2,1,0:T(8,128)(2,1)} %param.9) | copy-start | bytes 393220
  26.0 36.4 %all-to-all-start.1 = ((bf16[32,64,512]{2,1,0:T(8,128)(2,1)}), bf16[32,64,512]{2,1,0:T(8,128)(2,1)S(1)}, u32[]{:S(2)}, u32[]{:S(2)}) async-start(bf16[32,64,512]{2,1,0:T(8,128)(2,1)} %broadcast_in_dim.23), calls=%async_computation.1 | async-start | bytes 4194304 | tf_op jit(solution)/shard_map/all_to_all | solution.py:24
  33.5 16.3 %collective-permute-start.2 = (bf16[256,256]{1,0:T(8,128)(2,1)S(1)}, bf16[256,256]{1,0:T(8,128)(2,1)S(1)}, u32[]{:S(2)}, u32[]{:S(2)}) collective-permute-start(bf16[256,256]{1,0:T(8,128)(2,1)S(1)} %bitcast.103), channel_id=1, source_target_pairs={{0,1},{1,0},{2,3},{3,2},{4,5},{5,4},{6,7},{7,6},{8,9},{9,8},{10,11... | collective-permute-start | bytes 393224 | tf_op jit(solution)/shard_map/ppermute | solution.py:20
  62.4 1.3 copy-start.1
  65.5 4.8 %copy-start.3 = (bf16[1,8192]{1,0:T(2,128)(2,1)S(1)}, bf16[1,8192]{1,0:T(2,128)(2,1)}, u32[]{:S(2)}) copy-start(bf16[1,8192]{1,0:T(2,128)(2,1)} %param.8) | copy-start | bytes 49156
  65.5 5.0 %copy-start = (bf16[1,64,8192]{2,1,0:T(8,128)(2,1)S(1)}, bf16[1,64,8192]{2,1,0:T(8,128)(2,1)}, u32[]{:S(2)}) copy-start(bf16[1,64,8192]{2,1,0:T(8,128)(2,1)} %param.7) | copy-start | bytes 3145732
  65.5 21.5 %all-to-all-start.3 = ((bf16[32,64,1,256]{3,1,2,0:T(8,128)(2,1)}), bf16[32,64,1,256]{3,1,2,0:T(8,128)(2,1)}, u32[]{:S(2)}, u32[]{:S(2)}) async-start(bf16[32,64,1,256]{3,1,2,0:T(8,128)(2,1)} %bitcast.19), calls=%async_computation.3 | async-start | bytes 2097152 | tf_op jit(solution)/shard_map/all_to_all | solution.py:24
  87.0 21.4 %all-to-all-start = ((bf16[1,64,32,256]{3,1,0,2:T(8,128)(2,1)}), bf16[1,64,32,256]{3,1,0,2:T(8,128)(2,1)}, u32[]{:S(2)}, u32[]{:S(2)}) async-start(bf16[1,64,32,256]{3,1,0,2:T(8,128)(2,1)} %copy.39), calls=%async_computation | async-start | bytes 2097152 | tf_op jit(solution)/shard_map/all_to_all | solution.py:24
  97.0 11.5 %copy-start.2 = (bf16[32,64,512]{2,1,0:T(8,128)(2,1)S(1)}, bf16[32,64,512]{2,1,0:T(8,128)(2,1)}, u32[]{:S(2)}) copy-start(bf16[32,64,512]{2,1,0:T(8,128)(2,1)} %copy-done.1) | copy-start | bytes 6291460
  98.5 62.2 %collective-permute-start.4 = (bf16[64,8192]{1,0:T(8,128)(2,1)}, bf16[64,8192]{1,0:T(8,128)(2,1)S(1)}, u32[]{:S(2)}, u32[]{:S(2)}) collective-permute-start(bf16[64,8192]{1,0:T(8,128)(2,1)} %fusion.7), channel_id=1, source_target_pairs={{64,0},{128,64},{192,128},{256,192},{320,256},{384,320},{448,384},... | collective-permute-start | bytes 3145736 | tf_op jit(solution)/shard_map/ppermute | solution.py:16
  110.5 49.5 %collective-permute-start.1 = (bf16[256,256]{1,0:T(8,128)(2,1)S(1)}, bf16[256,256]{1,0:T(8,128)(2,1)S(1)}, u32[]{:S(2)}, u32[]{:S(2)}) collective-permute-start(bf16[256,256]{1,0:T(8,128)(2,1)S(1)} %slice.15), channel_id=1, source_target_pairs={{0,1},{1,0},{2,3},{3,2},{4,5},{5,4},{6,7},{7,6},{8,9},{9,8},{10,11... | collective-permute-start | bytes 393224 | tf_op jit(solution)/shard_map/ppermute | solution.py:20
  122.4 23.1 %collective-permute-start.3 = (f32[256]{0:T(256)S(1)}, f32[256]{0:T(256)S(1)}, u32[]{:S(2)}, u32[]{:S(2)}) collective-permute-start(f32[256]{0:T(256)S(1)} %get-tuple-element.3), channel_id=1, source_target_pairs={{0,1},{1,0},{2,3},{3,2},{4,5},{5,4},{6,7},{7,6},{8,9},{9,8},{10,11... | collective-permute-start | bytes 3080 | tf_op jit(solution)/shard_map/ppermute | solution.py:20

commit v2 on v1

--- a/solution.py
+++ b/solution.py
@@ -20,14 +20,30 @@
     return lax.ppermute(value, "tensor", [(0, 1), (1, 0)])
 
 
+def same_core():
+    count = lax.axis_size("dp")
+    return [list(range(core, count, 2)) for core in range(2)]
+
+
 def exchanged(value, split, joined):
-    return lax.all_to_all(value, "dp", split, joined)
+    return lax.all_to_all(value, "dp", split, joined, axis_index_groups=same_core())
 
 
 def gathered(value):
-    count = lax.axis_size("dp")
+    count = lax.axis_size("dp") // 2
     copies = jnp.broadcast_to(value[None], (count,) + value.shape)
     return exchanged(copies, 0, 0)
+
+
+def other_core(value):
+    count = lax.axis_size("dp")
+    return lax.ppermute(value, "dp", [(source, source ^ 1) for source in range(count)])
+
+
+def by_core(core, own, other):
+    first = jnp.where(core == 0, own, other)
+    second = jnp.where(core == 0, other, own)
+    return jnp.concatenate([first, second], axis=0)
 
 
 def attend(query_rows, key_rows, grad_rows, position_rows):
@@ -56,44 +72,61 @@
 
 def layer(hidden_in, norm_gain, value_weight, query_vectors, key_vectors, grad_attn, positions):
     n_dp = lax.axis_size("dp")
+    n_chip = n_dp // 2
     here = lax.axis_index("dp")
+    core = here % 2
     half = lax.axis_index("tensor")
     own_rows, width = hidden_in.shape[1:]
     chunk = width // n_dp
     local_weight = value_weight[0]
     own_columns = local_weight.shape[1]
-    other_weight = swapped(local_weight)
     rows_float = hidden_in[0].astype(jnp.float32)
     root_mean = jnp.sqrt(jnp.mean(rows_float * rows_float, axis=1, keepdims=True) + 1e-05)
     normed = rows_float / root_mean
     normed_columns = exchanged(
-        normed.astype(jnp.bfloat16).reshape(own_rows, n_dp, chunk), 1, 0
-    ).reshape(n_dp * own_rows, chunk)
+        normed.astype(jnp.bfloat16).reshape(own_rows, n_chip, 2 * chunk), 1, 0
+    ).reshape(n_chip * own_rows, 2 * chunk)
     value_grad = attend(query_vectors[0], key_vectors[0], grad_attn[0], positions[0])
     kept = lax.dynamic_slice_in_dim(value_grad, half * own_rows, own_rows, 0)
     given = lax.dynamic_slice_in_dim(value_grad, (1 - half) * own_rows, own_rows, 0)
     own_value = jnp.concatenate([kept, swapped(given)], axis=1)
-    plane_value = gathered(own_value).reshape(n_dp * own_rows, 2 * own_columns)
-    full_weight = jnp.concatenate([local_weight, other_weight], axis=1)
+    device_weight = jnp.concatenate([local_weight, swapped(local_weight)], axis=1)
+    full_weight = by_core(core, device_weight, other_core(device_weight))
+    group_value = gathered(own_value).reshape(n_chip * own_rows, 2 * own_columns)
     grad_columns = jnp.einsum(
-        "tk,ck->tc", plane_value, full_weight, preferred_element_type=jnp.float32
+        "tk,ck->tc", group_value, full_weight, preferred_element_type=jnp.float32
     ).astype(jnp.bfloat16)
     own_grad = (
-        exchanged(grad_columns.reshape(n_dp, own_rows, chunk), 0, 1)
+        exchanged(grad_columns.reshape(n_chip, own_rows, 2 * chunk), 0, 1)
         .reshape(own_rows, width)
         .astype(jnp.float32)
     )
-    normed_term = jnp.einsum(
-        "tc,tk->ck", normed_columns, plane_value, preferred_element_type=jnp.float32
+    group_term = jnp.einsum(
+        "tc,tk->ck", normed_columns, group_value, preferred_element_type=jnp.float32
     )
+    kept_term = lax.dynamic_slice_in_dim(group_term, core * chunk, chunk, 0)
+    given_term = lax.dynamic_slice_in_dim(group_term, (1 - core) * chunk, chunk, 0)
+    plane_term = kept_term + other_core(given_term.astype(jnp.bfloat16)).astype(jnp.float32)
+    gain_term = jnp.sum(plane_term * device_weight.astype(jnp.float32), axis=1)
+    gain_high = lax.reduce_precision(gain_term, 8, 7)
+    gain_low = gain_term - gain_high
+    sent_term = jnp.concatenate(
+        [
+            plane_term[:, own_columns:].astype(jnp.bfloat16),
+            jnp.pad(
+                jnp.stack([gain_high, gain_low]).astype(jnp.bfloat16), ((0, 14), (0, 0))
+            ),
+        ],
+        axis=0,
+    )
+    given_back = swapped(sent_term).astype(jnp.float32)
     gain_float = norm_gain[0].astype(jnp.float32)
     own_gain = lax.dynamic_slice_in_dim(gain_float, here * chunk, chunk, 0)
-    term = normed_term * own_gain[:, None]
-    weight_grad = term[:, :own_columns] + swapped(
-        term[:, own_columns:].astype(jnp.bfloat16)
-    ).astype(jnp.float32)
-    gain_term = jnp.sum(normed_term * full_weight.astype(jnp.float32), axis=1)
-    gain_grad = gathered(gain_term + swapped(gain_term)).reshape(width)
+    weight_grad = (plane_term[:, :own_columns] + given_back[:chunk]) * own_gain[:, None]
+    gain_chunk = gain_high + gain_low + given_back[chunk] + given_back[chunk + 1]
+    gain_grad = lax.all_to_all(
+        jnp.broadcast_to(gain_chunk[None], (n_dp, chunk)), "dp", 0, 0
+    ).reshape(width)
     grad_normed = own_grad * gain_float
     inner_mean = jnp.mean(grad_normed * normed, axis=1, keepdims=True)
     grad_hidden = ((grad_normed - normed * inner_mean) / root_mean).astype(jnp.bfloat16)

time: 163 us -> 154 us (0.945)
  the two profiles are of different devices: /device:TPU:32 before, /device:TPU:161 now
where the time goes in v2:
time: 154 us; the launch traced here: 153 us
  starting transfers between devices  77.5 us (50%)
  waiting for transfers between devices  44.4 us (29%)
  local copies, waits for them, and re-layouts  13.9 us (9%)
  other arithmetic  10 us (6%)
  matrix products  6.06 us (4%)
    ppermute x3, starting transfers between devices, swapped(): return lax.ppermute(value, 'tensor', [(0, 1), (1, 0)])  33.3 us
    ppermute x3, waiting for transfers between devices, swapped(): return lax.ppermute(value, 'tensor', [(0, 1), (1, 0)])  28.7 us
    all_to_all x3, starting transfers between devices, exchanged(): lax.all_to_all(value, 'dp', split, joined, axis_index_groups=same_core())  17.8 us
    all_to_all x1, starting transfers between devices, layer(): lax.all_to_all(jnp.broadcast_to(gain_chunk[None], (n_dp, chunk)), 'dp', 0...  15 us
    ppermute x2, starting transfers between devices, other_core(): lax.ppermute(value, 'dp', [(source, source ^ 1) for source in range(count)])  9.41 us
    unnamed x17, local copies, waits for them, and re-layouts  7.41 us
    all_to_all x1, waiting for transfers between devices, layer(): lax.all_to_all(jnp.broadcast_to(gain_chunk[None], (n_dp, chunk)), 'dp', 0...  6.46 us
    all_to_all x3, waiting for transfers between devices, exchanged(): lax.all_to_all(value, 'dp', split, joined, axis_index_groups=same_core())  6.44 us
  transfers between devices with their start and end apart: 10, of which 7 were waited for; matrix products, arithmetic and copies ran while one was open for 9% of the time, Pallas kernels for 0%

profile of v2, /device:TPU:161, one launch (start us, length us, event | category | flops | bytes accessed | tf_op | source)
XLA Modules:
  0.0 152.8 jit_solution(14775097426788690224)
XLA Ops:
  0.6 0.8 fusion.21
  1.5 0.9 reshape_squeeze.14
  2.3 1.1 copy.54
  3.5 1.3 copy.52
  4.8 0.5 fusion.38
  5.3 0.3 fusion.13
  5.6 0.0 copy-start.3
  5.7 0.1 constant_dynamic-slice_fusion.2
  5.8 9.9 %collective-permute-start = (bf16[64,256]{0,1:T(8,128)(2,1)S(1)}, bf16[64,256]{0,1:T(8,128)(2,1)S(1)}, u32[]{:S(2)}, u32[]{:S(2)}) collective-permute-start(bf16[64,256]{0,1:T(8,128)(2,1)S(1)} %get-tuple-element.8), channel_id=1, source_target_pairs={{0,1},{1,0},{2,3},{3,2},{4,5},{5,4},{6,7},{7,6},{8,9},{9,8},{10,11... | collective-permute-start | bytes 98312 | tf_op jit(solution)/shard_map/ppermute | solution.py:20
  15.7 4.1 %collective-permute-done = bf16[64,256]{0,1:T(8,128)(2,1)S(1)} collective-permute-done((bf16[64,256]{0,1:T(8,128)(2,1)S(1)}, bf16[64,256]{0,1:T(8,128)(2,1)S(1)}, u32[]{:S(2)}, u32[]{:S(2)}) %collective-permute-start) | collective-permute-done | bytes 32800 | tf_op jit(solution)/shard_map/ppermute | solution.py:20
  19.8 0.1 copy.44
  19.9 1.1 broadcast_in_dim.23
  21.0 6.8 %all-to-all-start.1 = ((bf16[16,64,512]{2,1,0:T(8,128)(2,1)}), bf16[16,64,512]{2,1,0:T(8,128)(2,1)}, u32[]{:S(2)}, u32[]{:S(2)}) async-start(bf16[16,64,512]{2,1,0:T(8,128)(2,1)} %broadcast_in_dim.23), calls=%async_computation.1 | async-start | bytes 2097152 | tf_op jit(solution)/shard_map/all_to_all | solution.py:29
  27.8 12.6 %collective-permute-start.2 = (bf16[256,256]{1,0:T(8,128)(2,1)S(1)}, bf16[256,256]{1,0:T(8,128)(2,1)S(1)}, u32[]{:S(2)}, u32[]{:S(2)}) collective-permute-start(bf16[256,256]{1,0:T(8,128)(2,1)S(1)} %bitcast.93), channel_id=1, source_target_pairs={{0,1},{1,0},{2,3},{3,2},{4,5},{5,4},{6,7},{7,6},{8,9},{9,8},{10,11... | collective-permute-start | bytes 393224 | tf_op jit(solution)/shard_map/ppermute | solution.py:20
  40.4 0.4 copy.53
  40.8 0.3 fusion.3
  41.1 0.3 fusion.1
  41.4 1.5 %copy.39 = bf16[1,64,16,512]{3,1,0,2:T(8,128)(2,1)} copy(bf16[1,64,16,512]{3,2,1,0:T(8,128)(2,1)S(1)} %fusion.1) | data formatting | bytes 2097152 | tf_op jit(solution)/shard_map/convert_element_type | solution.py:87
  43.0 6.7 %all-to-all-start = ((bf16[1,64,16,512]{3,1,0,2:T(8,128)(2,1)}), bf16[1,64,16,512]{3,1,0,2:T(8,128)(2,1)}, u32[]{:S(2)}, u32[]{:S(2)}) async-start(bf16[1,64,16,512]{3,1,0,2:T(8,128)(2,1)} %copy.39), calls=%async_computation | async-start | bytes 2097152 | tf_op jit(solution)/shard_map/all_to_all | solution.py:29
  49.6 0.7 pad_maximum_fusion
  50.4 4.5 %collective-permute-start.4 = (bf16[256,512]{1,0:T(8,128)(2,1)}, bf16[256,512]{1,0:T(8,128)(2,1)}, u32[]{:S(2)}, u32[]{:S(2)}) collective-permute-start(bf16[256,512]{1,0:T(8,128)(2,1)} %pad_maximum_fusion), channel_id=1, source_target_pairs={{0,2},{2,0},{4,6},{6,4},{8,10},{10,8},{12,14},{14,12},{16,18},{18,... | collective-permute-start | bytes 786440 | tf_op jit(solution)/shard_map/ppermute | solution.py:40
  54.9 1.5 collective-permute-done.4
  56.3 1.0 broadcast_select_fusion.1
  57.4 3.0 %convolution_convert_fusion = bf16[1024,512]{1,0:T(8,128)(2,1)} fusion(bf16[1024,512]{1,0:T(8,128)(2,1)} %bitcast.13, bf16[256,512]{1,0:T(8,128)(2,1)S(1)} %get-tuple-element.6, bf16[256,512]{1,0:T(8,128)(2,1)S(1)} %get-tuple-element.5), kind=kOutput, calls=%fused_computation.13 | convolution fusion | flops 538443776 | bytes 2621440 | tf_op jit(solution)/shard_map/tk,ck->tc/dot_general | solution.py:96
  60.3 4.7 %all-to-all-done = bf16[1,64,16,512]{3,1,0,2:T(8,128)(2,1)} async-done(((bf16[1,64,16,512]{3,1,0,2:T(8,128)(2,1)}), bf16[1,64,16,512]{3,1,0,2:T(8,128)(2,1)}, u32[]{:S(2)}, u32[]{:S(2)}) %all-to-all-start) | async-done | bytes 1048608 | tf_op jit(solution)/shard_map/all_to_all | solution.py:29
  65.0 4.3 %all-to-all-start.3 = ((bf16[16,64,1,512]{3,1,2,0:T(8,128)(2,1)}), bf16[16,64,1,512]{3,1,2,0:T(8,128)(2,1)}, u32[]{:S(2)}, u32[]{:S(2)}) async-start(bf16[16,64,1,512]{3,1,2,0:T(8,128)(2,1)} %bitcast.97), calls=%async_computation.3 | async-start | bytes 2097152 | tf_op jit(solution)/shard_map/all_to_all | solution.py:29
  69.4 2.3 %fusion.43 = f32[512,512]{1,0:T(8,128)S(1)} fusion(bf16[1024,512]{1,0:T(8,128)(2,1)} %bitcast.3, bf16[1024,512]{1,0:T(8,128)(2,1)} %bitcast.13), kind=kOutput, calls=%fused_computation.63 | convolution fusion | flops 536870912 | bytes 3145728 | tf_op jit(solution)/shard_map/tc,tk->ck/dot_general | solution.py:104
  71.7 1.0 copy-done.4
  72.6 0.7 dynamic-slice_convert_fusion
  73.4 4.9 %collective-permute-start.1 = (bf16[256,512]{1,0:T(8,128)(2,1)}, bf16[256,512]{1,0:T(8,128)(2,1)}, u32[]{:S(2)}, u32[]{:S(2)}) collective-permute-start(bf16[256,512]{1,0:T(8,128)(2,1)} %dynamic-slice_convert_fusion), channel_id=1, source_target_pairs={{0,2},{2,0},{4,6},{6,4},{8,10},{10,8},{12,14},{14,12},{16,18},{18,... | collective-permute-start | bytes 786440 | tf_op jit(solution)/shard_map/ppermute | solution.py:40
  78.4 0.1 convert_reduce_fusion
  78.5 1.3 collective-permute-done.1
  79.8 1.3 multiply_reduce_fusion
  81.1 0.8 copy-done.1
  81.9 1.7 %all-to-all-done.3 = bf16[16,64,1,512]{3,1,2,0:T(8,128)(2,1)} async-done(((bf16[16,64,1,512]{3,1,2,0:T(8,128)(2,1)}), bf16[16,64,1,512]{3,1,2,0:T(8,128)(2,1)}, u32[]{:S(2)}, u32[]{:S(2)}) %all-to-all-start.3) | async-done | bytes 1048608 | tf_op jit(solution)/shard_map/all_to_all | solution.py:29
  83.7 2.2 %fusion.2 = f32[64]{0:T(128)S(1)} fusion(f32[1,64,16,1,512]{4,2,1,3,0:T(8,128)S(1)} %bitcast.89, f32[64]{0:T(128)S(1)} %add_sqrt_fusion, f32[16,512]{1,0:T(8,128)S(1)} %mul.73, bf16[16,64,1,512]{3,1,2,0:T(8,128)(2,1)} %all-to-all-done.3), kind=kLoop, calls=%fused_computation.4 | loop fusion | flops 2621376 | bytes 3179008 | tf_op jit(solution)/shard_map/reduce_sum | solution.py:131
  85.9 1.8 %bitcast_convert_fusion = f32[16,1,64,1,512]{4,0,2,3,1:T(8,128)S(1)} fusion(bf16[16,64,1,512]{3,1,2,0:T(8,128)(2,1)} %all-to-all-done.3), kind=kLoop, calls=%fused_computation.21 | loop fusion | flops 524288 | bytes 3145728 | tf_op jit(solution)/shard_map/convert_element_type | solution.py:102
  87.7 1.2 copy.55
  89.0 0.5 fusion.7
  89.5 1.9 %collective-permute-start.5 = (bf16[64,8192]{1,0:T(8,128)(2,1)S(1)}, bf16[64,8192]{1,0:T(8,128)(2,1)}, u32[]{:S(2)}, u32[]{:S(2)}) collective-permute-start(bf16[64,8192]{1,0:T(8,128)(2,1)S(1)} %fusion.7), channel_id=1, source_target_pairs={{64,0},{128,64},{192,128},{256,192},{320,256},{384,320},{448,384},... | collective-permute-start | bytes 3145736 | tf_op jit(solution)/shard_map/ppermute | solution.py:16
  91.5 10.9 %collective-permute-start.3 = (bf16[272,256]{1,0:T(8,128)(2,1)S(1)}, bf16[272,256]{1,0:T(8,128)(2,1)S(1)}, u32[]{:S(2)}, u32[]{:S(2)}) collective-permute-start(bf16[272,256]{1,0:T(8,128)(2,1)S(1)} %pad_maximum_fusion.1), channel_id=1, source_target_pairs={{0,1},{1,0},{2,3},{3,2},{4,5},{5,4},{6,7},{7,6},{8,9},{9,8},{10,11... | collective-permute-start | bytes 417800 | tf_op jit(solution)/shard_map/ppermute | solution.py:20
  102.3 24.6 %collective-permute-done.3 = bf16[272,256]{1,0:T(8,128)(2,1)S(1)} collective-permute-done((bf16[272,256]{1,0:T(8,128)(2,1)S(1)}, bf16[272,256]{1,0:T(8,128)(2,1)S(1)}, u32[]{:S(2)}, u32[]{:S(2)}) %collective-permute-start.3) | collective-permute-done | bytes 139296 | tf_op jit(solution)/shard_map/ppermute | solution.py:20
  127.0 0.6 broadcast_in_dim.45
  127.6 15.0 %all-to-all-start.2 = ((f32[32,1,256]{2,1,0:T(1,128)}), f32[32,1,256]{2,1,0:T(1,128)S(1)}, u32[]{:S(2)}, u32[]{:S(2)}) async-start(f32[32,1,256]{2,1,0:T(1,128)} %broadcast_in_dim.45), calls=%async_computation.2 | async-start | bytes 65536 | tf_op jit(solution)/shard_map/all_to_all | solution.py:127
  142.7 0.8 fusion.19
  143.5 6.5 %all-to-all-done.2 = f32[32,1,256]{2,1,0:T(1,128)S(1)} async-done(((f32[32,1,256]{2,1,0:T(1,128)}), f32[32,1,256]{2,1,0:T(1,128)S(1)}, u32[]{:S(2)}, u32[]{:S(2)}) %all-to-all-start.2) | async-done | bytes 32800 | tf_op jit(solution)/shard_map/all_to_all | solution.py:127
  149.9 0.6 copy.78
  150.6 2.3 %copy.79 = bf16[1,64,8192]{2,1,0:T(8,128)(2,1)} copy(bf16[1,64,8192]{2,1,0:T(8,128)(2,1)} %bitcast.27) | data formatting | bytes 2097152
  (24 shorter events, 0.2 us)
Async XLA Ops:
  5.6 22.2 %copy-start.3 = (bf16[1,256,256]{2,1,0:T(8,128)(2,1)S(1)}, bf16[1,256,256]{2,1,0:T(8,128)(2,1)}, u32[]{:S(2)}) copy-start(bf16[1,256,256]{2,1,0:T(8,128)(2,1)} %param.9) | copy-start | bytes 393220
  5.7 34.8 %copy-start = (bf16[1,64,8192]{2,1,0:T(8,128)(2,1)S(1)}, bf16[1,64,8192]{2,1,0:T(8,128)(2,1)}, u32[]{:S(2)}) copy-start(bf16[1,64,8192]{2,1,0:T(8,128)(2,1)} %param.7) | copy-start | bytes 3145732
  5.8 14.0 %collective-permute-start = (bf16[64,256]{0,1:T(8,128)(2,1)S(1)}, bf16[64,256]{0,1:T(8,128)(2,1)S(1)}, u32[]{:S(2)}, u32[]{:S(2)}) collective-permute-start(bf16[64,256]{0,1:T(8,128)(2,1)S(1)} %get-tuple-element.8), channel_id=1, source_target_pairs={{0,1},{1,0},{2,3},{3,2},{4,5},{5,4},{6,7},{7,6},{8,9},{9,8},{10,11... | collective-permute-start | bytes 98312 | tf_op jit(solution)/shard_map/ppermute | solution.py:20
  21.0 22.0 %all-to-all-start.1 = ((bf16[16,64,512]{2,1,0:T(8,128)(2,1)}), bf16[16,64,512]{2,1,0:T(8,128)(2,1)}, u32[]{:S(2)}, u32[]{:S(2)}) async-start(bf16[16,64,512]{2,1,0:T(8,128)(2,1)} %broadcast_in_dim.23), calls=%async_computation.1 | async-start | bytes 2097152 | tf_op jit(solution)/shard_map/all_to_all | solution.py:29
  27.8 21.8 %collective-permute-start.2 = (bf16[256,256]{1,0:T(8,128)(2,1)S(1)}, bf16[256,256]{1,0:T(8,128)(2,1)S(1)}, u32[]{:S(2)}, u32[]{:S(2)}) collective-permute-start(bf16[256,256]{1,0:T(8,128)(2,1)S(1)} %bitcast.93), channel_id=1, source_target_pairs={{0,1},{1,0},{2,3},{3,2},{4,5},{5,4},{6,7},{7,6},{8,9},{9,8},{10,11... | collective-permute-start | bytes 393224 | tf_op jit(solution)/shard_map/ppermute | solution.py:20
  43.0 22.0 %all-to-all-start = ((bf16[1,64,16,512]{3,1,0,2:T(8,128)(2,1)}), bf16[1,64,16,512]{3,1,0,2:T(8,128)(2,1)}, u32[]{:S(2)}, u32[]{:S(2)}) async-start(bf16[1,64,16,512]{3,1,0,2:T(8,128)(2,1)} %copy.39), calls=%async_computation | async-start | bytes 2097152 | tf_op jit(solution)/shard_map/all_to_all | solution.py:29
  50.4 6.0 %collective-permute-start.4 = (bf16[256,512]{1,0:T(8,128)(2,1)}, bf16[256,512]{1,0:T(8,128)(2,1)}, u32[]{:S(2)}, u32[]{:S(2)}) collective-permute-start(bf16[256,512]{1,0:T(8,128)(2,1)} %pad_maximum_fusion), channel_id=1, source_target_pairs={{0,2},{2,0},{4,6},{6,4},{8,10},{10,8},{12,14},{14,12},{16,18},{18,... | collective-permute-start | bytes 786440 | tf_op jit(solution)/shard_map/ppermute | solution.py:40
  65.0 18.6 %all-to-all-start.3 = ((bf16[16,64,1,512]{3,1,2,0:T(8,128)(2,1)}), bf16[16,64,1,512]{3,1,2,0:T(8,128)(2,1)}, u32[]{:S(2)}, u32[]{:S(2)}) async-start(bf16[16,64,1,512]{3,1,2,0:T(8,128)(2,1)} %bitcast.97), calls=%async_computation.3 | async-start | bytes 2097152 | tf_op jit(solution)/shard_map/all_to_all | solution.py:29
  69.4 9.0 %copy-start.5 = (bf16[1,8192]{1,0:T(2,128)(2,1)S(1)}, bf16[1,8192]{1,0:T(2,128)(2,1)}, u32[]{:S(2)}) copy-start(bf16[1,8192]{1,0:T(2,128)(2,1)} %param.8) | copy-start | bytes 49156
  71.7 1.0 copy-start.4
  73.4 6.4 %collective-permute-start.1 = (bf16[256,512]{1,0:T(8,128)(2,1)}, bf16[256,512]{1,0:T(8,128)(2,1)}, u32[]{:S(2)}, u32[]{:S(2)}) collective-permute-start(bf16[256,512]{1,0:T(8,128)(2,1)} %dynamic-slice_convert_fusion), channel_id=1, source_target_pairs={{0,2},{2,0},{4,6},{6,4},{8,10},{10,8},{12,14},{14,12},{16,18},{18,... | collective-permute-start | bytes 786440 | tf_op jit(solution)/shard_map/ppermute | solution.py:40
  81.1 0.8 copy-start.1
  88.9 53.7 %copy-start.2 = (f32[256,512]{1,0:T(8,128)S(1)}, f32[256,512]{1,0:T(8,128)}, u32[]{:S(2)}) copy-start(f32[256,512]{1,0:T(8,128)} %copy-done.1) | copy-start | bytes 1572868
  89.5 60.5 %collective-permute-start.5 = (bf16[64,8192]{1,0:T(8,128)(2,1)S(1)}, bf16[64,8192]{1,0:T(8,128)(2,1)}, u32[]{:S(2)}, u32[]{:S(2)}) collective-permute-start(bf16[64,8192]{1,0:T(8,128)(2,1)S(1)} %fusion.7), channel_id=1, source_target_pairs={{64,0},{128,64},{192,128},{256,192},{320,256},{384,320},{448,384},... | collective-permute-start | bytes 3145736 | tf_op jit(solution)/shard_map/ppermute | solution.py:16
  91.5 35.5 %collective-permute-start.3 = (bf16[272,256]{1,0:T(8,128)(2,1)S(1)}, bf16[272,256]{1,0:T(8,128)(2,1)S(1)}, u32[]{:S(2)}, u32[]{:S(2)}) collective-permute-start(bf16[272,256]{1,0:T(8,128)(2,1)S(1)} %pad_maximum_fusion.1), channel_id=1, source_target_pairs={{0,1},{1,0},{2,3},{3,2},{4,5},{5,4},{6,7},{7,6},{8,9},{9,8},{10,11... | collective-permute-start | bytes 417800 | tf_op jit(solution)/shard_map/ppermute | solution.py:20
  127.6 22.3 %all-to-all-start.2 = ((f32[32,1,256]{2,1,0:T(1,128)}), f32[32,1,256]{2,1,0:T(1,128)S(1)}, u32[]{:S(2)}, u32[]{:S(2)}) async-start(f32[32,1,256]{2,1,0:T(1,128)} %broadcast_in_dim.45), calls=%async_computation.2 | async-start | bytes 65536 | tf_op jit(solution)/shard_map/all_to_all | solution.py:127

commit v3 on v2

--- a/solution.py
+++ b/solution.py
@@ -10,14 +10,12 @@
 QPK = 8
 
 
-def shifted(value, axis, steps):
-    count = lax.axis_size(axis)
-    first, last = (max(0, -steps), min(count, count - steps))
-    return lax.ppermute(value, axis, [(source, source + steps) for source in range(first, last)])
-
-
-def swapped(value):
-    return lax.ppermute(value, "tensor", [(0, 1), (1, 0)])
+def along(value, steps):
+    half = lax.axis_size("section")
+    count = 2 * half
+    place = [(plane % half) * 2 + plane // half for plane in range(count)]
+    pairs = [(place[plane], place[(plane + steps) % count]) for plane in range(count)]
+    return lax.ppermute(value, ("section", "tensor"), pairs)
 
 
 def same_core():
@@ -70,9 +68,16 @@
     return value_grad.reshape(length, groups * HD).astype(jnp.bfloat16)
 
 
+def statistics(rows):
+    rows_float = rows.astype(jnp.float32)
+    root_mean = jnp.sqrt(jnp.mean(rows_float * rows_float, axis=1, keepdims=True) + 1e-05)
+    return rows_float / root_mean, root_mean
+
+
 def layer(hidden_in, norm_gain, value_weight, query_vectors, key_vectors, grad_attn, positions):
     n_dp = lax.axis_size("dp")
     n_chip = n_dp // 2
+    n_section = lax.axis_size("section")
     here = lax.axis_index("dp")
     core = here % 2
     half = lax.axis_index("tensor")
@@ -80,19 +85,23 @@
     chunk = width // n_dp
     local_weight = value_weight[0]
     own_columns = local_weight.shape[1]
-    rows_float = hidden_in[0].astype(jnp.float32)
-    root_mean = jnp.sqrt(jnp.mean(rows_float * rows_float, axis=1, keepdims=True) + 1e-05)
-    normed = rows_float / root_mean
-    normed_columns = exchanged(
+    across = n_section - 1
+    work_hidden = along(hidden_in[0], -1)
+    normed, _ = statistics(hidden_in[0])
+    home_columns = exchanged(
         normed.astype(jnp.bfloat16).reshape(own_rows, n_chip, 2 * chunk), 1, 0
     ).reshape(n_chip * own_rows, 2 * chunk)
+    normed_columns = along(home_columns, -1)
     value_grad = attend(query_vectors[0], key_vectors[0], grad_attn[0], positions[0])
     kept = lax.dynamic_slice_in_dim(value_grad, half * own_rows, own_rows, 0)
     given = lax.dynamic_slice_in_dim(value_grad, (1 - half) * own_rows, own_rows, 0)
-    own_value = jnp.concatenate([kept, swapped(given)], axis=1)
-    device_weight = jnp.concatenate([local_weight, swapped(local_weight)], axis=1)
+    work_value = jnp.concatenate([along(kept, -1), along(given, across)], axis=1)
+    device_weight = jnp.concatenate(
+        [along(local_weight, -1), along(local_weight, across)],
+        axis=1,
+    )
     full_weight = by_core(core, device_weight, other_core(device_weight))
-    group_value = gathered(own_value).reshape(n_chip * own_rows, 2 * own_columns)
+    group_value = gathered(work_value).reshape(n_chip * own_rows, 2 * own_columns)
     grad_columns = jnp.einsum(
         "tk,ck->tc", group_value, full_weight, preferred_element_type=jnp.float32
     ).astype(jnp.bfloat16)
@@ -104,33 +113,28 @@
     group_term = jnp.einsum(
         "tc,tk->ck", normed_columns, group_value, preferred_element_type=jnp.float32
     )
+    group_sum = jnp.sum(group_term * full_weight.astype(jnp.float32), axis=1)
+    home_sum = along(group_sum, 1) + along(group_sum, -across)
+    all_sums = lax.all_to_all(
+        jnp.broadcast_to(home_sum[None], (n_dp, 2 * chunk)), "dp", 0, 0
+    )
+    gain_grad = jnp.sum(all_sums.reshape(n_chip, 2, 2 * chunk), axis=1).reshape(width)
     kept_term = lax.dynamic_slice_in_dim(group_term, core * chunk, chunk, 0)
     given_term = lax.dynamic_slice_in_dim(group_term, (1 - core) * chunk, chunk, 0)
     plane_term = kept_term + other_core(given_term.astype(jnp.bfloat16)).astype(jnp.float32)
-    gain_term = jnp.sum(plane_term * device_weight.astype(jnp.float32), axis=1)
-    gain_high = lax.reduce_precision(gain_term, 8, 7)
-    gain_low = gain_term - gain_high
-    sent_term = jnp.concatenate(
-        [
-            plane_term[:, own_columns:].astype(jnp.bfloat16),
-            jnp.pad(
-                jnp.stack([gain_high, gain_low]).astype(jnp.bfloat16), ((0, 14), (0, 0))
-            ),
-        ],
-        axis=0,
-    )
-    given_back = swapped(sent_term).astype(jnp.float32)
-    gain_float = norm_gain[0].astype(jnp.float32)
-    own_gain = lax.dynamic_slice_in_dim(gain_float, here * chunk, chunk, 0)
-    weight_grad = (plane_term[:, :own_columns] + given_back[:chunk]) * own_gain[:, None]
-    gain_chunk = gain_high + gain_low + given_back[chunk] + given_back[chunk + 1]
-    gain_grad = lax.all_to_all(
-        jnp.broadcast_to(gain_chunk[None], (n_dp, chunk)), "dp", 0, 0
-    ).reshape(width)
-    grad_normed = own_grad * gain_float
-    inner_mean = jnp.mean(grad_normed * normed, axis=1, keepdims=True)
-    grad_hidden = ((grad_normed - normed * inner_mean) / root_mean).astype(jnp.bfloat16)
-    to_previous = shifted(grad_hidden, "section", -1)
+    sent_term = plane_term.astype(jnp.bfloat16)
+    home_term = along(sent_term[:, :own_columns], 1).astype(jnp.float32) + along(
+        sent_term[:, own_columns:], -across
+    ).astype(jnp.float32)
+    own_gain = lax.dynamic_slice_in_dim(norm_gain[0], here * chunk, chunk, 0)
+    weight_grad = home_term * own_gain.astype(jnp.float32)[:, None]
+    work_gain = along(norm_gain[0], -1).astype(jnp.float32)
+    work_normed, root_mean = statistics(work_hidden)
+    last = lax.axis_index("section") == n_section - 1
+    grad_normed = own_grad * work_gain
+    inner_mean = jnp.mean(grad_normed * work_normed, axis=1, keepdims=True)
+    grad_hidden = (grad_normed - work_normed * inner_mean) / root_mean
+    to_previous = jnp.where(last, jnp.float32(0.0), grad_hidden).astype(jnp.bfloat16)
     return (weight_grad[None], gain_grad[None], to_previous[None])
 
 

time: 154 us -> 188 us (1.22)
  the two profiles are of different devices: /device:TPU:161 before, /device:TPU:35 now
where the time goes in v3:
time: 188 us; the launch traced here: 187 us
  starting transfers between devices  86.2 us (46%)
  waiting for transfers between devices  75.1 us (40%)
  local copies, waits for them, and re-layouts  11.9 us (6%)
  other arithmetic  6.91 us (4%)
  matrix products  5.49 us (3%)
    ppermute x11, waiting for transfers between devices, along(): return lax.ppermute(value, ('section', 'tensor'), pairs)  75.1 us
    ppermute x11, starting transfers between devices, along(): return lax.ppermute(value, ('section', 'tensor'), pairs)  52.3 us
    all_to_all x3, starting transfers between devices, exchanged(): lax.all_to_all(value, 'dp', split, joined, axis_index_groups=same_core())  20.3 us
    all_to_all x1, starting transfers between devices, layer(): lax.all_to_all(jnp.broadcast_to(home_sum[None], (n_dp, 2 * chunk)), 'dp',...  8.42 us
    ppermute x2, starting transfers between devices, other_core(): lax.ppermute(value, 'dp', [(source, source ^ 1) for source in range(count)])  5.26 us
    unnamed x29, local copies, waits for them, and re-layouts  5.24 us
  transfers between devices with their start and end apart: 17, of which 6 were waited for; matrix products, arithmetic and copies ran while one was open for 6% of the time, Pallas kernels for 0%

profile of v3, /device:TPU:35, one launch (start us, length us, event | category | flops | bytes accessed | tf_op | source)
XLA Modules:
  0.0 186.8 jit_solution(4369115414951218845)
XLA Ops:
  0.7 1.3 copy.91
  2.0 1.1 copy.95
  3.3 0.5 fusion.27
  3.8 0.3 fusion.8
  4.3 14.2 %collective-permute-start.2 = (bf16[64,256]{0,1:T(8,128)(2,1)S(1)}, bf16[64,256]{0,1:T(8,128)(2,1)S(1)}, u32[]{:S(2)}, u32[]{:S(2)}) collective-permute-start(bf16[64,256]{0,1:T(8,128)(2,1)S(1)} %get-tuple-element.32), channel_id=1, source_target_pairs={{0,448},{64,1},{128,65},{192,129},{256,193},{320,257},{384,321},{4... | collective-permute-start | bytes 98312 | tf_op jit(solution)/shard_map/ppermute | solution.py:18
  18.5 1.9 %collective-permute-start.1 = (bf16[64,256]{0,1:T(8,128)(2,1)S(1)}, bf16[64,256]{0,1:T(8,128)(2,1)S(1)}, u32[]{:S(2)}, u32[]{:S(2)}) collective-permute-start(bf16[64,256]{0,1:T(8,128)(2,1)S(1)} %get-tuple-element.31), channel_id=1, source_target_pairs={{0,449},{64,0},{128,64},{192,128},{256,192},{320,256},{384,320},{4... | collective-permute-start | bytes 98312 | tf_op jit(solution)/shard_map/ppermute | solution.py:18
  20.4 1.6 collective-permute-done.2
  22.1 1.5 collective-permute-done.1
  23.7 1.1 broadcast_in_dim.48
  24.7 6.9 %all-to-all-start.1 = ((bf16[16,64,512]{2,1,0:T(8,128)(2,1)}), bf16[16,64,512]{2,1,0:T(8,128)(2,1)S(1)}, u32[]{:S(2)}, u32[]{:S(2)}) async-start(bf16[16,64,512]{2,1,0:T(8,128)(2,1)} %broadcast_in_dim.48), calls=%async_computation.1 | async-start | bytes 2097152 | tf_op jit(solution)/shard_map/all_to_all | solution.py:27
  31.8 1.9 %collective-permute-start.6 = (bf16[256,256]{0,1:T(8,128)(2,1)S(1)}, bf16[256,256]{0,1:T(8,128)(2,1)S(1)}, u32[]{:S(2)}, u32[]{:S(2)}) collective-permute-start(bf16[256,256]{0,1:T(8,128)(2,1)S(1)} %bitcast.86), channel_id=1, source_target_pairs={{0,449},{64,0},{128,64},{192,128},{256,192},{320,256},{384,320},{4... | collective-permute-start | bytes 393224 | tf_op jit(solution)/shard_map/ppermute | solution.py:18
  33.7 9.6 %collective-permute-start.7 = (bf16[256,256]{0,1:T(8,128)(2,1)S(1)}, bf16[256,256]{0,1:T(8,128)(2,1)S(1)}, u32[]{:S(2)}, u32[]{:S(2)}) collective-permute-start(bf16[256,256]{0,1:T(8,128)(2,1)S(1)} %bitcast.87), channel_id=1, source_target_pairs={{0,448},{64,1},{128,65},{192,129},{256,193},{320,257},{384,321},{4... | collective-permute-start | bytes 393224 | tf_op jit(solution)/shard_map/ppermute | solution.py:18
  43.3 0.4 copy.94
  43.7 0.3 multiply_reduce_fusion.1
  44.0 0.3 fusion.2
  44.3 1.5 copy.75
  45.9 6.7 %all-to-all-start = ((bf16[1,64,16,512]{3,1,0,2:T(8,128)(2,1)}), bf16[1,64,16,512]{3,1,0,2:T(8,128)(2,1)}, u32[]{:S(2)}, u32[]{:S(2)}) async-start(bf16[1,64,16,512]{3,1,0,2:T(8,128)(2,1)} %copy.75), calls=%async_computation | async-start | bytes 2097152 | tf_op jit(solution)/shard_map/all_to_all | solution.py:27
  52.6 17.1 %collective-permute-done.7 = bf16[256,256]{0,1:T(8,128)(2,1)S(1)} collective-permute-done((bf16[256,256]{0,1:T(8,128)(2,1)S(1)}, bf16[256,256]{0,1:T(8,128)(2,1)S(1)}, u32[]{:S(2)}, u32[]{:S(2)}) %collective-permute-start.7) | collective-permute-done | bytes 131104 | tf_op jit(solution)/shard_map/ppermute | solution.py:18
  69.7 2.6 %collective-permute-start.8 = (bf16[256,512]{0,1:T(8,128)(2,1)S(1)}, bf16[256,512]{0,1:T(8,128)(2,1)}, u32[]{:S(2)}, u32[]{:S(2)}) collective-permute-start(bf16[256,512]{0,1:T(8,128)(2,1)S(1)} %constant_dynamic-update-slice_fusion), channel_id=1, source_target_pairs={{0,2},{2,0},{4,6},{6,4},{8,10},{10,8},{12,14},{14,12},{16,18},{18,... | collective-permute-start | bytes 786440 | tf_op jit(solution)/shard_map/ppermute | solution.py:38
  72.3 1.9 %collective-permute-start.12 = (bf16[64,8192]{1,0:T(8,128)(2,1)S(1)}, bf16[64,8192]{1,0:T(8,128)(2,1)S(1)}, u32[]{:S(2)}, u32[]{:S(2)}) collective-permute-start(bf16[64,8192]{1,0:T(8,128)(2,1)S(1)} %bitcast.77), channel_id=1, source_target_pairs={{0,449},{64,0},{128,64},{192,128},{256,192},{320,256},{384,320},{4... | collective-permute-start | bytes 3145736 | tf_op jit(solution)/shard_map/ppermute | solution.py:18
  74.2 1.0 broadcast_select_fusion.1
  75.2 0.7 copy-done.3
  76.0 1.7 convolution_convert_fusion
  77.7 6.7 %all-to-all-start.3 = ((bf16[16,64,1,512]{3,1,2,0:T(8,128)(2,1)}), bf16[16,64,1,512]{3,1,2,0:T(8,128)(2,1)S(1)}, u32[]{:S(2)}, u32[]{:S(2)}) async-start(bf16[16,64,1,512]{3,1,2,0:T(8,128)(2,1)} %bitcast.80), calls=%async_computation.3 | async-start | bytes 2097152 | tf_op jit(solution)/shard_map/all_to_all | solution.py:27
  84.4 1.9 %collective-permute-start = (bf16[1024,512]{1,0:T(8,128)(2,1)}, bf16[1024,512]{1,0:T(8,128)(2,1)}, u32[]{:S(2)}, u32[]{:S(2)}) collective-permute-start(bf16[1024,512]{1,0:T(8,128)(2,1)} %bitcast.3), channel_id=1, source_target_pairs={{0,449},{64,0},{128,64},{192,128},{256,192},{320,256},{384,320},{4... | collective-permute-start | bytes 3145736 | tf_op jit(solution)/shard_map/ppermute | solution.py:18
  86.4 1.9 %collective-permute-start.11 = (bf16[8192]{0:T(1024)(128)(2,1)S(1)}, bf16[8192]{0:T(1024)(128)(2,1)S(1)}, u32[]{:S(2)}, u32[]{:S(2)}) collective-permute-start(bf16[8192]{0:T(1024)(128)(2,1)S(1)} %reduce.1), channel_id=1, source_target_pairs={{0,449},{64,0},{128,64},{192,128},{256,192},{320,256},{384,320},{4... | collective-permute-start | bytes 49160 | tf_op jit(solution)/shard_map/ppermute | solution.py:18
  88.4 33.4 %collective-permute-done.11 = bf16[8192]{0:T(1024)(128)(2,1)S(1)} collective-permute-done((bf16[8192]{0:T(1024)(128)(2,1)S(1)}, bf16[8192]{0:T(1024)(128)(2,1)S(1)}, u32[]{:S(2)}, u32[]{:S(2)}) %collective-permute-start.11) | collective-permute-done | bytes 16416 | tf_op jit(solution)/shard_map/ppermute | solution.py:18
  121.8 0.3 fusion.1
  122.1 0.3 fusion.32
  122.7 1.0 copy-done.2
  123.8 3.0 %multiply_reduce_fusion.2 = (f32[512]{0:T(512)S(1)}, f32[512,512]{0,1:T(8,128)}) fusion(bf16[256,512]{0,1:T(8,128)(2,1)S(1)} %copy-done.6, bf16[256,512]{0,1:T(8,128)(2,1)S(1)} %copy-done.4, bf16[1024,512]{1,0:T(8,128)(2,1)} %collective-permute-done, bf16[1024,512]{1,0:T(8,128)(2,1)S(1)} %bitcast.79), kind=kOutput, calls=%fused_computation.19 | convolution fusion | flops 538443264 | bytes 3672064 | tf_op jit(solution)/shard_map/tc,tk->ck/dot_general | solution.py:113
  126.7 1.1 dynamic-slice_convert_fusion
  127.8 2.7 %collective-permute-start.3 = (bf16[256,512]{0,1:T(8,128)(2,1)S(1)}, bf16[256,512]{0,1:T(8,128)(2,1)}, u32[]{:S(2)}, u32[]{:S(2)}) collective-permute-start(bf16[256,512]{0,1:T(8,128)(2,1)S(1)} %dynamic-slice_convert_fusion), channel_id=1, source_target_pairs={{0,2},{2,0},{4,6},{6,4},{8,10},{10,8},{12,14},{14,12},{16,18},{18,... | collective-permute-start | bytes 786440 | tf_op jit(solution)/shard_map/ppermute | solution.py:38
  130.5 0.6 multiply_reduce_fusion
  131.1 2.6 %collective-permute-start.9 = (f32[512]{0:T(512)S(1)}, f32[512]{0:T(512)S(1)}, u32[]{:S(2)}, u32[]{:S(2)}) collective-permute-start(f32[512]{0:T(512)S(1)} %get-tuple-element.35), channel_id=1, source_target_pairs={{0,64},{64,128},{128,192},{192,256},{256,320},{320,384},{384,448},... | collective-permute-start | bytes 6152 | tf_op jit(solution)/shard_map/ppermute | solution.py:18
  133.7 7.3 %collective-permute-start.10 = (f32[512]{0:T(512)S(1)}, f32[512]{0:T(512)S(1)}, u32[]{:S(2)}, u32[]{:S(2)}) collective-permute-start(f32[512]{0:T(512)S(1)} %get-tuple-element.35), channel_id=1, source_target_pairs={{0,65},{64,129},{128,193},{192,257},{256,321},{320,385},{384,449},... | collective-permute-start | bytes 6152 | tf_op jit(solution)/shard_map/ppermute | solution.py:18
  141.0 4.8 %collective-permute-done.10 = f32[512]{0:T(512)S(1)} collective-permute-done((f32[512]{0:T(512)S(1)}, f32[512]{0:T(512)S(1)}, u32[]{:S(2)}, u32[]{:S(2)}) %collective-permute-start.10) | collective-permute-done | bytes 2080 | tf_op jit(solution)/shard_map/ppermute | solution.py:18
  145.8 0.7 broadcast_in_dim.50
  146.5 8.4 %all-to-all-start.2 = ((f32[32,1,512]{2,1,0:T(1,128)}), f32[32,1,512]{2,1,0:T(1,128)S(1)}, u32[]{:S(2)}, u32[]{:S(2)}) async-start(f32[32,1,512]{2,1,0:T(1,128)} %broadcast_in_dim.50), calls=%async_computation.2 | async-start | bytes 131072 | tf_op jit(solution)/shard_map/all_to_all | solution.py:118
  154.9 1.2 add_convert_fusion
  156.1 0.7 fusion.26
  156.8 7.0 %collective-permute-start.5 = (bf16[256,256]{0,1:T(8,128)(2,1)}, bf16[256,256]{0,1:T(8,128)(2,1)S(1)}, u32[]{:S(2)}, u32[]{:S(2)}) collective-permute-start(bf16[256,256]{0,1:T(8,128)(2,1)} %get-tuple-element.30), channel_id=1, source_target_pairs={{0,65},{64,129},{128,193},{192,257},{256,321},{320,385},{384,449},... | collective-permute-start | bytes 393224 | tf_op jit(solution)/shard_map/ppermute | solution.py:18
  163.8 1.9 %collective-permute-start.4 = (bf16[256,256]{0,1:T(8,128)(2,1)S(1)}, bf16[256,256]{0,1:T(8,128)(2,1)}, u32[]{:S(2)}, u32[]{:S(2)}) collective-permute-start(bf16[256,256]{0,1:T(8,128)(2,1)S(1)} %get-tuple-element.29), channel_id=1, source_target_pairs={{0,64},{64,128},{128,192},{192,256},{256,320},{320,384},{384,448},... | collective-permute-start | bytes 393224 | tf_op jit(solution)/shard_map/ppermute | solution.py:18
  165.8 1.5 fusion.9
  167.6 0.6 copy.96
  168.2 16.7 %collective-permute-done.5 = bf16[256,256]{0,1:T(8,128)(2,1)S(1)} collective-permute-done((bf16[256,256]{0,1:T(8,128)(2,1)}, bf16[256,256]{0,1:T(8,128)(2,1)S(1)}, u32[]{:S(2)}, u32[]{:S(2)}) %collective-permute-start.5) | collective-permute-done | bytes 131104 | tf_op jit(solution)/shard_map/ppermute | solution.py:18
  185.0 0.9 multiply_bitcast_fusion
  185.9 0.8 copy.85
  (50 shorter events, 1.3 us)
Async XLA Ops:
  0.6 2.5 %copy-start.10 = (s32[1,128]{1,0:T(1,128)S(1)}, s32[1,128]{1,0:T(1,128)}, u32[]{:S(2)}) copy-start(s32[1,128]{1,0:T(1,128)} %param.13) | copy-start | bytes 1540
  0.6 2.6 %copy-start.8 = (bf16[1,128,256]{2,1,0:T(8,128)(2,1)S(1)}, bf16[1,128,256]{2,1,0:T(8,128)(2,1)}, u32[]{:S(2)}) copy-start(bf16[1,128,256]{2,1,0:T(8,128)(2,1)} %param.11) | copy-start | bytes 196612
  4.1 27.5 %copy-start.7 = (bf16[1,256,256]{2,1,0:T(8,128)(2,1)S(1)}, bf16[1,256,256]{2,1,0:T(8,128)(2,1)}, u32[]{:S(2)}) copy-start(bf16[1,256,256]{2,1,0:T(8,128)(2,1)} %param.9) | copy-start | bytes 393220
  4.1 39.2 %copy-start = (bf16[1,64,8192]{2,1,0:T(8,128)(2,1)S(1)}, bf16[1,64,8192]{2,1,0:T(8,128)(2,1)}, u32[]{:S(2)}) copy-start(bf16[1,64,8192]{2,1,0:T(8,128)(2,1)} %param.7) | copy-start | bytes 3145732
  4.3 17.8 %collective-permute-start.2 = (bf16[64,256]{0,1:T(8,128)(2,1)S(1)}, bf16[64,256]{0,1:T(8,128)(2,1)S(1)}, u32[]{:S(2)}, u32[]{:S(2)}) collective-permute-start(bf16[64,256]{0,1:T(8,128)(2,1)S(1)} %get-tuple-element.32), channel_id=1, source_target_pairs={{0,448},{64,1},{128,65},{192,129},{256,193},{320,257},{384,321},{4... | collective-permute-start | bytes 98312 | tf_op jit(solution)/shard_map/ppermute | solution.py:18
  18.5 5.0 %collective-permute-start.1 = (bf16[64,256]{0,1:T(8,128)(2,1)S(1)}, bf16[64,256]{0,1:T(8,128)(2,1)S(1)}, u32[]{:S(2)}, u32[]{:S(2)}) collective-permute-start(bf16[64,256]{0,1:T(8,128)(2,1)S(1)} %get-tuple-element.31), channel_id=1, source_target_pairs={{0,449},{64,0},{128,64},{192,128},{256,192},{320,256},{384,320},{4... | collective-permute-start | bytes 98312 | tf_op jit(solution)/shard_map/ppermute | solution.py:18
  24.7 21.2 %all-to-all-start.1 = ((bf16[16,64,512]{2,1,0:T(8,128)(2,1)}), bf16[16,64,512]{2,1,0:T(8,128)(2,1)S(1)}, u32[]{:S(2)}, u32[]{:S(2)}) async-start(bf16[16,64,512]{2,1,0:T(8,128)(2,1)} %broadcast_in_dim.48), calls=%async_computation.1 | async-start | bytes 2097152 | tf_op jit(solution)/shard_map/all_to_all | solution.py:27
  31.8 20.8 %collective-permute-start.6 = (bf16[256,256]{0,1:T(8,128)(2,1)S(1)}, bf16[256,256]{0,1:T(8,128)(2,1)S(1)}, u32[]{:S(2)}, u32[]{:S(2)}) collective-permute-start(bf16[256,256]{0,1:T(8,128)(2,1)S(1)} %bitcast.86), channel_id=1, source_target_pairs={{0,449},{64,0},{128,64},{192,128},{256,192},{320,256},{384,320},{4... | collective-permute-start | bytes 393224 | tf_op jit(solution)/shard_map/ppermute | solution.py:18
  33.7 36.0 %collective-permute-start.7 = (bf16[256,256]{0,1:T(8,128)(2,1)S(1)}, bf16[256,256]{0,1:T(8,128)(2,1)S(1)}, u32[]{:S(2)}, u32[]{:S(2)}) collective-permute-start(bf16[256,256]{0,1:T(8,128)(2,1)S(1)} %bitcast.87), channel_id=1, source_target_pairs={{0,448},{64,1},{128,65},{192,129},{256,193},{320,257},{384,321},{4... | collective-permute-start | bytes 393224 | tf_op jit(solution)/shard_map/ppermute | solution.py:18
  45.9 31.8 %copy-start.1 = (bf16[16,64,512]{2,1,0:T(8,128)(2,1)}, bf16[16,64,512]{2,1,0:T(8,128)(2,1)S(1)}, u32[]{:S(2)}) copy-start(bf16[16,64,512]{2,1,0:T(8,128)(2,1)S(1)} %all-to-all-done.1) | copy-start | bytes 3145732
  45.9 31.8 %all-to-all-start = ((bf16[1,64,16,512]{3,1,0,2:T(8,128)(2,1)}), bf16[1,64,16,512]{3,1,0,2:T(8,128)(2,1)}, u32[]{:S(2)}, u32[]{:S(2)}) async-start(bf16[1,64,16,512]{3,1,0,2:T(8,128)(2,1)} %copy.75), calls=%async_computation | async-start | bytes 2097152 | tf_op jit(solution)/shard_map/all_to_all | solution.py:27
  69.7 4.5 %collective-permute-start.8 = (bf16[256,512]{0,1:T(8,128)(2,1)S(1)}, bf16[256,512]{0,1:T(8,128)(2,1)}, u32[]{:S(2)}, u32[]{:S(2)}) collective-permute-start(bf16[256,512]{0,1:T(8,128)(2,1)S(1)} %constant_dynamic-update-slice_fusion), channel_id=1, source_target_pairs={{0,2},{2,0},{4,6},{6,4},{8,10},{10,8},{12,14},{14,12},{16,18},{18,... | collective-permute-start | bytes 786440 | tf_op jit(solution)/shard_map/ppermute | solution.py:38
  72.3 49.5 %collective-permute-start.12 = (bf16[64,8192]{1,0:T(8,128)(2,1)S(1)}, bf16[64,8192]{1,0:T(8,128)(2,1)S(1)}, u32[]{:S(2)}, u32[]{:S(2)}) collective-permute-start(bf16[64,8192]{1,0:T(8,128)(2,1)S(1)} %bitcast.77), channel_id=1, source_target_pairs={{0,449},{64,0},{128,64},{192,128},{256,192},{320,256},{384,320},{4... | collective-permute-start | bytes 3145736 | tf_op jit(solution)/shard_map/ppermute | solution.py:18
  75.2 0.7 copy-start.3
  75.2 0.8 copy-start.5
  76.0 10.3 %copy-start.9 = (bf16[1,8192]{1,0:T(2,128)(2,1)S(1)}, bf16[1,8192]{1,0:T(2,128)(2,1)}, u32[]{:S(2)}) copy-start(bf16[1,8192]{1,0:T(2,128)(2,1)} %param.8) | copy-start | bytes 49156
  77.7 44.4 %all-to-all-start.3 = ((bf16[16,64,1,512]{3,1,2,0:T(8,128)(2,1)}), bf16[16,64,1,512]{3,1,2,0:T(8,128)(2,1)S(1)}, u32[]{:S(2)}, u32[]{:S(2)}) async-start(bf16[16,64,1,512]{3,1,2,0:T(8,128)(2,1)} %bitcast.80), calls=%async_computation.3 | async-start | bytes 2097152 | tf_op jit(solution)/shard_map/all_to_all | solution.py:27
  84.4 38.3 %collective-permute-start = (bf16[1024,512]{1,0:T(8,128)(2,1)}, bf16[1024,512]{1,0:T(8,128)(2,1)}, u32[]{:S(2)}, u32[]{:S(2)}) collective-permute-start(bf16[1024,512]{1,0:T(8,128)(2,1)} %bitcast.3), channel_id=1, source_target_pairs={{0,449},{64,0},{128,64},{192,128},{256,192},{320,256},{384,320},{4... | collective-permute-start | bytes 3145736 | tf_op jit(solution)/shard_map/ppermute | solution.py:18
  86.4 35.4 %collective-permute-start.11 = (bf16[8192]{0:T(1024)(128)(2,1)S(1)}, bf16[8192]{0:T(1024)(128)(2,1)S(1)}, u32[]{:S(2)}, u32[]{:S(2)}) collective-permute-start(bf16[8192]{0:T(1024)(128)(2,1)S(1)} %reduce.1), channel_id=1, source_target_pairs={{0,449},{64,0},{128,64},{192,128},{256,192},{320,256},{384,320},{4... | collective-permute-start | bytes 49160 | tf_op jit(solution)/shard_map/ppermute | solution.py:18
  122.4 1.2 copy-start.2
  122.4 1.3 copy-start.4
  122.4 1.3 copy-start.6
  127.8 27.1 %collective-permute-start.3 = (bf16[256,512]{0,1:T(8,128)(2,1)S(1)}, bf16[256,512]{0,1:T(8,128)(2,1)}, u32[]{:S(2)}, u32[]{:S(2)}) collective-permute-start(bf16[256,512]{0,1:T(8,128)(2,1)S(1)} %dynamic-slice_convert_fusion), channel_id=1, source_target_pairs={{0,2},{2,0},{4,6},{6,4},{8,10},{10,8},{12,14},{14,12},{16,18},{18,... | collective-permute-start | bytes 786440 | tf_op jit(solution)/shard_map/ppermute | solution.py:38
  131.1 10.0 %collective-permute-start.9 = (f32[512]{0:T(512)S(1)}, f32[512]{0:T(512)S(1)}, u32[]{:S(2)}, u32[]{:S(2)}) collective-permute-start(f32[512]{0:T(512)S(1)} %get-tuple-element.35), channel_id=1, source_target_pairs={{0,64},{64,128},{128,192},{192,256},{256,320},{320,384},{384,448},... | collective-permute-start | bytes 6152 | tf_op jit(solution)/shard_map/ppermute | solution.py:18
  133.7 12.1 %collective-permute-start.10 = (f32[512]{0:T(512)S(1)}, f32[512]{0:T(512)S(1)}, u32[]{:S(2)}, u32[]{:S(2)}) collective-permute-start(f32[512]{0:T(512)S(1)} %get-tuple-element.35), channel_id=1, source_target_pairs={{0,65},{64,129},{128,193},{192,257},{256,321},{320,385},{384,449},... | collective-permute-start | bytes 6152 | tf_op jit(solution)/shard_map/ppermute | solution.py:18
  146.5 20.8 %all-to-all-start.2 = ((f32[32,1,512]{2,1,0:T(1,128)}), f32[32,1,512]{2,1,0:T(1,128)S(1)}, u32[]{:S(2)}, u32[]{:S(2)}) async-start(f32[32,1,512]{2,1,0:T(1,128)} %broadcast_in_dim.50), calls=%async_computation.2 | async-start | bytes 131072 | tf_op jit(solution)/shard_map/all_to_all | solution.py:118
  156.8 28.2 %collective-permute-start.5 = (bf16[256,256]{0,1:T(8,128)(2,1)}, bf16[256,256]{0,1:T(8,128)(2,1)S(1)}, u32[]{:S(2)}, u32[]{:S(2)}) collective-permute-start(bf16[256,256]{0,1:T(8,128)(2,1)} %get-tuple-element.30), channel_id=1, source_target_pairs={{0,65},{64,129},{128,193},{192,257},{256,321},{320,385},{384,449},... | collective-permute-start | bytes 393224 | tf_op jit(solution)/shard_map/ppermute | solution.py:18
  163.8 21.2 %collective-permute-start.4 = (bf16[256,256]{0,1:T(8,128)(2,1)S(1)}, bf16[256,256]{0,1:T(8,128)(2,1)}, u32[]{:S(2)}, u32[]{:S(2)}) collective-permute-start(bf16[256,256]{0,1:T(8,128)(2,1)S(1)} %get-tuple-element.29), channel_id=1, source_target_pairs={{0,64},{64,128},{128,192},{192,256},{256,320},{320,384},{384,448},... | collective-permute-start | bytes 393224 | tf_op jit(solution)/shard_map/ppermute | solution.py:18

commit v4 on v3

v4 whole, which is shorter than its diff:
```python
import math

import jax
import jax.numpy as jnp
from jax import lax
from jax.experimental import pallas as pl
from jax.experimental.pallas import tpu as pltpu
from jax.sharding import PartitionSpec as P


HD = 128
QPK = 8


def along(value, steps):
    half = lax.axis_size("section")
    count = 2 * half
    place = [(plane % half) * 2 + plane // half for plane in range(count)]
    pairs = [(place[plane], place[(plane + steps) % count]) for plane in range(count)]
    return lax.ppermute(value, ("section", "tensor"), pairs)


def same_core():
    count = lax.axis_size("dp")
    return [list(range(core, count, 2)) for core in range(2)]


def exchanged(value, split, joined):
    return lax.all_to_all(value, "dp", split, joined, axis_index_groups=same_core())


def gathered(value):
    count = lax.axis_size("dp") // 2
    copies = jnp.broadcast_to(value[None], (count,) + value.shape)
    return exchanged(copies, 0, 0)


def other_core(value):
    count = lax.axis_size("dp")
    return lax.ppermute(value, "dp", [(source, source ^ 1) for source in range(count)])


def by_core(core, own, other):
    first = jnp.where(core == 0, own, other)
    second = jnp.where(core == 0, other, own)
    return jnp.concatenate([first, second], axis=0)


def whole(memory=pltpu.VMEM):
    return pl.BlockSpec(memory_space=memory)


def norm_kernel(hidden_ref, normed_ref):
    rows = hidden_ref[...].astype(jnp.float32)
    root_mean = jnp.sqrt(jnp.mean(rows * rows, axis=1, keepdims=True) + 1e-05)
    normed = (rows / root_mean).astype(jnp.bfloat16)
    count, _, columns = normed_ref.shape
    for place in range(count):
        normed_ref[place] = normed[:, place * columns : (place + 1) * columns]


def normed_blocks(rows, count):
    length, width = rows.shape
    return pl.pallas_call(
        norm_kernel,
        out_shape=jax.ShapeDtypeStruct((count, length, width // count), jnp.bfloat16),
        in_specs=[whole()],
        out_specs=whole(),
    )(rows)


def attend_kernel(half_ref, query_ref, key_ref, grad_ref, position_ref, kept_ref, given_ref, scratch_ref):
    length = query_ref.shape[0]
    groups = key_ref.shape[1] // HD
    seen_row = lax.broadcasted_iota(jnp.int32, (length, length), 0)
    query_row = lax.broadcasted_iota(jnp.int32, (length, length), 1)
    query_start = jnp.broadcast_to(position_ref[...], (length, length)) - query_row
    seen_start = query_start.T
    visible = (seen_row <= query_row) & (query_start == seen_start)
    for group in range(groups):
        keys = key_ref[:, group * HD : (group + 1) * HD]
        total = jnp.zeros((length, HD), jnp.float32)
        for head in range(group * QPK, (group + 1) * QPK):
            queries = query_ref[:, head * HD : (head + 1) * HD]
            scores = lax.dot_general(
                keys, queries, (((1,), (1,)), ((), ())), preferred_element_type=jnp.float32
            ) * (1.0 / math.sqrt(HD))
            masked = jnp.where(visible, scores, jnp.float32(-1e30))
            largest = jnp.max(masked, axis=0, keepdims=True)
            powers = jnp.where(visible, jnp.exp(masked - largest), jnp.float32(0.0))
            weights = powers / jnp.sum(powers, axis=0, keepdims=True)
            total += lax.dot_general(
                weights.astype(jnp.bfloat16),
                grad_ref[:, head * HD : (head + 1) * HD],
                (((1,), (0,)), ((), ())),
                preferred_element_type=jnp.float32,
            )
        scratch_ref[:, group * HD : (group + 1) * HD] = total
    rows = kept_ref.shape[0]
    half = half_ref[0]
    kept_ref[...] = scratch_ref[pl.ds(half * rows, rows), :].astype(jnp.bfloat16)
    given_ref[...] = scratch_ref[pl.ds((1 - half) * rows, rows), :].astype(jnp.bfloat16)


def attend(half, query_rows, key_rows, grad_rows, position_rows):
    length, columns = key_rows.shape
    part = jax.ShapeDtypeStruct((length // 2, columns), jnp.bfloat16)
    return pl.pallas_call(
        attend_kernel,
        out_shape=(part, part),
        in_specs=[whole(pltpu.SMEM)] + [whole()] * 4,
        out_specs=(whole(), whole()),
        scratch_shapes=[pltpu.VMEM((length, columns), jnp.float32)],
    )(half[None], query_rows, key_rows, grad_rows, position_rows)


def finish_kernel(last_ref, grad_ref, hidden_ref, result_ref):
    rows = hidden_ref[...].astype(jnp.float32)
    root_mean = jnp.sqrt(jnp.mean(rows * rows, axis=1, keepdims=True) + 1e-05)
    count, _, columns = grad_ref.shape
    total = jnp.zeros_like(root_mean)
    for place in range(count):
        block = rows[:, place * columns : (place + 1) * columns] / root_mean
        total += jnp.sum(grad_ref[place].astype(jnp.float32) * block, axis=1, keepdims=True)
    inner_mean = total / rows.shape[1]
    for place in range(count):
        part = pl.ds(place * columns, columns)
        normed = rows[:, place * columns : (place + 1) * columns] / root_mean
        grad_hidden = (grad_ref[place].astype(jnp.float32) - normed * inner_mean) / root_mean
        result_ref[:, part] = jnp.where(last_ref[0] != 0, jnp.float32(0.0), grad_hidden).astype(
            jnp.bfloat16
        )


def finished(last, grad_blocks, rows):
    return pl.pallas_call(
        finish_kernel,
        out_shape=jax.ShapeDtypeStruct(rows.shape, jnp.bfloat16),
        in_specs=[whole(pltpu.SMEM), whole(), whole()],
        out_specs=whole(),
    )(last.astype(jnp.int32)[None], grad_blocks, rows)


def layer(hidden_in, norm_gain, value_weight, query_vectors, key_vectors, grad_attn, positions):
    n_dp = lax.axis_size("dp")
    n_chip = n_dp // 2
    n_section = lax.axis_size("section")
    here = lax.axis_index("dp")
    core = here % 2
    half = lax.axis_index("tensor")
    own_rows, width = hidden_in.shape[1:]
    chunk = width // n_dp
    local_weight = value_weight[0]
    own_columns = local_weight.shape[1]
    across = n_section - 1
    own_gain = lax.dynamic_slice_in_dim(norm_gain[0], here * chunk, chunk, 0)
    gained_weight = jnp.concatenate(
        [local_weight, jnp.broadcast_to(own_gain.reshape(1, -1), (16, own_columns))], axis=0
    )
    work_weight = along(gained_weight, -1)
    other_weight = along(local_weight, across)
    normed = normed_blocks(hidden_in[0], n_chip)
    home_columns = exchanged(normed, 0, 0).reshape(n_chip * own_rows, 2 * chunk)
    work_hidden = along(hidden_in[0], -1)
    kept, given = attend(half, query_vectors[0], key_vectors[0], grad_attn[0], positions)
    work_value = jnp.concatenate([along(kept, -1), along(given, across)], axis=1)
    normed_columns = along(home_columns, -1)
    device_weight = jnp.concatenate(
        [
            jnp.concatenate([work_weight[:chunk], other_weight], axis=1),
            jnp.concatenate([work_weight[chunk:], work_weight[chunk:]], axis=1),
        ],
        axis=0,
    )
    swapped_weight = other_core(device_weight)
    full_weight = by_core(core, device_weight[:chunk], swapped_weight[:chunk])
    work_gain = by_core(
        core, device_weight[chunk, :own_columns], swapped_weight[chunk, :own_columns]
    ).astype(jnp.float32)
    group_value = gathered(work_value).reshape(n_chip * own_rows, 2 * own_columns)
    group_term = jnp.einsum(
        "tc,tk->ck", normed_columns, group_value, preferred_element_type=jnp.float32
    )
    group_sum = jnp.sum(group_term * full_weight.astype(jnp.float32), axis=1)
    kept_term = lax.dynamic_slice_in_dim(group_term, core * chunk, chunk, 0)
    given_term = lax.dynamic_slice_in_dim(group_term, (1 - core) * chunk, chunk, 0)
    plane_term = kept_term + other_core(given_term.astype(jnp.bfloat16)).astype(jnp.float32)
    grad_columns = (
        jnp.einsum("tk,ck->tc", group_value, full_weight, preferred_element_type=jnp.float32)
        * work_gain
    ).astype(jnp.bfloat16)
    grad_blocks = exchanged(grad_columns.reshape(n_chip, own_rows, 2 * chunk), 0, 0)
    sent_term = plane_term.astype(jnp.bfloat16)
    home_term = along(sent_term[:, :own_columns], 1).astype(jnp.float32) + along(
        sent_term[:, own_columns:], -across
    ).astype(jnp.float32)
    weight_grad = home_term * own_gain.astype(jnp.float32)[:, None]
    home_sum = along(group_sum, 1) + along(group_sum, -across)
    all_sums = lax.all_to_all(
        jnp.broadcast_to(home_sum[None], (n_dp, 2 * chunk)), "dp", 0, 0
    )
    gain_grad = jnp.sum(all_sums.reshape(n_chip, 2, 2 * chunk), axis=1).reshape(width)
    to_previous = finished(
        lax.axis_index("section") == n_section - 1, grad_blocks, work_hidden
    )
    return (weight_grad[None], gain_grad[None], to_previous[None])


def solution(mesh):
    placed = (
        P("section", ("dp", "tensor"), None),
        P("section", None),
        P("section", "dp", "tensor"),
        P("section", "dp", "tensor"),
        P("section", "dp", "tensor"),
        P("section", "dp", "tensor"),
        P("section", "dp"),
    )
    return jax.shard_map(
        layer,
        mesh=mesh,
        in_specs=placed,
        out_specs=(
            P("section", "dp", "tensor"),
            P("section", None),
            P("section", ("dp", "tensor"), None),
        ),
        check_vma=False,
    )
```

time: 188 us -> 151 us (0.80)
  the two profiles are of different devices: /device:TPU:35 before, /device:TPU:129 now
where the time goes in v4:
time: 151 us; the launch traced here: 150 us
  starting transfers between devices  76.5 us (51%)
  waiting for transfers between devices  49 us (32%)
  Pallas kernels  9.47 us (6%)
  local copies, waits for them, and re-layouts  6.24 us (4%)
  matrix products  5.24 us (3%)
  other arithmetic  2.65 us (2%)
    ppermute x10, starting transfers between devices, along(): return lax.ppermute(value, ('section', 'tensor'), pairs)  41 us
    ppermute x10, waiting for transfers between devices, along(): return lax.ppermute(value, ('section', 'tensor'), pairs)  37.7 us
    all_to_all x3, starting transfers between devices, exchanged(): lax.all_to_all(value, 'dp', split, joined, axis_index_groups=same_core())  18 us
    all_to_all x1, starting transfers between devices, layer(): lax.all_to_all(jnp.broadcast_to(home_sum[None], (n_dp, 2 * chunk)), 'dp',...  9.27 us
    ppermute x2, starting transfers between devices, other_core(): lax.ppermute(value, 'dp', [(source, source ^ 1) for source in range(count)])  8.25 us
    all_to_all x3, waiting for transfers between devices, exchanged(): lax.all_to_all(value, 'dp', split, joined, axis_index_groups=same_core())  7.42 us
    pallas_call x1, Pallas kernels, finished(): pl.pallas_call(finish_kernel, out_shape=jax.ShapeDtypeStruct(rows.shape,...  3.67 us
    unnamed x21, local copies, waits for them, and re-layouts  3.56 us
  transfers between devices with their start and end apart: 16, of which 6 were waited for; matrix products, arithmetic and copies ran while one was open for 7% of the time, Pallas kernels for 5%

profile of v4, /device:TPU:129, one launch (start us, length us, event | category | flops | bytes accessed | tf_op | source)
XLA Modules:
  0.0 150.2 jit_solution(9346981945419992522)
XLA Ops:
  0.6 0.0 copy-start
  0.6 2.7 %shard_map.95 = bf16[16,64,512]{2,1,0:T(8,128)(2,1)} custom-call(bf16[64,8192]{1,0:T(8,128)(2,1)} %bitcast.29), custom_call_target="tpu_custom_call" | custom-call | tf_op jit(solution)/shard_map/pallas_call | solution.py:64
  3.3 6.9 %all-to-all-start.1 = ((bf16[16,64,512]{2,1,0:T(8,128)(2,1)}), bf16[16,64,512]{2,1,0:T(8,128)(2,1)}, u32[]{:S(2)}, u32[]{:S(2)}) async-start(bf16[16,64,512]{2,1,0:T(8,128)(2,1)} %shard_map.95), calls=%async_computation.1 | async-start | bytes 2097152 | tf_op jit(solution)/shard_map/all_to_all | solution.py:29
  10.3 0.1 copy.24
  10.4 10.2 %collective-permute-start.7 = (bf16[256,256]{0,1:T(8,128)(2,1)S(1)}, bf16[256,256]{0,1:T(8,128)(2,1)S(1)}, u32[]{:S(2)}, u32[]{:S(2)}) collective-permute-start(bf16[256,256]{0,1:T(8,128)(2,1)S(1)} %bitcast.35), channel_id=1, source_target_pairs={{0,448},{64,1},{128,65},{192,129},{256,193},{320,257},{384,321},{4... | collective-permute-start | bytes 393224 | tf_op jit(solution)/shard_map/ppermute | solution.py:20
  20.6 3.1 %shard_map.94 = (bf16[64,256]{1,0:T(8,128)(2,1)}, bf16[64,256]{1,0:T(8,128)(2,1)}) custom-call(s32[1]{0:T(128)} %bitcast.half_ref, bf16[128,2048]{1,0:T(8,128)(2,1)} %bitcast.33, bf16[128,256]{1,0:T(8,128)(2,1)} %bitcast.38, bf16[128,2048]{1,0:T(8,128)(2,1)} %bitcast.34, s32[1,128]{1,0:T(1,128)} %position_ref.1), custom_call_target="tpu_custom_call" | custom-call | tf_op jit(solution)/shard_map/pallas_call | solution.py:108
  23.7 1.9 %collective-permute-start.1 = (bf16[64,256]{1,0:T(8,128)(2,1)}, bf16[64,256]{1,0:T(8,128)(2,1)S(1)}, u32[]{:S(2)}, u32[]{:S(2)}) collective-permute-start(bf16[64,256]{1,0:T(8,128)(2,1)} %get-tuple-element.6), channel_id=1, source_target_pairs={{0,448},{64,1},{128,65},{192,129},{256,193},{320,257},{384,321},{4... | collective-permute-start | bytes 98312 | tf_op jit(solution)/shard_map/ppermute | solution.py:20
  25.6 3.8 %collective-permute-start = (bf16[64,256]{1,0:T(8,128)(2,1)}, bf16[64,256]{1,0:T(8,128)(2,1)S(1)}, u32[]{:S(2)}, u32[]{:S(2)}) collective-permute-start(bf16[64,256]{1,0:T(8,128)(2,1)} %get-tuple-element.5), channel_id=1, source_target_pairs={{0,449},{64,0},{128,64},{192,128},{256,192},{320,256},{384,320},{4... | collective-permute-start | bytes 98312 | tf_op jit(solution)/shard_map/ppermute | solution.py:20
  29.5 0.1 broadcast_in_dim.36
  29.6 2.6 %collective-permute-start.6 = (bf16[272,256]{0,1:T(8,128)(2,1)S(1)}, bf16[272,256]{0,1:T(8,128)(2,1)S(1)}, u32[]{:S(2)}, u32[]{:S(2)}) collective-permute-start(bf16[272,256]{0,1:T(8,128)(2,1)S(1)} %pad_maximum_fusion.3), channel_id=1, source_target_pairs={{0,449},{64,0},{128,64},{192,128},{256,192},{320,256},{384,320},{4... | collective-permute-start | bytes 417800 | tf_op jit(solution)/shard_map/ppermute | solution.py:20
  32.3 14.3 %collective-permute-done.1 = bf16[64,256]{1,0:T(8,128)(2,1)S(1)} collective-permute-done((bf16[64,256]{1,0:T(8,128)(2,1)}, bf16[64,256]{1,0:T(8,128)(2,1)S(1)}, u32[]{:S(2)}, u32[]{:S(2)}) %collective-permute-start.1) | collective-permute-done | bytes 32800 | tf_op jit(solution)/shard_map/ppermute | solution.py:20
  46.6 1.1 broadcast_in_dim.34
  47.7 6.7 %all-to-all-start = ((bf16[16,64,512]{2,1,0:T(8,128)(2,1)}), bf16[16,64,512]{2,1,0:T(8,128)(2,1)}, u32[]{:S(2)}, u32[]{:S(2)}) async-start(bf16[16,64,512]{2,1,0:T(8,128)(2,1)} %broadcast_in_dim.34), calls=%async_computation | async-start | bytes 2097152 | tf_op jit(solution)/shard_map/all_to_all | solution.py:29
  54.3 0.0 copy-start.2
  54.3 0.0 collective-permute-done.6
  54.4 2.5 %collective-permute-start.2 = (bf16[1024,512]{1,0:T(8,128)(2,1)}, bf16[1024,512]{1,0:T(8,128)(2,1)}, u32[]{:S(2)}, u32[]{:S(2)}) collective-permute-start(bf16[1024,512]{1,0:T(8,128)(2,1)} %bitcast.6), channel_id=1, source_target_pairs={{0,449},{64,0},{128,64},{192,128},{256,192},{320,256},{384,320},{4... | collective-permute-start | bytes 3145736 | tf_op jit(solution)/shard_map/ppermute | solution.py:20
  56.9 0.0 collective-permute-done.7
  56.9 3.5 %collective-permute-start.8 = (bf16[272,512]{0,1:T(8,128)(2,1)S(1)}, bf16[272,512]{0,1:T(8,128)(2,1)S(1)}, u32[]{:S(2)}, u32[]{:S(2)}) collective-permute-start(bf16[272,512]{0,1:T(8,128)(2,1)S(1)} %maximum_maximum_fusion), channel_id=1, source_target_pairs={{0,2},{2,0},{4,6},{6,4},{8,10},{10,8},{12,14},{14,12},{16,18},{18,... | collective-permute-start | bytes 835592 | tf_op jit(solution)/shard_map/ppermute | solution.py:40
  60.4 1.9 %collective-permute-start.11 = (bf16[64,8192]{1,0:T(8,128)(2,1)S(1)}, bf16[64,8192]{1,0:T(8,128)(2,1)S(1)}, u32[]{:S(2)}, u32[]{:S(2)}) collective-permute-start(bf16[64,8192]{1,0:T(8,128)(2,1)S(1)} %bitcast.30), channel_id=1, source_target_pairs={{0,449},{64,0},{128,64},{192,128},{256,192},{320,256},{384,320},{4... | collective-permute-start | bytes 3145736 | tf_op jit(solution)/shard_map/ppermute | solution.py:20
  62.4 0.1 select_reduce_fusion.1
  62.5 0.1 broadcast_select_fusion.1
  62.6 0.0 copy-start.7
  62.6 7.4 %all-to-all-done = bf16[16,64,512]{2,1,0:T(8,128)(2,1)} async-done(((bf16[16,64,512]{2,1,0:T(8,128)(2,1)}), bf16[16,64,512]{2,1,0:T(8,128)(2,1)}, u32[]{:S(2)}, u32[]{:S(2)}) %all-to-all-start) | async-done | bytes 1048608 | tf_op jit(solution)/shard_map/all_to_all | solution.py:29
  70.0 2.9 %multiply_convert_fusion = bf16[1024,512]{1,0:T(8,128)(2,1)} fusion(bf16[1024,512]{1,0:T(8,128)(2,1)} %bitcast.4, f32[512]{0:T(512)S(1)} %maximum_convert_fusion, bf16[256,512]{0,1:T(8,128)(2,1)S(1)} %get-tuple-element.28, bf16[256,512]{0,1:T(8,128)(2,1)S(1)} %get-tuple-element.27), kind=kOutput, calls=%fused_computation | convolution fusion | flops 538968064 | bytes 2623488 | tf_op jit(solution)/shard_map/tk,ck->tc/dot_general | solution.py:189
  72.9 4.4 %all-to-all-start.3 = ((bf16[16,64,512]{2,1,0:T(8,128)(2,1)}), bf16[16,64,512]{2,1,0:T(8,128)(2,1)S(1)}, u32[]{:S(2)}, u32[]{:S(2)}) async-start(bf16[16,64,512]{2,1,0:T(8,128)(2,1)} %bitcast.31), calls=%async_computation.3 | async-start | bytes 2097152 | tf_op jit(solution)/shard_map/all_to_all | solution.py:29
  77.3 3.3 %collective-permute-done.2 = bf16[1024,512]{1,0:T(8,128)(2,1)} collective-permute-done((bf16[1024,512]{1,0:T(8,128)(2,1)}, bf16[1024,512]{1,0:T(8,128)(2,1)}, u32[]{:S(2)}, u32[]{:S(2)}) %collective-permute-start.2) | collective-permute-done | bytes 1048608 | tf_op jit(solution)/shard_map/ppermute | solution.py:20
  80.7 2.3 %fusion = (f32[512]{0:T(512)S(1)}, f32[512,512]{1,0:T(8,128)S(1)}) fusion(bf16[256,512]{0,1:T(8,128)(2,1)} %copy-done.7, bf16[256,512]{0,1:T(8,128)(2,1)S(1)} %copy-done.6, bf16[1024,512]{1,0:T(8,128)(2,1)} %bitcast.4, bf16[1024,512]{1,0:T(8,128)(2,1)} %collective-permute-done.2), kind=kOutput, calls=%fused_computation.2 | convolution fusion | flops 538443264 | bytes 3672064 | tf_op jit(solution)/shard_map/tc,tk->ck/dot_general | solution.py:181
  83.0 0.0 copy-start.4
  83.0 1.0 copy-done.4
  84.0 4.8 %collective-permute-start.3 = (bf16[256,512]{0,1:T(8,128)(2,1)S(1)}, bf16[256,512]{0,1:T(8,128)(2,1)}, u32[]{:S(2)}, u32[]{:S(2)}) collective-permute-start(bf16[256,512]{0,1:T(8,128)(2,1)S(1)} %fusion.2), channel_id=1, source_target_pairs={{0,2},{2,0},{4,6},{6,4},{8,10},{10,8},{12,14},{14,12},{16,18},{18,... | collective-permute-start | bytes 786440 | tf_op jit(solution)/shard_map/ppermute | solution.py:40
  88.8 1.3 collective-permute-done.3
  90.1 1.2 fusion.1
  91.2 0.7 fusion.4
  91.9 4.1 %collective-permute-start.5 = (bf16[256,256]{0,1:T(8,128)(2,1)}, bf16[256,256]{0,1:T(8,128)(2,1)S(1)}, u32[]{:S(2)}, u32[]{:S(2)}) collective-permute-start(bf16[256,256]{0,1:T(8,128)(2,1)} %get-tuple-element.30), channel_id=1, source_target_pairs={{0,65},{64,129},{128,193},{192,257},{256,321},{320,385},{384,449},... | collective-permute-start | bytes 393224 | tf_op jit(solution)/shard_map/ppermute | solution.py:20
  96.0 1.9 %collective-permute-start.4 = (bf16[256,256]{0,1:T(8,128)(2,1)S(1)}, bf16[256,256]{0,1:T(8,128)(2,1)}, u32[]{:S(2)}, u32[]{:S(2)}) collective-permute-start(bf16[256,256]{0,1:T(8,128)(2,1)S(1)} %get-tuple-element.29), channel_id=1, source_target_pairs={{0,64},{64,128},{128,192},{192,256},{256,320},{320,384},{384,448},... | collective-permute-start | bytes 393224 | tf_op jit(solution)/shard_map/ppermute | solution.py:20
  98.0 2.3 %collective-permute-start.9 = (f32[512]{0:T(512)S(1)}, f32[512]{0:T(512)S(1)}, u32[]{:S(2)}, u32[]{:S(2)}) collective-permute-start(f32[512]{0:T(512)S(1)} %get-tuple-element.31), channel_id=1, source_target_pairs={{0,64},{64,128},{128,192},{192,256},{256,320},{320,384},{384,448},... | collective-permute-start | bytes 6152 | tf_op jit(solution)/shard_map/ppermute | solution.py:20
  100.3 9.7 %collective-permute-start.10 = (f32[512]{0:T(512)S(1)}, f32[512]{0:T(512)S(1)}, u32[]{:S(2)}, u32[]{:S(2)}) collective-permute-start(f32[512]{0:T(512)S(1)} %get-tuple-element.31), channel_id=1, source_target_pairs={{0,65},{64,129},{128,193},{192,257},{256,321},{320,385},{384,449},... | collective-permute-start | bytes 6152 | tf_op jit(solution)/shard_map/ppermute | solution.py:20
  110.0 20.1 %collective-permute-done.10 = f32[512]{0:T(512)S(1)} collective-permute-done((f32[512]{0:T(512)S(1)}, f32[512]{0:T(512)S(1)}, u32[]{:S(2)}, u32[]{:S(2)}) %collective-permute-start.10) | collective-permute-done | bytes 2080 | tf_op jit(solution)/shard_map/ppermute | solution.py:20
  130.1 0.7 broadcast_in_dim.37
  130.8 9.3 %all-to-all-start.2 = ((f32[32,1,512]{2,1,0:T(1,128)}), f32[32,1,512]{2,1,0:T(1,128)S(1)}, u32[]{:S(2)}, u32[]{:S(2)}) async-start(f32[32,1,512]{2,1,0:T(1,128)} %broadcast_in_dim.37), calls=%async_computation.2 | async-start | bytes 131072 | tf_op jit(solution)/shard_map/all_to_all | solution.py:199
  140.2 1.0 copy-done.3
  141.1 3.7 %shard_map.96 = bf16[64,8192]{1,0:T(8,128)(2,1)} custom-call(s32[1]{0:T(128)} %bitcast.12.last_ref, bf16[16,64,512]{2,1,0:T(8,128)(2,1)} %copy-done.1, bf16[64,8192]{1,0:T(8,128)(2,1)} %copy-done.3), custom_call_target="tpu_custom_call" | custom-call | tf_op jit(solution)/shard_map/pallas_call | solution.py:136
  144.8 2.7 %all-to-all-done.2 = f32[32,1,512]{2,1,0:T(1,128)S(1)} async-done(((f32[32,1,512]{2,1,0:T(1,128)}), f32[32,1,512]{2,1,0:T(1,128)S(1)}, u32[]{:S(2)}, u32[]{:S(2)}) %all-to-all-start.2) | async-done | bytes 65568 | tf_op jit(solution)/shard_map/all_to_all | solution.py:199
  147.5 0.2 reduce.1
  147.7 0.1 reduce_sum.19
  147.8 0.6 copy.29
  148.4 0.9 multiply_bitcast_fusion
  149.4 0.8 copy.26
  (31 shorter events, 0.2 us)
Async XLA Ops:
  0.6 28.8 %copy-start = (bf16[1,8192]{1,0:T(2,128)(2,1)S(1)}, bf16[1,8192]{1,0:T(2,128)(2,1)}, u32[]{:S(2)}) copy-start(bf16[1,8192]{1,0:T(2,128)(2,1)} %param.8) | copy-start | bytes 49156
  3.3 6.9 %copy-start.8 = (bf16[1,256,256]{2,1,0:T(8,128)(2,1)S(1)}, bf16[1,256,256]{2,1,0:T(8,128)(2,1)}, u32[]{:S(2)}) copy-start(bf16[1,256,256]{2,1,0:T(8,128)(2,1)} %param.9) | copy-start | bytes 393220
  3.3 43.3 %all-to-all-start.1 = ((bf16[16,64,512]{2,1,0:T(8,128)(2,1)}), bf16[16,64,512]{2,1,0:T(8,128)(2,1)}, u32[]{:S(2)}, u32[]{:S(2)}) async-start(bf16[16,64,512]{2,1,0:T(8,128)(2,1)} %shard_map.95), calls=%async_computation.1 | async-start | bytes 2097152 | tf_op jit(solution)/shard_map/all_to_all | solution.py:29
  10.4 46.5 %collective-permute-start.7 = (bf16[256,256]{0,1:T(8,128)(2,1)S(1)}, bf16[256,256]{0,1:T(8,128)(2,1)S(1)}, u32[]{:S(2)}, u32[]{:S(2)}) collective-permute-start(bf16[256,256]{0,1:T(8,128)(2,1)S(1)} %bitcast.35), channel_id=1, source_target_pairs={{0,448},{64,1},{128,65},{192,129},{256,193},{320,257},{384,321},{4... | collective-permute-start | bytes 393224 | tf_op jit(solution)/shard_map/ppermute | solution.py:20
  23.7 22.9 %collective-permute-start.1 = (bf16[64,256]{1,0:T(8,128)(2,1)}, bf16[64,256]{1,0:T(8,128)(2,1)S(1)}, u32[]{:S(2)}, u32[]{:S(2)}) collective-permute-start(bf16[64,256]{1,0:T(8,128)(2,1)} %get-tuple-element.6), channel_id=1, source_target_pairs={{0,448},{64,1},{128,65},{192,129},{256,193},{320,257},{384,321},{4... | collective-permute-start | bytes 98312 | tf_op jit(solution)/shard_map/ppermute | solution.py:20
  25.6 21.0 %collective-permute-start = (bf16[64,256]{1,0:T(8,128)(2,1)}, bf16[64,256]{1,0:T(8,128)(2,1)S(1)}, u32[]{:S(2)}, u32[]{:S(2)}) collective-permute-start(bf16[64,256]{1,0:T(8,128)(2,1)} %get-tuple-element.5), channel_id=1, source_target_pairs={{0,449},{64,0},{128,64},{192,128},{256,192},{320,256},{384,320},{4... | collective-permute-start | bytes 98312 | tf_op jit(solution)/shard_map/ppermute | solution.py:20
  29.6 24.7 %collective-permute-start.6 = (bf16[272,256]{0,1:T(8,128)(2,1)S(1)}, bf16[272,256]{0,1:T(8,128)(2,1)S(1)}, u32[]{:S(2)}, u32[]{:S(2)}) collective-permute-start(bf16[272,256]{0,1:T(8,128)(2,1)S(1)} %pad_maximum_fusion.3), channel_id=1, source_target_pairs={{0,449},{64,0},{128,64},{192,128},{256,192},{320,256},{384,320},{4... | collective-permute-start | bytes 417800 | tf_op jit(solution)/shard_map/ppermute | solution.py:20
  47.7 22.4 %all-to-all-start = ((bf16[16,64,512]{2,1,0:T(8,128)(2,1)}), bf16[16,64,512]{2,1,0:T(8,128)(2,1)}, u32[]{:S(2)}, u32[]{:S(2)}) async-start(bf16[16,64,512]{2,1,0:T(8,128)(2,1)} %broadcast_in_dim.34), calls=%async_computation | async-start | bytes 2097152 | tf_op jit(solution)/shard_map/all_to_all | solution.py:29
  54.3 6.1 %copy-start.2 = (bf16[1,64,8192]{2,1,0:T(8,128)(2,1)S(1)}, bf16[1,64,8192]{2,1,0:T(8,128)(2,1)}, u32[]{:S(2)}) copy-start(bf16[1,64,8192]{2,1,0:T(8,128)(2,1)} %param.7) | copy-start | bytes 3145732
  54.4 26.3 %collective-permute-start.2 = (bf16[1024,512]{1,0:T(8,128)(2,1)}, bf16[1024,512]{1,0:T(8,128)(2,1)}, u32[]{:S(2)}, u32[]{:S(2)}) collective-permute-start(bf16[1024,512]{1,0:T(8,128)(2,1)} %bitcast.6), channel_id=1, source_target_pairs={{0,449},{64,0},{128,64},{192,128},{256,192},{320,256},{384,320},{4... | collective-permute-start | bytes 3145736 | tf_op jit(solution)/shard_map/ppermute | solution.py:20
  56.9 5.4 %collective-permute-start.8 = (bf16[272,512]{0,1:T(8,128)(2,1)S(1)}, bf16[272,512]{0,1:T(8,128)(2,1)S(1)}, u32[]{:S(2)}, u32[]{:S(2)}) collective-permute-start(bf16[272,512]{0,1:T(8,128)(2,1)S(1)} %maximum_maximum_fusion), channel_id=1, source_target_pairs={{0,2},{2,0},{4,6},{6,4},{8,10},{10,8},{12,14},{14,12},{16,18},{18,... | collective-permute-start | bytes 835592 | tf_op jit(solution)/shard_map/ppermute | solution.py:40
  60.4 79.7 %collective-permute-start.11 = (bf16[64,8192]{1,0:T(8,128)(2,1)S(1)}, bf16[64,8192]{1,0:T(8,128)(2,1)S(1)}, u32[]{:S(2)}, u32[]{:S(2)}) collective-permute-start(bf16[64,8192]{1,0:T(8,128)(2,1)S(1)} %bitcast.30), channel_id=1, source_target_pairs={{0,449},{64,0},{128,64},{192,128},{256,192},{320,256},{384,320},{4... | collective-permute-start | bytes 3145736 | tf_op jit(solution)/shard_map/ppermute | solution.py:20
  62.6 10.3 %copy-start.5 = (bf16[256,512]{0,1:T(8,128)(2,1)}, bf16[256,512]{0,1:T(8,128)(2,1)S(1)}, u32[]{:S(2)}) copy-start(bf16[256,512]{0,1:T(8,128)(2,1)S(1)} %get-tuple-element.27) | copy-start | bytes 786436
  62.6 10.3 %copy-start.7 = (bf16[256,512]{0,1:T(8,128)(2,1)}, bf16[256,512]{0,1:T(8,128)(2,1)S(1)}, u32[]{:S(2)}) copy-start(bf16[256,512]{0,1:T(8,128)(2,1)S(1)} %get-tuple-element.28) | copy-start | bytes 786436
  72.9 7.7 %copy-start.6 = (bf16[256,512]{0,1:T(8,128)(2,1)S(1)}, bf16[256,512]{0,1:T(8,128)(2,1)}, u32[]{:S(2)}) copy-start(bf16[256,512]{0,1:T(8,128)(2,1)} %copy-done.5) | copy-start | bytes 786436
  72.9 57.2 %all-to-all-start.3 = ((bf16[16,64,512]{2,1,0:T(8,128)(2,1)}), bf16[16,64,512]{2,1,0:T(8,128)(2,1)S(1)}, u32[]{:S(2)}, u32[]{:S(2)}) async-start(bf16[16,64,512]{2,1,0:T(8,128)(2,1)} %bitcast.31), calls=%async_computation.3 | async-start | bytes 2097152 | tf_op jit(solution)/shard_map/all_to_all | solution.py:29
  83.0 1.0 copy-start.4
  84.0 6.1 %collective-permute-start.3 = (bf16[256,512]{0,1:T(8,128)(2,1)S(1)}, bf16[256,512]{0,1:T(8,128)(2,1)}, u32[]{:S(2)}, u32[]{:S(2)}) collective-permute-start(bf16[256,512]{0,1:T(8,128)(2,1)S(1)} %fusion.2), channel_id=1, source_target_pairs={{0,2},{2,0},{4,6},{6,4},{8,10},{10,8},{12,14},{14,12},{16,18},{18,... | collective-permute-start | bytes 786440 | tf_op jit(solution)/shard_map/ppermute | solution.py:40
  91.9 56.5 %collective-permute-start.5 = (bf16[256,256]{0,1:T(8,128)(2,1)}, bf16[256,256]{0,1:T(8,128)(2,1)S(1)}, u32[]{:S(2)}, u32[]{:S(2)}) collective-permute-start(bf16[256,256]{0,1:T(8,128)(2,1)} %get-tuple-element.30), channel_id=1, source_target_pairs={{0,65},{64,129},{128,193},{192,257},{256,321},{320,385},{384,449},... | collective-permute-start | bytes 393224 | tf_op jit(solution)/shard_map/ppermute | solution.py:20
  96.0 52.4 %collective-permute-start.4 = (bf16[256,256]{0,1:T(8,128)(2,1)S(1)}, bf16[256,256]{0,1:T(8,128)(2,1)}, u32[]{:S(2)}, u32[]{:S(2)}) collective-permute-start(bf16[256,256]{0,1:T(8,128)(2,1)S(1)} %get-tuple-element.29), channel_id=1, source_target_pairs={{0,64},{64,128},{128,192},{192,256},{256,320},{320,384},{384,448},... | collective-permute-start | bytes 393224 | tf_op jit(solution)/shard_map/ppermute | solution.py:20
  98.0 12.1 %collective-permute-start.9 = (f32[512]{0:T(512)S(1)}, f32[512]{0:T(512)S(1)}, u32[]{:S(2)}, u32[]{:S(2)}) collective-permute-start(f32[512]{0:T(512)S(1)} %get-tuple-element.31), channel_id=1, source_target_pairs={{0,64},{64,128},{128,192},{192,256},{256,320},{320,384},{384,448},... | collective-permute-start | bytes 6152 | tf_op jit(solution)/shard_map/ppermute | solution.py:20
  100.3 29.8 %collective-permute-start.10 = (f32[512]{0:T(512)S(1)}, f32[512]{0:T(512)S(1)}, u32[]{:S(2)}, u32[]{:S(2)}) collective-permute-start(f32[512]{0:T(512)S(1)} %get-tuple-element.31), channel_id=1, source_target_pairs={{0,65},{64,129},{128,193},{192,257},{256,321},{320,385},{384,449},... | collective-permute-start | bytes 6152 | tf_op jit(solution)/shard_map/ppermute | solution.py:20
  130.1 10.0 %copy-start.1 = (bf16[16,64,512]{2,1,0:T(8,128)(2,1)}, bf16[16,64,512]{2,1,0:T(8,128)(2,1)S(1)}, u32[]{:S(2)}) copy-start(bf16[16,64,512]{2,1,0:T(8,128)(2,1)S(1)} %all-to-all-done.3.grad_ref) | copy-start | bytes 3145732
  130.8 16.6 %all-to-all-start.2 = ((f32[32,1,512]{2,1,0:T(1,128)}), f32[32,1,512]{2,1,0:T(1,128)S(1)}, u32[]{:S(2)}, u32[]{:S(2)}) async-start(f32[32,1,512]{2,1,0:T(1,128)} %broadcast_in_dim.37), calls=%async_computation.2 | async-start | bytes 131072 | tf_op jit(solution)/shard_map/all_to_all | solution.py:199
  140.1 1.0 copy-start.3

commit v5 on v4

--- a/solution.py
+++ b/solution.py
@@ -12,12 +12,14 @@
 QPK = 8
 
 
-def along(value, steps):
-    half = lax.axis_size("section")
-    count = 2 * half
-    place = [(plane % half) * 2 + plane // half for plane in range(count)]
-    pairs = [(place[plane], place[(plane + steps) % count]) for plane in range(count)]
-    return lax.ppermute(value, ("section", "tensor"), pairs)
+def shifted(value, axis, steps):
+    count = lax.axis_size(axis)
+    first, last = (max(0, -steps), min(count, count - steps))
+    return lax.ppermute(value, axis, [(source, source + steps) for source in range(first, last)])
+
+
+def swapped(value):
+    return lax.ppermute(value, "tensor", [(0, 1), (1, 0)])
 
 
 def same_core():
@@ -114,7 +116,7 @@
     )(half[None], query_rows, key_rows, grad_rows, position_rows)
 
 
-def finish_kernel(last_ref, grad_ref, hidden_ref, result_ref):
+def finish_kernel(grad_ref, hidden_ref, result_ref):
     rows = hidden_ref[...].astype(jnp.float32)
     root_mean = jnp.sqrt(jnp.mean(rows * rows, axis=1, keepdims=True) + 1e-05)
     count, _, columns = grad_ref.shape
@@ -127,57 +129,43 @@
         part = pl.ds(place * columns, columns)
         normed = rows[:, place * columns : (place + 1) * columns] / root_mean
         grad_hidden = (grad_ref[place].astype(jnp.float32) - normed * inner_mean) / root_mean
-        result_ref[:, part] = jnp.where(last_ref[0] != 0, jnp.float32(0.0), grad_hidden).astype(
-            jnp.bfloat16
-        )
-
-
-def finished(last, grad_blocks, rows):
+        result_ref[:, part] = grad_hidden.astype(jnp.bfloat16)
+
+
+def finished(grad_blocks, rows):
     return pl.pallas_call(
         finish_kernel,
         out_shape=jax.ShapeDtypeStruct(rows.shape, jnp.bfloat16),
-        in_specs=[whole(pltpu.SMEM), whole(), whole()],
+        in_specs=[whole(), whole()],
         out_specs=whole(),
-    )(last.astype(jnp.int32)[None], grad_blocks, rows)
+    )(grad_blocks, rows)
 
 
 def layer(hidden_in, norm_gain, value_weight, query_vectors, key_vectors, grad_attn, positions):
     n_dp = lax.axis_size("dp")
     n_chip = n_dp // 2
-    n_section = lax.axis_size("section")
     here = lax.axis_index("dp")
+    chip = here // 2
     core = here % 2
     half = lax.axis_index("tensor")
     own_rows, width = hidden_in.shape[1:]
     chunk = width // n_dp
     local_weight = value_weight[0]
     own_columns = local_weight.shape[1]
-    across = n_section - 1
+    normed = normed_blocks(hidden_in[0], n_chip)
+    normed_columns = exchanged(normed, 0, 0).reshape(n_chip * own_rows, 2 * chunk)
+    kept, given = attend(half, query_vectors[0], key_vectors[0], grad_attn[0], positions)
+    own_value = jnp.concatenate([kept, swapped(given)], axis=1)
+    device_weight = jnp.concatenate([local_weight, swapped(local_weight)], axis=1)
+    full_weight = by_core(core, device_weight, other_core(device_weight))
+    chip_gain = lax.dynamic_slice_in_dim(norm_gain[0], chip * 2 * chunk, 2 * chunk, 0)
     own_gain = lax.dynamic_slice_in_dim(norm_gain[0], here * chunk, chunk, 0)
-    gained_weight = jnp.concatenate(
-        [local_weight, jnp.broadcast_to(own_gain.reshape(1, -1), (16, own_columns))], axis=0
-    )
-    work_weight = along(gained_weight, -1)
-    other_weight = along(local_weight, across)
-    normed = normed_blocks(hidden_in[0], n_chip)
-    home_columns = exchanged(normed, 0, 0).reshape(n_chip * own_rows, 2 * chunk)
-    work_hidden = along(hidden_in[0], -1)
-    kept, given = attend(half, query_vectors[0], key_vectors[0], grad_attn[0], positions)
-    work_value = jnp.concatenate([along(kept, -1), along(given, across)], axis=1)
-    normed_columns = along(home_columns, -1)
-    device_weight = jnp.concatenate(
-        [
-            jnp.concatenate([work_weight[:chunk], other_weight], axis=1),
-            jnp.concatenate([work_weight[chunk:], work_weight[chunk:]], axis=1),
-        ],
-        axis=0,
-    )
-    swapped_weight = other_core(device_weight)
-    full_weight = by_core(core, device_weight[:chunk], swapped_weight[:chunk])
-    work_gain = by_core(
-        core, device_weight[chunk, :own_columns], swapped_weight[chunk, :own_columns]
-    ).astype(jnp.float32)
-    group_value = gathered(work_value).reshape(n_chip * own_rows, 2 * own_columns)
+    group_value = gathered(own_value).reshape(n_chip * own_rows, 2 * own_columns)
+    grad_columns = (
+        jnp.einsum("tk,ck->tc", group_value, full_weight, preferred_element_type=jnp.float32)
+        * chip_gain.astype(jnp.float32)
+    ).astype(jnp.bfloat16)
+    grad_blocks = exchanged(grad_columns.reshape(n_chip, own_rows, 2 * chunk), 0, 0)
     group_term = jnp.einsum(
         "tc,tk->ck", normed_columns, group_value, preferred_element_type=jnp.float32
     )
@@ -185,24 +173,16 @@
     kept_term = lax.dynamic_slice_in_dim(group_term, core * chunk, chunk, 0)
     given_term = lax.dynamic_slice_in_dim(group_term, (1 - core) * chunk, chunk, 0)
     plane_term = kept_term + other_core(given_term.astype(jnp.bfloat16)).astype(jnp.float32)
-    grad_columns = (
-        jnp.einsum("tk,ck->tc", group_value, full_weight, preferred_element_type=jnp.float32)
-        * work_gain
-    ).astype(jnp.bfloat16)
-    grad_blocks = exchanged(grad_columns.reshape(n_chip, own_rows, 2 * chunk), 0, 0)
-    sent_term = plane_term.astype(jnp.bfloat16)
-    home_term = along(sent_term[:, :own_columns], 1).astype(jnp.float32) + along(
-        sent_term[:, own_columns:], -across
-    ).astype(jnp.float32)
-    weight_grad = home_term * own_gain.astype(jnp.float32)[:, None]
-    home_sum = along(group_sum, 1) + along(group_sum, -across)
+    given_back = swapped(plane_term[:, own_columns:].astype(jnp.bfloat16))
+    weight_grad = (plane_term[:, :own_columns] + given_back.astype(jnp.float32)) * own_gain.astype(
+        jnp.float32
+    )[:, None]
     all_sums = lax.all_to_all(
-        jnp.broadcast_to(home_sum[None], (n_dp, 2 * chunk)), "dp", 0, 0
-    )
-    gain_grad = jnp.sum(all_sums.reshape(n_chip, 2, 2 * chunk), axis=1).reshape(width)
-    to_previous = finished(
-        lax.axis_index("section") == n_section - 1, grad_blocks, work_hidden
-    )
+        jnp.broadcast_to(group_sum[None], (2 * n_dp, 2 * chunk)), ("dp", "tensor"), 0, 0
+    )
+    gain_grad = jnp.sum(all_sums.reshape(n_chip, 4, 2 * chunk), axis=1).reshape(width)
+    grad_hidden = finished(grad_blocks, hidden_in[0])
+    to_previous = shifted(grad_hidden, "section", -1)
     return (weight_grad[None], gain_grad[None], to_previous[None])
 
 

time: 151 us -> 153 us (1.013)
  the two profiles are of different devices: /device:TPU:129 before, /device:TPU:39 now
where the time goes in v5:
time: 153 us; the launch traced here: 152 us
  starting transfers between devices  90.7 us (59%)
  waiting for transfers between devices  39.6 us (26%)
  Pallas kernels  9.41 us (6%)
  local copies, waits for them, and re-layouts  5.46 us (4%)
  matrix products  3.69 us (2%)
  other arithmetic  2.75 us (2%)
    ppermute x3, starting transfers between devices, swapped(): return lax.ppermute(value, 'tensor', [(0, 1), (1, 0)])  38.4 us
    ppermute x3, waiting for transfers between devices, swapped(): return lax.ppermute(value, 'tensor', [(0, 1), (1, 0)])  19.9 us
    all_to_all x3, starting transfers between devices, exchanged(): lax.all_to_all(value, 'dp', split, joined, axis_index_groups=same_core())  19.3 us
    all_to_all x3, waiting for transfers between devices, exchanged(): lax.all_to_all(value, 'dp', split, joined, axis_index_groups=same_core())  19.2 us
    ppermute x2, starting transfers between devices, other_core(): lax.ppermute(value, 'dp', [(source, source ^ 1) for source in range(count)])  15.6 us
    all_to_all x1, starting transfers between devices, layer(): lax.all_to_all(jnp.broadcast_to(group_sum[None], (2 * n_dp, 2 * chunk)),...  15.5 us
    pallas_call x1, Pallas kernels, finished(): pl.pallas_call(finish_kernel, out_shape=jax.ShapeDtypeStruct(rows.shape,...  3.62 us
    unnamed x10, local copies, waits for them, and re-layouts  3.57 us
  transfers between devices with their start and end apart: 10, of which 6 were waited for; matrix products, arithmetic and copies ran while one was open for 4% of the time, Pallas kernels for 4%

profile of v5, /device:TPU:39, one launch (start us, length us, event | category | flops | bytes accessed | tf_op | source)
XLA Modules:
  0.0 152.4 jit_solution(16450760061457029694)
XLA Ops:
  0.6 3.1 %shard_map.94 = (bf16[64,256]{1,0:T(8,128)(2,1)}, bf16[64,256]{1,0:T(8,128)(2,1)}) custom-call(s32[1]{0:T(128)} %bitcast.half_ref, bf16[128,2048]{1,0:T(8,128)(2,1)} %bitcast.38, bf16[128,256]{1,0:T(8,128)(2,1)} %bitcast.41, bf16[128,2048]{1,0:T(8,128)(2,1)} %bitcast.39, s32[1,128]{1,0:T(1,128)} %position_ref.1), custom_call_target="tpu_custom_call" | custom-call | tf_op jit(solution)/shard_map/pallas_call | solution.py:110
  3.8 14.5 %collective-permute-start = (bf16[64,256]{1,0:T(8,128)(2,1)}, bf16[64,256]{1,0:T(8,128)(2,1)S(1)}, u32[]{:S(2)}, u32[]{:S(2)}) collective-permute-start(bf16[64,256]{1,0:T(8,128)(2,1)} %get-tuple-element.6), channel_id=1, source_target_pairs={{0,1},{1,0},{2,3},{3,2},{4,5},{5,4},{6,7},{7,6},{8,9},{9,8},{10,11... | collective-permute-start | bytes 98312 | tf_op jit(solution)/shard_map/ppermute | solution.py:22
  18.3 1.5 collective-permute-done
  19.8 0.8 pad_maximum_fusion.3
  20.6 1.1 broadcast_in_dim.11
  21.6 0.0 copy-start.2
  21.6 7.0 %all-to-all-start = ((bf16[16,64,512]{2,1,0:T(8,128)(2,1)}), bf16[16,64,512]{2,1,0:T(8,128)(2,1)S(1)}, u32[]{:S(2)}, u32[]{:S(2)}) async-start(bf16[16,64,512]{2,1,0:T(8,128)(2,1)} %broadcast_in_dim.11), calls=%async_computation | async-start | bytes 2097152 | tf_op jit(solution)/shard_map/all_to_all | solution.py:31
  28.6 0.0 copy-done.2
  28.6 0.1 copy.17
  28.8 12.1 %collective-permute-start.3 = (bf16[256,256]{0,1:T(8,128)(2,1)S(1)}, bf16[256,256]{0,1:T(8,128)(2,1)S(1)}, u32[]{:S(2)}, u32[]{:S(2)}) collective-permute-start(bf16[256,256]{0,1:T(8,128)(2,1)S(1)} %bitcast.31), channel_id=1, source_target_pairs={{0,1},{1,0},{2,3},{3,2},{4,5},{5,4},{6,7},{7,6},{8,9},{9,8},{10,11... | collective-permute-start | bytes 393224 | tf_op jit(solution)/shard_map/ppermute | solution.py:22
  40.8 4.0 %collective-permute-done.3 = bf16[256,256]{0,1:T(8,128)(2,1)S(1)} collective-permute-done((bf16[256,256]{0,1:T(8,128)(2,1)S(1)}, bf16[256,256]{0,1:T(8,128)(2,1)S(1)}, u32[]{:S(2)}, u32[]{:S(2)}) %collective-permute-start.3) | collective-permute-done | bytes 131104 | tf_op jit(solution)/shard_map/ppermute | solution.py:22
  44.8 10.0 %collective-permute-start.4 = (bf16[256,512]{0,1:T(8,128)(2,1)S(1)}, bf16[256,512]{0,1:T(8,128)(2,1)S(1)}, u32[]{:S(2)}, u32[]{:S(2)}) collective-permute-start(bf16[256,512]{0,1:T(8,128)(2,1)S(1)} %pad_maximum_fusion.2), channel_id=1, source_target_pairs={{0,2},{2,0},{4,6},{6,4},{8,10},{10,8},{12,14},{14,12},{16,18},{18,... | collective-permute-start | bytes 786440 | tf_op jit(solution)/shard_map/ppermute | solution.py:42
  54.8 0.7 dynamic-slice_convert_fusion.1
  55.5 0.4 collective-permute-done.4
  55.9 0.1 broadcast_select_fusion.1
  56.0 0.0 copy-start.1
  56.1 0.0 all-to-all-done
  56.1 1.7 %multiply_convert_fusion = bf16[1024,512]{1,0:T(8,128)(2,1)} fusion(bf16[1024,512]{1,0:T(8,128)(2,1)S(1)} %bitcast.34, f32[512]{0:T(512)S(1)} %bitcast.44, bf16[256,512]{0,1:T(8,128)(2,1)S(1)} %get-tuple-element.20, bf16[256,512]{0,1:T(8,128)(2,1)S(1)} %get-tuple-element.19), kind=kOutput, calls=%fused_computation | convolution fusion | flops 538968064 | bytes 2623488 | tf_op jit(solution)/shard_map/tk,ck->tc/dot_general | solution.py:165
  57.7 0.0 copy-done.1
  57.7 6.7 %all-to-all-start.3 = ((bf16[16,64,512]{2,1,0:T(8,128)(2,1)}), bf16[16,64,512]{2,1,0:T(8,128)(2,1)S(1)}, u32[]{:S(2)}, u32[]{:S(2)}) async-start(bf16[16,64,512]{2,1,0:T(8,128)(2,1)} %bitcast.14), calls=%async_computation.3 | async-start | bytes 2097152 | tf_op jit(solution)/shard_map/all_to_all | solution.py:31
  64.4 2.7 %shard_map.95 = bf16[16,64,512]{2,1,0:T(8,128)(2,1)} custom-call(bf16[64,8192]{1,0:T(8,128)(2,1)} %bitcast.29), custom_call_target="tpu_custom_call" | custom-call | tf_op jit(solution)/shard_map/pallas_call | solution.py:66
  67.1 11.8 %all-to-all-done.3.grad_ref = bf16[16,64,512]{2,1,0:T(8,128)(2,1)S(1)} async-done(((bf16[16,64,512]{2,1,0:T(8,128)(2,1)}), bf16[16,64,512]{2,1,0:T(8,128)(2,1)S(1)}, u32[]{:S(2)}, u32[]{:S(2)}) %all-to-all-start.3) | async-done | bytes 1048608 | tf_op jit(solution)/shard_map/all_to_all | solution.py:31
  78.9 0.0 copy-start
  78.9 1.0 copy-done
  79.9 5.7 %all-to-all-start.1 = ((bf16[16,64,512]{2,1,0:T(8,128)(2,1)}), bf16[16,64,512]{2,1,0:T(8,128)(2,1)}, u32[]{:S(2)}, u32[]{:S(2)}) async-start(bf16[16,64,512]{2,1,0:T(8,128)(2,1)} %shard_map.95), calls=%async_computation.1 | async-start | bytes 2097152 | tf_op jit(solution)/shard_map/all_to_all | solution.py:31
  85.6 3.6 %shard_map.96 = bf16[64,8192]{1,0:T(8,128)(2,1)} custom-call(bf16[16,64,512]{2,1,0:T(8,128)(2,1)} %copy-done, bf16[64,8192]{1,0:T(8,128)(2,1)} %bitcast.30), custom_call_target="tpu_custom_call" | custom-call | tf_op jit(solution)/shard_map/pallas_call | solution.py:136
  89.2 1.9 %collective-permute-start.5 = (bf16[64,8192]{1,0:T(8,128)(2,1)}, bf16[64,8192]{1,0:T(8,128)(2,1)S(1)}, u32[]{:S(2)}, u32[]{:S(2)}) collective-permute-start(bf16[64,8192]{1,0:T(8,128)(2,1)} %shard_map.96), channel_id=1, source_target_pairs={{64,0},{128,64},{192,128},{256,192},{320,256},{384,320},{448,384},... | collective-permute-start | bytes 3145736 | tf_op jit(solution)/shard_map/ppermute | solution.py:18
  91.1 7.4 %all-to-all-done.1 = bf16[16,64,512]{2,1,0:T(8,128)(2,1)} async-done(((bf16[16,64,512]{2,1,0:T(8,128)(2,1)}), bf16[16,64,512]{2,1,0:T(8,128)(2,1)}, u32[]{:S(2)}, u32[]{:S(2)}) %all-to-all-start.1) | async-done | bytes 1048608 | tf_op jit(solution)/shard_map/all_to_all | solution.py:31
  98.5 2.0 %fusion = (f32[512]{0:T(512)S(1)}, f32[512,512,1]{1,0,2:T(8,128)S(1)}) fusion(bf16[256,512]{0,1:T(8,128)(2,1)} %copy-done.1, bf16[256,512]{0,1:T(8,128)(2,1)S(1)} %get-tuple-element.19, bf16[16,64,512]{2,1,0:T(8,128)(2,1)S(1)} %all-to-all-done, bf16[16,64,512]{2,1,0:T(8,128)(2,1)} %all-to-all-done.1), kind=kOutput, calls=%fused_computation.2 | convolution fusion | flops 538443264 | bytes 3672064 | tf_op jit(solution)/shard_map/tc,tk->ck/dot_general | solution.py:169
  100.6 5.6 %collective-permute-start.1 = (bf16[256,512]{0,1:T(8,128)(2,1)S(1)}, bf16[256,512]{0,1:T(8,128)(2,1)S(1)}, u32[]{:S(2)}, u32[]{:S(2)}) collective-permute-start(bf16[256,512]{0,1:T(8,128)(2,1)S(1)} %fusion.1), channel_id=1, source_target_pairs={{0,2},{2,0},{4,6},{6,4},{8,10},{10,8},{12,14},{14,12},{16,18},{18,... | collective-permute-start | bytes 786440 | tf_op jit(solution)/shard_map/ppermute | solution.py:42
  106.1 0.7 broadcast_in_dim.26
  106.9 15.5 %all-to-all-start.2 = ((f32[64,1,512]{2,1,0:T(1,128)}), f32[64,1,512]{2,1,0:T(1,128)S(1)}, u32[]{:S(2)}, u32[]{:S(2)}) async-start(f32[64,1,512]{2,1,0:T(1,128)} %broadcast_in_dim.26), calls=%async_computation.2 | async-start | bytes 262144 | tf_op jit(solution)/shard_map/all_to_all | solution.py:180
  122.4 0.0 collective-permute-done.1
  122.4 0.1 bitcast_add_fusion
  122.5 11.8 %collective-permute-start.2 = (bf16[256,256]{0,1:T(8,128)(2,1)S(1)}, bf16[256,256]{0,1:T(8,128)(2,1)S(1)}, u32[]{:S(2)}, u32[]{:S(2)}) collective-permute-start(bf16[256,256]{0,1:T(8,128)(2,1)S(1)} %slice.17), channel_id=1, source_target_pairs={{0,1},{1,0},{2,3},{3,2},{4,5},{5,4},{6,7},{7,6},{8,9},{9,8},{10,11... | collective-permute-start | bytes 393224 | tf_op jit(solution)/shard_map/ppermute | solution.py:22
  134.3 0.7 dynamic-slice_convert_fusion.2
  135.0 14.5 %collective-permute-done.2 = bf16[256,256]{0,1:T(8,128)(2,1)S(1)} collective-permute-done((bf16[256,256]{0,1:T(8,128)(2,1)S(1)}, bf16[256,256]{0,1:T(8,128)(2,1)S(1)}, u32[]{:S(2)}, u32[]{:S(2)}) %collective-permute-start.2) | collective-permute-done | bytes 131104 | tf_op jit(solution)/shard_map/ppermute | solution.py:22
  149.5 0.8 copy.19
  150.4 0.0 all-to-all-done.2
  150.4 0.3 reduce
  150.7 0.1 reduce_sum.19
  150.8 0.6 copy.22
  151.5 0.0 collective-permute-done.5
  151.5 1.0 copy.24
  (5 shorter events, 0.1 us)
Async XLA Ops:
  3.8 16.0 %collective-permute-start = (bf16[64,256]{1,0:T(8,128)(2,1)}, bf16[64,256]{1,0:T(8,128)(2,1)S(1)}, u32[]{:S(2)}, u32[]{:S(2)}) collective-permute-start(bf16[64,256]{1,0:T(8,128)(2,1)} %get-tuple-element.6), channel_id=1, source_target_pairs={{0,1},{1,0},{2,3},{3,2},{4,5},{5,4},{6,7},{7,6},{8,9},{9,8},{10,11... | collective-permute-start | bytes 98312 | tf_op jit(solution)/shard_map/ppermute | solution.py:22
  21.6 7.0 %copy-start.2 = (bf16[1,256,256]{2,1,0:T(8,128)(2,1)S(1)}, bf16[1,256,256]{2,1,0:T(8,128)(2,1)}, u32[]{:S(2)}) copy-start(bf16[1,256,256]{2,1,0:T(8,128)(2,1)} %param.9) | copy-start | bytes 393220
  21.6 34.4 %all-to-all-start = ((bf16[16,64,512]{2,1,0:T(8,128)(2,1)}), bf16[16,64,512]{2,1,0:T(8,128)(2,1)S(1)}, u32[]{:S(2)}, u32[]{:S(2)}) async-start(bf16[16,64,512]{2,1,0:T(8,128)(2,1)} %broadcast_in_dim.11), calls=%async_computation | async-start | bytes 2097152 | tf_op jit(solution)/shard_map/all_to_all | solution.py:31
  28.8 16.0 %collective-permute-start.3 = (bf16[256,256]{0,1:T(8,128)(2,1)S(1)}, bf16[256,256]{0,1:T(8,128)(2,1)S(1)}, u32[]{:S(2)}, u32[]{:S(2)}) collective-permute-start(bf16[256,256]{0,1:T(8,128)(2,1)S(1)} %bitcast.31), channel_id=1, source_target_pairs={{0,1},{1,0},{2,3},{3,2},{4,5},{5,4},{6,7},{7,6},{8,9},{9,8},{10,11... | collective-permute-start | bytes 393224 | tf_op jit(solution)/shard_map/ppermute | solution.py:22
  44.8 11.1 %collective-permute-start.4 = (bf16[256,512]{0,1:T(8,128)(2,1)S(1)}, bf16[256,512]{0,1:T(8,128)(2,1)S(1)}, u32[]{:S(2)}, u32[]{:S(2)}) collective-permute-start(bf16[256,512]{0,1:T(8,128)(2,1)S(1)} %pad_maximum_fusion.2), channel_id=1, source_target_pairs={{0,2},{2,0},{4,6},{6,4},{8,10},{10,8},{12,14},{14,12},{16,18},{18,... | collective-permute-start | bytes 786440 | tf_op jit(solution)/shard_map/ppermute | solution.py:42
  56.0 1.7 %copy-start.1 = (bf16[256,512]{0,1:T(8,128)(2,1)}, bf16[256,512]{0,1:T(8,128)(2,1)S(1)}, u32[]{:S(2)}) copy-start(bf16[256,512]{0,1:T(8,128)(2,1)S(1)} %get-tuple-element.20) | copy-start | bytes 786436
  57.7 21.2 %all-to-all-start.3 = ((bf16[16,64,512]{2,1,0:T(8,128)(2,1)}), bf16[16,64,512]{2,1,0:T(8,128)(2,1)S(1)}, u32[]{:S(2)}, u32[]{:S(2)}) async-start(bf16[16,64,512]{2,1,0:T(8,128)(2,1)} %bitcast.14), calls=%async_computation.3 | async-start | bytes 2097152 | tf_op jit(solution)/shard_map/all_to_all | solution.py:31
  78.9 1.0 copy-start
  79.9 18.6 %all-to-all-start.1 = ((bf16[16,64,512]{2,1,0:T(8,128)(2,1)}), bf16[16,64,512]{2,1,0:T(8,128)(2,1)}, u32[]{:S(2)}, u32[]{:S(2)}) async-start(bf16[16,64,512]{2,1,0:T(8,128)(2,1)} %shard_map.95), calls=%async_computation.1 | async-start | bytes 2097152 | tf_op jit(solution)/shard_map/all_to_all | solution.py:31
  89.2 62.3 %collective-permute-start.5 = (bf16[64,8192]{1,0:T(8,128)(2,1)}, bf16[64,8192]{1,0:T(8,128)(2,1)S(1)}, u32[]{:S(2)}, u32[]{:S(2)}) collective-permute-start(bf16[64,8192]{1,0:T(8,128)(2,1)} %shard_map.96), channel_id=1, source_target_pairs={{64,0},{128,64},{192,128},{256,192},{320,256},{384,320},{448,384},... | collective-permute-start | bytes 3145736 | tf_op jit(solution)/shard_map/ppermute | solution.py:18
  100.6 21.8 %collective-permute-start.1 = (bf16[256,512]{0,1:T(8,128)(2,1)S(1)}, bf16[256,512]{0,1:T(8,128)(2,1)S(1)}, u32[]{:S(2)}, u32[]{:S(2)}) collective-permute-start(bf16[256,512]{0,1:T(8,128)(2,1)S(1)} %fusion.1), channel_id=1, source_target_pairs={{0,2},{2,0},{4,6},{6,4},{8,10},{10,8},{12,14},{14,12},{16,18},{18,... | collective-permute-start | bytes 786440 | tf_op jit(solution)/shard_map/ppermute | solution.py:42
  106.9 43.5 %all-to-all-start.2 = ((f32[64,1,512]{2,1,0:T(1,128)}), f32[64,1,512]{2,1,0:T(1,128)S(1)}, u32[]{:S(2)}, u32[]{:S(2)}) async-start(f32[64,1,512]{2,1,0:T(1,128)} %broadcast_in_dim.26), calls=%async_computation.2 | async-start | bytes 262144 | tf_op jit(solution)/shard_map/all_to_all | solution.py:180
  122.5 27.0 %collective-permute-start.2 = (bf16[256,256]{0,1:T(8,128)(2,1)S(1)}, bf16[256,256]{0,1:T(8,128)(2,1)S(1)}, u32[]{:S(2)}, u32[]{:S(2)}) collective-permute-start(bf16[256,256]{0,1:T(8,128)(2,1)S(1)} %slice.17), channel_id=1, source_target_pairs={{0,1},{1,0},{2,3},{3,2},{4,5},{5,4},{6,7},{7,6},{8,9},{9,8},{10,11... | collective-permute-start | bytes 393224 | tf_op jit(solution)/shard_map/ppermute | solution.py:22

commit v6 on v5

--- a/solution.py
+++ b/solution.py
@@ -10,6 +10,7 @@
 
 HD = 128
 QPK = 8
+STEP = 16
 
 
 def shifted(value, axis, steps):
@@ -22,6 +23,14 @@
     return lax.ppermute(value, "tensor", [(0, 1), (1, 0)])
 
 
+def halfway(value):
+    half = lax.axis_size("section")
+    count = 2 * half
+    place = [(plane % half) * 2 + plane // half for plane in range(count)]
+    pairs = [(place[plane], place[(plane + half // 2) % count]) for plane in range(count)]
+    return lax.ppermute(value, ("section", "tensor"), pairs)
+
+
 def same_core():
     count = lax.axis_size("dp")
     return [list(range(core, count, 2)) for core in range(2)]
@@ -53,12 +62,18 @@
 
 
 def norm_kernel(hidden_ref, normed_ref):
-    rows = hidden_ref[...].astype(jnp.float32)
-    root_mean = jnp.sqrt(jnp.mean(rows * rows, axis=1, keepdims=True) + 1e-05)
-    normed = (rows / root_mean).astype(jnp.bfloat16)
-    count, _, columns = normed_ref.shape
-    for place in range(count):
-        normed_ref[place] = normed[:, place * columns : (place + 1) * columns]
+    count, length, columns = normed_ref.shape
+    for start in range(0, length, STEP):
+        rows = pl.ds(start, STEP)
+        squares = jnp.zeros((STEP, columns), jnp.float32)
+        for place in range(count):
+            block = hidden_ref[rows, pl.ds(place * columns, columns)].astype(jnp.float32)
+            squares += block * block
+        mean = jnp.sum(squares, axis=1, keepdims=True) / (count * columns)
+        inverse = 1.0 / jnp.sqrt(mean + 1e-05)
+        for place in range(count):
+            block = hidden_ref[rows, pl.ds(place * columns, columns)].astype(jnp.float32)
+            normed_ref[place, rows] = (block * inverse).astype(jnp.bfloat16)
 
 
 def normed_blocks(rows, count):
@@ -90,7 +105,7 @@
             masked = jnp.where(visible, scores, jnp.float32(-1e30))
             largest = jnp.max(masked, axis=0, keepdims=True)
             powers = jnp.where(visible, jnp.exp(masked - largest), jnp.float32(0.0))
-            weights = powers / jnp.sum(powers, axis=0, keepdims=True)
+            weights = powers * (1.0 / jnp.sum(powers, axis=0, keepdims=True))
             total += lax.dot_general(
                 weights.astype(jnp.bfloat16),
                 grad_ref[:, head * HD : (head + 1) * HD],
@@ -117,19 +132,23 @@
 
 
 def finish_kernel(grad_ref, hidden_ref, result_ref):
-    rows = hidden_ref[...].astype(jnp.float32)
-    root_mean = jnp.sqrt(jnp.mean(rows * rows, axis=1, keepdims=True) + 1e-05)
-    count, _, columns = grad_ref.shape
-    total = jnp.zeros_like(root_mean)
-    for place in range(count):
-        block = rows[:, place * columns : (place + 1) * columns] / root_mean
-        total += jnp.sum(grad_ref[place].astype(jnp.float32) * block, axis=1, keepdims=True)
-    inner_mean = total / rows.shape[1]
-    for place in range(count):
-        part = pl.ds(place * columns, columns)
-        normed = rows[:, place * columns : (place + 1) * columns] / root_mean
-        grad_hidden = (grad_ref[place].astype(jnp.float32) - normed * inner_mean) / root_mean
-        result_ref[:, part] = grad_hidden.astype(jnp.bfloat16)
+    count, length, columns = grad_ref.shape
+    for start in range(0, length, STEP):
+        rows = pl.ds(start, STEP)
+        squares = jnp.zeros((STEP, columns), jnp.float32)
+        total = jnp.zeros((STEP, columns), jnp.float32)
+        for place in range(count):
+            block = hidden_ref[rows, pl.ds(place * columns, columns)].astype(jnp.float32)
+            squares += block * block
+            total += grad_ref[place, rows].astype(jnp.float32) * block
+        mean = jnp.sum(squares, axis=1, keepdims=True) / (count * columns)
+        inverse = 1.0 / jnp.sqrt(mean + 1e-05)
+        inner = jnp.sum(total, axis=1, keepdims=True) * inverse / (count * columns) * inverse
+        for place in range(count):
+            part = pl.ds(place * columns, columns)
+            block = hidden_ref[rows, part].astype(jnp.float32)
+            grads = grad_ref[place, rows].astype(jnp.float32)
+            result_ref[rows, part] = ((grads - block * inner) * inverse).astype(jnp.bfloat16)
 
 
 def finished(grad_blocks, rows):
@@ -169,18 +188,18 @@
     group_term = jnp.einsum(
         "tc,tk->ck", normed_columns, group_value, preferred_element_type=jnp.float32
     )
-    group_sum = jnp.sum(group_term * full_weight.astype(jnp.float32), axis=1)
     kept_term = lax.dynamic_slice_in_dim(group_term, core * chunk, chunk, 0)
     given_term = lax.dynamic_slice_in_dim(group_term, (1 - core) * chunk, chunk, 0)
     plane_term = kept_term + other_core(given_term.astype(jnp.bfloat16)).astype(jnp.float32)
-    given_back = swapped(plane_term[:, own_columns:].astype(jnp.bfloat16))
+    half_way = halfway(plane_term[:, own_columns:].astype(jnp.bfloat16))
+    given_back = halfway(half_way)
+    plane_sum = jnp.sum(plane_term * device_weight.astype(jnp.float32), axis=1)
     weight_grad = (plane_term[:, :own_columns] + given_back.astype(jnp.float32)) * own_gain.astype(
         jnp.float32
     )[:, None]
-    all_sums = lax.all_to_all(
-        jnp.broadcast_to(group_sum[None], (2 * n_dp, 2 * chunk)), ("dp", "tensor"), 0, 0
-    )
-    gain_grad = jnp.sum(all_sums.reshape(n_chip, 4, 2 * chunk), axis=1).reshape(width)
+    home_sum = plane_sum + halfway(halfway(plane_sum))
+    all_sums = lax.all_to_all(jnp.broadcast_to(home_sum[None], (n_dp, chunk)), "dp", 0, 0)
+    gain_grad = all_sums.reshape(width)
     grad_hidden = finished(grad_blocks, hidden_in[0])
     to_previous = shifted(grad_hidden, "section", -1)
     return (weight_grad[None], gain_grad[None], to_previous[None])

time: 153 us -> 161 us (1.052)
  the two profiles are of different devices: /device:TPU:39 before, /device:TPU:1 now
where the time goes in v6:
time: 161 us; the launch traced here: 160 us
  starting transfers between devices  99 us (61%)
  waiting for transfers between devices  38.2 us (24%)
  Pallas kernels  8.86 us (6%)
  local copies, waits for them, and re-layouts  6.3 us (4%)
  other arithmetic  3.45 us (2%)
  matrix products  3.4 us (2%)
    ppermute x2, starting transfers between devices, swapped(): return lax.ppermute(value, 'tensor', [(0, 1), (1, 0)])  28.6 us
    ppermute x4, starting transfers between devices, halfway(): return lax.ppermute(value, ('section', 'tensor'), pairs)  28.4 us
    all_to_all x3, waiting for transfers between devices, exchanged(): lax.all_to_all(value, 'dp', split, joined, axis_index_groups=same_core())  20.5 us
    all_to_all x3, starting transfers between devices, exchanged(): lax.all_to_all(value, 'dp', split, joined, axis_index_groups=same_core())  18.3 us
    all_to_all x1, starting transfers between devices, layer(): lax.all_to_all(jnp.broadcast_to(home_sum[None], (n_dp, chunk)), 'dp', 0, 0)  12.7 us
    ppermute x2, starting transfers between devices, other_core(): lax.ppermute(value, 'dp', [(source, source ^ 1) for source in range(count)])  9.63 us
    ppermute x4, waiting for transfers between devices, halfway(): return lax.ppermute(value, ('section', 'tensor'), pairs)  8 us
    all_to_all x1, waiting for transfers between devices, layer(): lax.all_to_all(jnp.broadcast_to(home_sum[None], (n_dp, chunk)), 'dp', 0, 0)  6.59 us
  transfers between devices with their start and end apart: 13, of which 10 were waited for; matrix products, arithmetic and copies ran while one was open for 5% of the time, Pallas kernels for 2%

profile of v6, /device:TPU:1, one launch (start us, length us, event | category | flops | bytes accessed | tf_op | source)
XLA Modules:
  0.0 160.1 jit_solution(6288226083595957639)
XLA Ops:
  0.6 3.1 %shard_map.94 = (bf16[64,256]{1,0:T(8,128)(2,1)}, bf16[64,256]{1,0:T(8,128)(2,1)}) custom-call(s32[1]{0:T(128)} %bitcast.half_ref, bf16[128,2048]{1,0:T(8,128)(2,1)} %bitcast.33, bf16[128,256]{1,0:T(8,128)(2,1)} %bitcast.36, bf16[128,2048]{1,0:T(8,128)(2,1)} %bitcast.34, s32[1,128]{1,0:T(1,128)} %position_ref.1), custom_call_target="tpu_custom_call" | custom-call | tf_op jit(solution)/shard_map/pallas_call | solution.py:125
  3.8 16.3 %collective-permute-start = (bf16[64,256]{1,0:T(8,128)(2,1)}, bf16[64,256]{1,0:T(8,128)(2,1)S(1)}, u32[]{:S(2)}, u32[]{:S(2)}) collective-permute-start(bf16[64,256]{1,0:T(8,128)(2,1)} %get-tuple-element.6), channel_id=1, source_target_pairs={{0,1},{1,0},{2,3},{3,2},{4,5},{5,4},{6,7},{7,6},{8,9},{9,8},{10,11... | collective-permute-start | bytes 98312 | tf_op jit(solution)/shard_map/ppermute | solution.py:23
  20.0 1.6 %collective-permute-done = bf16[64,256]{1,0:T(8,128)(2,1)S(1)} collective-permute-done((bf16[64,256]{1,0:T(8,128)(2,1)}, bf16[64,256]{1,0:T(8,128)(2,1)S(1)}, u32[]{:S(2)}, u32[]{:S(2)}) %collective-permute-start) | collective-permute-done | bytes 32800 | tf_op jit(solution)/shard_map/ppermute | solution.py:23
  21.6 0.8 pad_maximum_fusion.1
  22.4 1.1 broadcast_in_dim.11
  23.5 0.0 copy-start.1
  23.5 6.9 %all-to-all-start = ((bf16[16,64,512]{2,1,0:T(8,128)(2,1)}), bf16[16,64,512]{2,1,0:T(8,128)(2,1)S(1)}, u32[]{:S(2)}, u32[]{:S(2)}) async-start(bf16[16,64,512]{2,1,0:T(8,128)(2,1)} %broadcast_in_dim.11), calls=%async_computation | async-start | bytes 2097152 | tf_op jit(solution)/shard_map/all_to_all | solution.py:40
  30.4 0.0 copy-done.1
  30.4 0.1 copy.12
  30.5 12.4 %collective-permute-start.4 = (bf16[256,256]{0,1:T(8,128)(2,1)S(1)}, bf16[256,256]{0,1:T(8,128)(2,1)S(1)}, u32[]{:S(2)}, u32[]{:S(2)}) collective-permute-start(bf16[256,256]{0,1:T(8,128)(2,1)S(1)} %bitcast.26), channel_id=1, source_target_pairs={{0,1},{1,0},{2,3},{3,2},{4,5},{5,4},{6,7},{7,6},{8,9},{9,8},{10,11... | collective-permute-start | bytes 393224 | tf_op jit(solution)/shard_map/ppermute | solution.py:23
  42.9 2.5 %shard_map.95 = bf16[16,64,512]{2,1,0:T(8,128)(2,1)} custom-call(bf16[64,8192]{1,0:T(8,128)(2,1)} %bitcast.24), custom_call_target="tpu_custom_call" | custom-call | tf_op jit(solution)/shard_map/pallas_call | solution.py:81
  45.4 0.3 all-to-all-done
  45.7 6.4 %all-to-all-start.1 = ((bf16[16,64,512]{2,1,0:T(8,128)(2,1)}), bf16[16,64,512]{2,1,0:T(8,128)(2,1)S(1)}, u32[]{:S(2)}, u32[]{:S(2)}) async-start(bf16[16,64,512]{2,1,0:T(8,128)(2,1)} %shard_map.95), calls=%async_computation.1 | async-start | bytes 2097152 | tf_op jit(solution)/shard_map/all_to_all | solution.py:40
  52.0 0.0 collective-permute-done.4
  52.1 4.6 %collective-permute-start.7 = (bf16[256,512]{0,1:T(8,128)(2,1)S(1)}, bf16[256,512]{0,1:T(8,128)(2,1)S(1)}, u32[]{:S(2)}, u32[]{:S(2)}) collective-permute-start(bf16[256,512]{0,1:T(8,128)(2,1)S(1)} %pad_maximum_fusion), channel_id=1, source_target_pairs={{0,2},{2,0},{4,6},{6,4},{8,10},{10,8},{12,14},{14,12},{16,18},{18,... | collective-permute-start | bytes 786440 | tf_op jit(solution)/shard_map/ppermute | solution.py:51
  56.7 0.7 dynamic-slice_convert_fusion.1
  57.4 0.4 collective-permute-done.7
  57.8 0.1 broadcast_select_fusion.1
  57.9 1.7 %multiply_convert_fusion = bf16[1024,512]{1,0:T(8,128)(2,1)} fusion(bf16[1024,512]{1,0:T(8,128)(2,1)S(1)} %bitcast.30, f32[512]{0:T(512)S(1)} %bitcast.38, bf16[256,512]{0,1:T(8,128)(2,1)S(1)} %get-tuple-element.16, bf16[256,512]{0,1:T(8,128)(2,1)S(1)} %get-tuple-element.15), kind=kOutput, calls=%fused_computation | convolution fusion | flops 538968064 | bytes 2623488 | tf_op jit(solution)/shard_map/tk,ck->tc/dot_general | solution.py:184
  59.6 7.0 %all-to-all-done.1 = bf16[16,64,512]{2,1,0:T(8,128)(2,1)S(1)} async-done(((bf16[16,64,512]{2,1,0:T(8,128)(2,1)}), bf16[16,64,512]{2,1,0:T(8,128)(2,1)S(1)}, u32[]{:S(2)}, u32[]{:S(2)}) %all-to-all-start.1) | async-done | bytes 1048608 | tf_op jit(solution)/shard_map/all_to_all | solution.py:40
  66.6 5.0 %all-to-all-start.3 = ((bf16[16,64,512]{2,1,0:T(8,128)(2,1)}), bf16[16,64,512]{2,1,0:T(8,128)(2,1)S(1)}, u32[]{:S(2)}, u32[]{:S(2)}) async-start(bf16[16,64,512]{2,1,0:T(8,128)(2,1)} %bitcast.32), calls=%async_computation.3 | async-start | bytes 2097152 | tf_op jit(solution)/shard_map/all_to_all | solution.py:40
  71.6 1.7 %convolution_bitcast_fusion = f32[512,512]{1,0:T(8,128)} fusion(bf16[16,64,512]{2,1,0:T(8,128)(2,1)S(1)} %all-to-all-done, bf16[16,64,512]{2,1,0:T(8,128)(2,1)S(1)} %all-to-all-done.1), kind=kOutput, calls=%fused_computation.1 | convolution fusion | flops 536870912 | bytes 3145728 | tf_op jit(solution)/shard_map/tc,tk->ck/dot_general | solution.py:188
  73.3 13.2 %all-to-all-done.3.grad_ref = bf16[16,64,512]{2,1,0:T(8,128)(2,1)S(1)} async-done(((bf16[16,64,512]{2,1,0:T(8,128)(2,1)}), bf16[16,64,512]{2,1,0:T(8,128)(2,1)S(1)}, u32[]{:S(2)}, u32[]{:S(2)}) %all-to-all-start.3) | async-done | bytes 1048608 | tf_op jit(solution)/shard_map/all_to_all | solution.py:40
  86.6 0.0 copy-start
  86.6 1.0 copy-done
  87.6 3.2 %shard_map.96 = bf16[64,8192]{1,0:T(8,128)(2,1)} custom-call(bf16[16,64,512]{2,1,0:T(8,128)(2,1)} %copy-done, bf16[64,8192]{1,0:T(8,128)(2,1)} %bitcast.25), custom_call_target="tpu_custom_call" | custom-call | tf_op jit(solution)/shard_map/pallas_call | solution.py:155
  90.8 1.3 collective-permute-start.8
  92.1 1.1 fusion.3
  93.2 5.0 %collective-permute-start.1 = (bf16[256,512]{0,1:T(8,128)(2,1)S(1)}, bf16[256,512]{0,1:T(8,128)(2,1)S(1)}, u32[]{:S(2)}, u32[]{:S(2)}) collective-permute-start(bf16[256,512]{0,1:T(8,128)(2,1)S(1)} %fusion.3), channel_id=1, source_target_pairs={{0,2},{2,0},{4,6},{6,4},{8,10},{10,8},{12,14},{14,12},{16,18},{18,... | collective-permute-start | bytes 786440 | tf_op jit(solution)/shard_map/ppermute | solution.py:51
  98.2 1.1 collective-permute-done.1
  99.3 1.2 multiply_reduce_fusion
  100.5 6.6 %collective-permute-start.2 = (bf16[256,256]{0,1:T(8,128)(2,1)S(1)}, bf16[256,256]{0,1:T(8,128)(2,1)S(1)}, u32[]{:S(2)}, u32[]{:S(2)}) collective-permute-start(bf16[256,256]{0,1:T(8,128)(2,1)S(1)} %slice.17), channel_id=1, source_target_pairs={{0,256},{64,320},{128,384},{192,448},{256,1},{320,65},{384,129},{4... | collective-permute-start | bytes 393224 | tf_op jit(solution)/shard_map/ppermute | solution.py:31
  107.2 6.6 %collective-permute-done.2 = bf16[256,256]{0,1:T(8,128)(2,1)S(1)} collective-permute-done((bf16[256,256]{0,1:T(8,128)(2,1)S(1)}, bf16[256,256]{0,1:T(8,128)(2,1)S(1)}, u32[]{:S(2)}, u32[]{:S(2)}) %collective-permute-start.2) | collective-permute-done | bytes 131104 | tf_op jit(solution)/shard_map/ppermute | solution.py:31
  113.7 6.3 %collective-permute-start.3 = (bf16[256,256]{0,1:T(8,128)(2,1)S(1)}, bf16[256,256]{0,1:T(8,128)(2,1)S(1)}, u32[]{:S(2)}, u32[]{:S(2)}) collective-permute-start(bf16[256,256]{0,1:T(8,128)(2,1)S(1)} %collective-permute-done.2), channel_id=1, source_target_pairs={{0,256},{64,320},{128,384},{192,448},{256,1},{320,65},{384,129},{4... | collective-permute-start | bytes 393224 | tf_op jit(solution)/shard_map/ppermute | solution.py:31
  120.1 7.8 %collective-permute-start.5 = (f32[256]{0:T(256)S(1)}, f32[256]{0:T(256)S(1)}, u32[]{:S(2)}, u32[]{:S(2)}) collective-permute-start(f32[256]{0:T(256)S(1)} %get-tuple-element.13), channel_id=1, source_target_pairs={{0,256},{64,320},{128,384},{192,448},{256,1},{320,65},{384,129},{4... | collective-permute-start | bytes 3080 | tf_op jit(solution)/shard_map/ppermute | solution.py:31
  127.9 0.7 collective-permute-done.5
  128.6 7.6 %collective-permute-start.6 = (f32[256]{0:T(256)S(1)}, f32[256]{0:T(256)S(1)}, u32[]{:S(2)}, u32[]{:S(2)}) collective-permute-start(f32[256]{0:T(256)S(1)} %collective-permute-done.5), channel_id=1, source_target_pairs={{0,256},{64,320},{128,384},{192,448},{256,1},{320,65},{384,129},{4... | collective-permute-start | bytes 3080 | tf_op jit(solution)/shard_map/ppermute | solution.py:31
  136.3 0.7 collective-permute-done.6
  137.0 0.6 broadcast_in_dim.26
  137.6 12.7 %all-to-all-start.2 = ((f32[32,1,256]{2,1,0:T(1,128)}), f32[32,1,256]{2,1,0:T(1,128)S(1)}, u32[]{:S(2)}, u32[]{:S(2)}) async-start(f32[32,1,256]{2,1,0:T(1,128)} %broadcast_in_dim.26), calls=%async_computation.2 | async-start | bytes 65536 | tf_op jit(solution)/shard_map/all_to_all | solution.py:201
  150.3 0.7 dynamic-slice_convert_fusion.2
  151.0 6.6 %all-to-all-done.2 = f32[32,1,256]{2,1,0:T(1,128)S(1)} async-done(((f32[32,1,256]{2,1,0:T(1,128)}), f32[32,1,256]{2,1,0:T(1,128)S(1)}, u32[]{:S(2)}, u32[]{:S(2)}) %all-to-all-start.2) | async-done | bytes 32800 | tf_op jit(solution)/shard_map/all_to_all | solution.py:201
  157.6 0.0 collective-permute-done.3
  157.6 0.8 copy.13
  158.5 0.0 collective-permute-done.8
  158.5 0.6 copy.16
  159.1 1.0 copy.17
  (4 shorter events, 0.1 us)
Async XLA Ops:
  3.8 17.9 %collective-permute-start = (bf16[64,256]{1,0:T(8,128)(2,1)}, bf16[64,256]{1,0:T(8,128)(2,1)S(1)}, u32[]{:S(2)}, u32[]{:S(2)}) collective-permute-start(bf16[64,256]{1,0:T(8,128)(2,1)} %get-tuple-element.6), channel_id=1, source_target_pairs={{0,1},{1,0},{2,3},{3,2},{4,5},{5,4},{6,7},{7,6},{8,9},{9,8},{10,11... | collective-permute-start | bytes 98312 | tf_op jit(solution)/shard_map/ppermute | solution.py:23
  23.5 6.9 %copy-start.1 = (bf16[1,256,256]{2,1,0:T(8,128)(2,1)S(1)}, bf16[1,256,256]{2,1,0:T(8,128)(2,1)}, u32[]{:S(2)}) copy-start(bf16[1,256,256]{2,1,0:T(8,128)(2,1)} %param.9) | copy-start | bytes 393220
  23.5 22.2 %all-to-all-start = ((bf16[16,64,512]{2,1,0:T(8,128)(2,1)}), bf16[16,64,512]{2,1,0:T(8,128)(2,1)S(1)}, u32[]{:S(2)}, u32[]{:S(2)}) async-start(bf16[16,64,512]{2,1,0:T(8,128)(2,1)} %broadcast_in_dim.11), calls=%async_computation | async-start | bytes 2097152 | tf_op jit(solution)/shard_map/all_to_all | solution.py:40
  30.5 21.6 %collective-permute-start.4 = (bf16[256,256]{0,1:T(8,128)(2,1)S(1)}, bf16[256,256]{0,1:T(8,128)(2,1)S(1)}, u32[]{:S(2)}, u32[]{:S(2)}) collective-permute-start(bf16[256,256]{0,1:T(8,128)(2,1)S(1)} %bitcast.26), channel_id=1, source_target_pairs={{0,1},{1,0},{2,3},{3,2},{4,5},{5,4},{6,7},{7,6},{8,9},{9,8},{10,11... | collective-permute-start | bytes 393224 | tf_op jit(solution)/shard_map/ppermute | solution.py:23
  45.7 20.9 %all-to-all-start.1 = ((bf16[16,64,512]{2,1,0:T(8,128)(2,1)}), bf16[16,64,512]{2,1,0:T(8,128)(2,1)S(1)}, u32[]{:S(2)}, u32[]{:S(2)}) async-start(bf16[16,64,512]{2,1,0:T(8,128)(2,1)} %shard_map.95), calls=%async_computation.1 | async-start | bytes 2097152 | tf_op jit(solution)/shard_map/all_to_all | solution.py:40
  52.1 5.8 %collective-permute-start.7 = (bf16[256,512]{0,1:T(8,128)(2,1)S(1)}, bf16[256,512]{0,1:T(8,128)(2,1)S(1)}, u32[]{:S(2)}, u32[]{:S(2)}) collective-permute-start(bf16[256,512]{0,1:T(8,128)(2,1)S(1)} %pad_maximum_fusion), channel_id=1, source_target_pairs={{0,2},{2,0},{4,6},{6,4},{8,10},{10,8},{12,14},{14,12},{16,18},{18,... | collective-permute-start | bytes 786440 | tf_op jit(solution)/shard_map/ppermute | solution.py:51
  66.6 20.0 %all-to-all-start.3 = ((bf16[16,64,512]{2,1,0:T(8,128)(2,1)}), bf16[16,64,512]{2,1,0:T(8,128)(2,1)S(1)}, u32[]{:S(2)}, u32[]{:S(2)}) async-start(bf16[16,64,512]{2,1,0:T(8,128)(2,1)} %bitcast.32), calls=%async_computation.3 | async-start | bytes 2097152 | tf_op jit(solution)/shard_map/all_to_all | solution.py:40
  86.6 1.0 copy-start
  90.8 67.7 %collective-permute-start.8 = (bf16[64,8192]{1,0:T(8,128)(2,1)}, bf16[64,8192]{1,0:T(8,128)(2,1)S(1)}, u32[]{:S(2)}, u32[]{:S(2)}) collective-permute-start(bf16[64,8192]{1,0:T(8,128)(2,1)} %shard_map.96), channel_id=1, source_target_pairs={{64,0},{128,64},{192,128},{256,192},{320,256},{384,320},{448,384},... | collective-permute-start | bytes 3145736 | tf_op jit(solution)/shard_map/ppermute | solution.py:19
  93.2 6.2 %collective-permute-start.1 = (bf16[256,512]{0,1:T(8,128)(2,1)S(1)}, bf16[256,512]{0,1:T(8,128)(2,1)S(1)}, u32[]{:S(2)}, u32[]{:S(2)}) collective-permute-start(bf16[256,512]{0,1:T(8,128)(2,1)S(1)} %fusion.3), channel_id=1, source_target_pairs={{0,2},{2,0},{4,6},{6,4},{8,10},{10,8},{12,14},{14,12},{16,18},{18,... | collective-permute-start | bytes 786440 | tf_op jit(solution)/shard_map/ppermute | solution.py:51
  100.5 13.2 %collective-permute-start.2 = (bf16[256,256]{0,1:T(8,128)(2,1)S(1)}, bf16[256,256]{0,1:T(8,128)(2,1)S(1)}, u32[]{:S(2)}, u32[]{:S(2)}) collective-permute-start(bf16[256,256]{0,1:T(8,128)(2,1)S(1)} %slice.17), channel_id=1, source_target_pairs={{0,256},{64,320},{128,384},{192,448},{256,1},{320,65},{384,129},{4... | collective-permute-start | bytes 393224 | tf_op jit(solution)/shard_map/ppermute | solution.py:31
  113.7 43.9 %collective-permute-start.3 = (bf16[256,256]{0,1:T(8,128)(2,1)S(1)}, bf16[256,256]{0,1:T(8,128)(2,1)S(1)}, u32[]{:S(2)}, u32[]{:S(2)}) collective-permute-start(bf16[256,256]{0,1:T(8,128)(2,1)S(1)} %collective-permute-done.2), channel_id=1, source_target_pairs={{0,256},{64,320},{128,384},{192,448},{256,1},{320,65},{384,129},{4... | collective-permute-start | bytes 393224 | tf_op jit(solution)/shard_map/ppermute | solution.py:31
  120.1 8.6 %collective-permute-start.5 = (f32[256]{0:T(256)S(1)}, f32[256]{0:T(256)S(1)}, u32[]{:S(2)}, u32[]{:S(2)}) collective-permute-start(f32[256]{0:T(256)S(1)} %get-tuple-element.13), channel_id=1, source_target_pairs={{0,256},{64,320},{128,384},{192,448},{256,1},{320,65},{384,129},{4... | collective-permute-start | bytes 3080 | tf_op jit(solution)/shard_map/ppermute | solution.py:31
  128.6 8.3 %collective-permute-start.6 = (f32[256]{0:T(256)S(1)}, f32[256]{0:T(256)S(1)}, u32[]{:S(2)}, u32[]{:S(2)}) collective-permute-start(f32[256]{0:T(256)S(1)} %collective-permute-done.5), channel_id=1, source_target_pairs={{0,256},{64,320},{128,384},{192,448},{256,1},{320,65},{384,129},{4... | collective-permute-start | bytes 3080 | tf_op jit(solution)/shard_map/ppermute | solution.py:31
  137.6 20.0 %all-to-all-start.2 = ((f32[32,1,256]{2,1,0:T(1,128)}), f32[32,1,256]{2,1,0:T(1,128)S(1)}, u32[]{:S(2)}, u32[]{:S(2)}) async-start(f32[32,1,256]{2,1,0:T(1,128)} %broadcast_in_dim.26), calls=%async_computation.2 | async-start | bytes 65536 | tf_op jit(solution)/shard_map/all_to_all | solution.py:201

commit v7 on v6

--- a/solution.py
+++ b/solution.py
@@ -23,14 +23,6 @@
     return lax.ppermute(value, "tensor", [(0, 1), (1, 0)])
 
 
-def halfway(value):
-    half = lax.axis_size("section")
-    count = 2 * half
-    place = [(plane % half) * 2 + plane // half for plane in range(count)]
-    pairs = [(place[plane], place[(plane + half // 2) % count]) for plane in range(count)]
-    return lax.ppermute(value, ("section", "tensor"), pairs)
-
-
 def same_core():
     count = lax.axis_size("dp")
     return [list(range(core, count, 2)) for core in range(2)]
@@ -38,12 +30,6 @@
 
 def exchanged(value, split, joined):
     return lax.all_to_all(value, "dp", split, joined, axis_index_groups=same_core())
-
-
-def gathered(value):
-    count = lax.axis_size("dp") // 2
-    copies = jnp.broadcast_to(value[None], (count,) + value.shape)
-    return exchanged(copies, 0, 0)
 
 
 def other_core(value):
@@ -59,6 +45,23 @@
 
 def whole(memory=pltpu.VMEM):
     return pl.BlockSpec(memory_space=memory)
+
+
+def spread_kernel(kept_ref, given_ref, copies_ref):
+    columns = kept_ref.shape[1]
+    for place in range(copies_ref.shape[0]):
+        copies_ref[place, :, :columns] = kept_ref[...]
+        copies_ref[place, :, columns:] = given_ref[...]
+
+
+def spread(kept, given, count):
+    length, columns = kept.shape
+    return pl.pallas_call(
+        spread_kernel,
+        out_shape=jax.ShapeDtypeStruct((count, length, 2 * columns), kept.dtype),
+        in_specs=[whole(), whole()],
+        out_specs=whole(),
+    )(kept, given)
 
 
 def norm_kernel(hidden_ref, normed_ref):
@@ -174,12 +177,12 @@
     normed = normed_blocks(hidden_in[0], n_chip)
     normed_columns = exchanged(normed, 0, 0).reshape(n_chip * own_rows, 2 * chunk)
     kept, given = attend(half, query_vectors[0], key_vectors[0], grad_attn[0], positions)
-    own_value = jnp.concatenate([kept, swapped(given)], axis=1)
+    own_values = spread(kept, swapped(given), n_chip)
     device_weight = jnp.concatenate([local_weight, swapped(local_weight)], axis=1)
     full_weight = by_core(core, device_weight, other_core(device_weight))
     chip_gain = lax.dynamic_slice_in_dim(norm_gain[0], chip * 2 * chunk, 2 * chunk, 0)
     own_gain = lax.dynamic_slice_in_dim(norm_gain[0], here * chunk, chunk, 0)
-    group_value = gathered(own_value).reshape(n_chip * own_rows, 2 * own_columns)
+    group_value = exchanged(own_values, 0, 0).reshape(n_chip * own_rows, 2 * own_columns)
     grad_columns = (
         jnp.einsum("tk,ck->tc", group_value, full_weight, preferred_element_type=jnp.float32)
         * chip_gain.astype(jnp.float32)
@@ -190,14 +193,21 @@
     )
     kept_term = lax.dynamic_slice_in_dim(group_term, core * chunk, chunk, 0)
     given_term = lax.dynamic_slice_in_dim(group_term, (1 - core) * chunk, chunk, 0)
-    plane_term = kept_term + other_core(given_term.astype(jnp.bfloat16)).astype(jnp.float32)
-    half_way = halfway(plane_term[:, own_columns:].astype(jnp.bfloat16))
-    given_back = halfway(half_way)
+    plane_term = kept_term + other_core(given_term.astype(jnp.bfloat16)).astype(
+        jnp.float32
+    )
     plane_sum = jnp.sum(plane_term * device_weight.astype(jnp.float32), axis=1)
-    weight_grad = (plane_term[:, :own_columns] + given_back.astype(jnp.float32)) * own_gain.astype(
+    sum_high = lax.reduce_precision(plane_sum, 8, 7)
+    sums = jnp.stack([sum_high, plane_sum - sum_high]).astype(jnp.bfloat16)
+    sent_term = jnp.concatenate(
+        [plane_term[:, own_columns:].astype(jnp.bfloat16), jnp.pad(sums, ((0, 14), (0, 0)))], axis=0
+    )
+    received = swapped(sent_term).astype(jnp.float32)
+    given_back = received[:chunk]
+    home_sum = plane_sum + received[chunk] + received[chunk + 1]
+    weight_grad = (plane_term[:, :own_columns] + given_back) * own_gain.astype(
         jnp.float32
     )[:, None]
-    home_sum = plane_sum + halfway(halfway(plane_sum))
     all_sums = lax.all_to_all(jnp.broadcast_to(home_sum[None], (n_dp, chunk)), "dp", 0, 0)
     gain_grad = all_sums.reshape(width)
     grad_hidden = finished(grad_blocks, hidden_in[0])

time: 161 us -> 150 us (0.932)
  the two profiles are of different devices: /device:TPU:1 before, /device:TPU:32 now
where the time goes in v7:
time: 150 us; the launch traced here: 149 us
  starting transfers between devices  67 us (45%)
  waiting for transfers between devices  59.5 us (40%)
  Pallas kernels  10.7 us (7%)
  local copies, waits for them, and re-layouts  4.82 us (3%)
  other arithmetic  3.55 us (2%)
  matrix products  2.48 us (2%)
    ppermute x3, starting transfers between devices, swapped(): return lax.ppermute(value, 'tensor', [(0, 1), (1, 0)])  37.4 us
    ppermute x3, waiting for transfers between devices, swapped(): return lax.ppermute(value, 'tensor', [(0, 1), (1, 0)])  30.5 us
    all_to_all x3, waiting for transfers between devices, exchanged(): lax.all_to_all(value, 'dp', split, joined, axis_index_groups=same_core())  20.1 us
    all_to_all x3, starting transfers between devices, exchanged(): lax.all_to_all(value, 'dp', split, joined, axis_index_groups=same_core())  17.1 us
    all_to_all x1, waiting for transfers between devices, layer(): lax.all_to_all(jnp.broadcast_to(home_sum[None], (n_dp, chunk)), 'dp', 0, 0)  6.63 us
    all_to_all x1, starting transfers between devices, layer(): lax.all_to_all(jnp.broadcast_to(home_sum[None], (n_dp, chunk)), 'dp', 0, 0)  5.34 us
    unnamed x10, local copies, waits for them, and re-layouts  4.14 us
    ppermute x2, starting transfers between devices, other_core(): lax.ppermute(value, 'dp', [(source, source ^ 1) for source in range(count)])  3.84 us
  transfers between devices with their start and end apart: 10, of which 8 were waited for; matrix products, arithmetic and copies ran while one was open for 5% of the time, Pallas kernels for 2%

profile of v7, /device:TPU:32, one launch (start us, length us, event | category | flops | bytes accessed | tf_op | source)
XLA Modules:
  0.0 148.9 jit_solution(17627144926149018562)
XLA Ops:
  0.6 3.1 %shard_map.94 = (bf16[64,256]{1,0:T(8,128)(2,1)}, bf16[64,256]{1,0:T(8,128)(2,1)}) custom-call(s32[1]{0:T(128)} %bitcast.half_ref, bf16[128,2048]{1,0:T(8,128)(2,1)} %bitcast.35, bf16[128,256]{1,0:T(8,128)(2,1)} %bitcast.38, bf16[128,2048]{1,0:T(8,128)(2,1)} %bitcast.36, s32[1,128]{1,0:T(1,128)} %position_ref.1), custom_call_target="tpu_custom_call" | custom-call | tf_op jit(solution)/shard_map/pallas_call | solution.py:128
  3.8 14.8 %collective-permute-start = (bf16[64,256]{1,0:T(8,128)(2,1)}, bf16[64,256]{1,0:T(8,128)(2,1)S(1)}, u32[]{:S(2)}, u32[]{:S(2)}) collective-permute-start(bf16[64,256]{1,0:T(8,128)(2,1)} %get-tuple-element.6), channel_id=1, source_target_pairs={{0,1},{1,0},{2,3},{3,2},{4,5},{5,4},{6,7},{7,6},{8,9},{9,8},{10,11... | collective-permute-start | bytes 98312 | tf_op jit(solution)/shard_map/ppermute | solution.py:23
  18.6 2.5 %collective-permute-done.given_ref = bf16[64,256]{1,0:T(8,128)(2,1)S(1)} collective-permute-done((bf16[64,256]{1,0:T(8,128)(2,1)}, bf16[64,256]{1,0:T(8,128)(2,1)S(1)}, u32[]{:S(2)}, u32[]{:S(2)}) %collective-permute-start) | collective-permute-done | bytes 32800 | tf_op jit(solution)/shard_map/ppermute | solution.py:23
  21.1 0.0 copy-start.3
  21.1 0.6 copy-done.3
  21.7 1.8 %shard_map.95 = bf16[16,64,512]{2,1,0:T(8,128)(2,1)} custom-call(bf16[64,256]{1,0:T(8,128)(2,1)} %get-tuple-element.5.kept_ref, bf16[64,256]{1,0:T(8,128)(2,1)} %copy-done.3), custom_call_target="tpu_custom_call" | custom-call | tf_op jit(solution)/shard_map/pallas_call | solution.py:59
  23.6 0.0 copy-start.1
  23.6 7.2 %all-to-all-start = ((bf16[16,64,512]{2,1,0:T(8,128)(2,1)}), bf16[16,64,512]{2,1,0:T(8,128)(2,1)S(1)}, u32[]{:S(2)}, u32[]{:S(2)}) async-start(bf16[16,64,512]{2,1,0:T(8,128)(2,1)} %shard_map.95), calls=%async_computation | async-start | bytes 2097152 | tf_op jit(solution)/shard_map/all_to_all | solution.py:32
  30.8 0.0 copy-done.1
  30.8 12.3 %collective-permute-start.2 = (bf16[256,256]{1,0:T(8,128)(2,1)S(1)}, bf16[256,256]{1,0:T(8,128)(2,1)S(1)}, u32[]{:S(2)}, u32[]{:S(2)}) collective-permute-start(bf16[256,256]{1,0:T(8,128)(2,1)S(1)} %bitcast.28), channel_id=1, source_target_pairs={{0,1},{1,0},{2,3},{3,2},{4,5},{5,4},{6,7},{7,6},{8,9},{9,8},{10,11... | collective-permute-start | bytes 393224 | tf_op jit(solution)/shard_map/ppermute | solution.py:23
  43.1 2.5 %shard_map.96 = bf16[16,64,512]{2,1,0:T(8,128)(2,1)} custom-call(bf16[64,8192]{1,0:T(8,128)(2,1)} %bitcast.26), custom_call_target="tpu_custom_call" | custom-call | tf_op jit(solution)/shard_map/pallas_call | solution.py:84
  45.6 0.9 all-to-all-done
  46.5 6.3 %all-to-all-start.1 = ((bf16[16,64,512]{2,1,0:T(8,128)(2,1)}), bf16[16,64,512]{2,1,0:T(8,128)(2,1)S(1)}, u32[]{:S(2)}, u32[]{:S(2)}) async-start(bf16[16,64,512]{2,1,0:T(8,128)(2,1)} %shard_map.96), calls=%async_computation.1 | async-start | bytes 2097152 | tf_op jit(solution)/shard_map/all_to_all | solution.py:32
  52.8 0.0 collective-permute-done.2
  52.9 1.9 %collective-permute-start.4 = (bf16[256,512]{1,0:T(8,128)(2,1)S(1)}, bf16[256,512]{1,0:T(8,128)(2,1)S(1)}, u32[]{:S(2)}, u32[]{:S(2)}) collective-permute-start(bf16[256,512]{1,0:T(8,128)(2,1)S(1)} %pad_maximum_fusion), channel_id=1, source_target_pairs={{0,2},{2,0},{4,6},{6,4},{8,10},{10,8},{12,14},{14,12},{16,18},{18,... | collective-permute-start | bytes 786440 | tf_op jit(solution)/shard_map/ppermute | solution.py:37
  54.8 0.7 dynamic-slice_convert_fusion.1
  55.5 0.8 collective-permute-done.4
  56.3 0.1 broadcast_select_fusion.1
  56.4 1.7 %multiply_convert_fusion = bf16[1024,512]{1,0:T(8,128)(2,1)} fusion(bf16[1024,512]{1,0:T(8,128)(2,1)S(1)} %bitcast.32, f32[512]{0:T(512)S(1)} %bitcast.43, bf16[256,512]{1,0:T(8,128)(2,1)S(1)} %get-tuple-element.10, bf16[256,512]{1,0:T(8,128)(2,1)S(1)} %get-tuple-element.9), kind=kOutput, calls=%fused_computation | convolution fusion | flops 538968064 | bytes 2623488 | tf_op jit(solution)/shard_map/tk,ck->tc/dot_general | solution.py:187
  58.1 9.8 %all-to-all-done.1 = bf16[16,64,512]{2,1,0:T(8,128)(2,1)S(1)} async-done(((bf16[16,64,512]{2,1,0:T(8,128)(2,1)}), bf16[16,64,512]{2,1,0:T(8,128)(2,1)S(1)}, u32[]{:S(2)}, u32[]{:S(2)}) %all-to-all-start.1) | async-done | bytes 1048608 | tf_op jit(solution)/shard_map/all_to_all | solution.py:32
  68.0 3.7 %all-to-all-start.3 = ((bf16[16,64,512]{2,1,0:T(8,128)(2,1)}), bf16[16,64,512]{2,1,0:T(8,128)(2,1)S(1)}, u32[]{:S(2)}, u32[]{:S(2)}) async-start(bf16[16,64,512]{2,1,0:T(8,128)(2,1)} %bitcast.34), calls=%async_computation.3 | async-start | bytes 2097152 | tf_op jit(solution)/shard_map/all_to_all | solution.py:32
  71.6 0.8 convolution_bitcast_fusion
  72.4 0.0 copy-start.2
  72.4 1.0 copy-done.2
  73.4 1.9 %collective-permute-start.1 = (bf16[256,512]{1,0:T(8,128)(2,1)S(1)}, bf16[256,512]{1,0:T(8,128)(2,1)S(1)}, u32[]{:S(2)}, u32[]{:S(2)}) collective-permute-start(bf16[256,512]{1,0:T(8,128)(2,1)S(1)} %fusion.3), channel_id=1, source_target_pairs={{0,2},{2,0},{4,6},{6,4},{8,10},{10,8},{12,14},{14,12},{16,18},{18,... | collective-permute-start | bytes 786440 | tf_op jit(solution)/shard_map/ppermute | solution.py:37
  75.3 1.5 %collective-permute-done.1 = bf16[256,512]{1,0:T(8,128)(2,1)S(1)} collective-permute-done((bf16[256,512]{1,0:T(8,128)(2,1)S(1)}, bf16[256,512]{1,0:T(8,128)(2,1)S(1)}, u32[]{:S(2)}, u32[]{:S(2)}) %collective-permute-start.1) | collective-permute-done | bytes 262176 | tf_op jit(solution)/shard_map/ppermute | solution.py:37
  76.8 1.2 multiply_reduce_fusion
  78.1 9.3 %all-to-all-done.3.grad_ref = bf16[16,64,512]{2,1,0:T(8,128)(2,1)S(1)} async-done(((bf16[16,64,512]{2,1,0:T(8,128)(2,1)}), bf16[16,64,512]{2,1,0:T(8,128)(2,1)S(1)}, u32[]{:S(2)}, u32[]{:S(2)}) %all-to-all-start.3) | async-done | bytes 1048608 | tf_op jit(solution)/shard_map/all_to_all | solution.py:32
  87.4 0.0 copy-start
  87.4 1.0 copy-done
  88.4 3.2 %shard_map.97 = bf16[64,8192]{1,0:T(8,128)(2,1)} custom-call(bf16[16,64,512]{2,1,0:T(8,128)(2,1)} %copy-done, bf16[64,8192]{1,0:T(8,128)(2,1)} %bitcast.27), custom_call_target="tpu_custom_call" | custom-call | tf_op jit(solution)/shard_map/pallas_call | solution.py:158
  91.6 3.3 %collective-permute-start.5 = (bf16[64,8192]{1,0:T(8,128)(2,1)}, bf16[64,8192]{1,0:T(8,128)(2,1)S(1)}, u32[]{:S(2)}, u32[]{:S(2)}) collective-permute-start(bf16[64,8192]{1,0:T(8,128)(2,1)} %shard_map.97), channel_id=1, source_target_pairs={{64,0},{128,64},{192,128},{256,192},{320,256},{384,320},{448,384},... | collective-permute-start | bytes 3145736 | tf_op jit(solution)/shard_map/ppermute | solution.py:19
  95.0 10.2 %collective-permute-start.3 = (bf16[272,256]{1,0:T(8,128)(2,1)S(1)}, bf16[272,256]{1,0:T(8,128)(2,1)S(1)}, u32[]{:S(2)}, u32[]{:S(2)}) collective-permute-start(bf16[272,256]{1,0:T(8,128)(2,1)S(1)} %pad_maximum_fusion.1), channel_id=1, source_target_pairs={{0,1},{1,0},{2,3},{3,2},{4,5},{5,4},{6,7},{7,6},{8,9},{9,8},{10,11... | collective-permute-start | bytes 417800 | tf_op jit(solution)/shard_map/ppermute | solution.py:23
  105.2 0.7 dynamic-slice_convert_fusion.2
  105.9 27.9 %collective-permute-done.3 = bf16[272,256]{1,0:T(8,128)(2,1)S(1)} collective-permute-done((bf16[272,256]{1,0:T(8,128)(2,1)S(1)}, bf16[272,256]{1,0:T(8,128)(2,1)S(1)}, u32[]{:S(2)}, u32[]{:S(2)}) %collective-permute-start.3) | collective-permute-done | bytes 139296 | tf_op jit(solution)/shard_map/ppermute | solution.py:23
  133.9 0.6 broadcast_in_dim.19
  134.5 5.3 %all-to-all-start.2 = ((f32[32,1,256]{2,1,0:T(1,128)}), f32[32,1,256]{2,1,0:T(1,128)S(1)}, u32[]{:S(2)}, u32[]{:S(2)}) async-start(f32[32,1,256]{2,1,0:T(1,128)} %broadcast_in_dim.19), calls=%async_computation.2 | async-start | bytes 65536 | tf_op jit(solution)/shard_map/all_to_all | solution.py:211
  139.9 0.8 fusion.5
  140.7 6.6 %all-to-all-done.2 = f32[32,1,256]{2,1,0:T(1,128)S(1)} async-done(((f32[32,1,256]{2,1,0:T(1,128)}), f32[32,1,256]{2,1,0:T(1,128)S(1)}, u32[]{:S(2)}, u32[]{:S(2)}) %all-to-all-start.2) | async-done | bytes 32800 | tf_op jit(solution)/shard_map/all_to_all | solution.py:211
  147.3 0.0 collective-permute-done.5
  147.3 0.6 copy.12
  147.9 1.0 copy.13
  (8 shorter events, 0.1 us)
Async XLA Ops:
  3.8 17.4 %collective-permute-start = (bf16[64,256]{1,0:T(8,128)(2,1)}, bf16[64,256]{1,0:T(8,128)(2,1)S(1)}, u32[]{:S(2)}, u32[]{:S(2)}) collective-permute-start(bf16[64,256]{1,0:T(8,128)(2,1)} %get-tuple-element.6), channel_id=1, source_target_pairs={{0,1},{1,0},{2,3},{3,2},{4,5},{5,4},{6,7},{7,6},{8,9},{9,8},{10,11... | collective-permute-start | bytes 98312 | tf_op jit(solution)/shard_map/ppermute | solution.py:23
  21.1 0.6 copy-start.3
  23.6 7.2 %copy-start.1 = (bf16[1,256,256]{2,1,0:T(8,128)(2,1)S(1)}, bf16[1,256,256]{2,1,0:T(8,128)(2,1)}, u32[]{:S(2)}) copy-start(bf16[1,256,256]{2,1,0:T(8,128)(2,1)} %param.9) | copy-start | bytes 393220
  23.6 23.0 %all-to-all-start = ((bf16[16,64,512]{2,1,0:T(8,128)(2,1)}), bf16[16,64,512]{2,1,0:T(8,128)(2,1)S(1)}, u32[]{:S(2)}, u32[]{:S(2)}) async-start(bf16[16,64,512]{2,1,0:T(8,128)(2,1)} %shard_map.95), calls=%async_computation | async-start | bytes 2097152 | tf_op jit(solution)/shard_map/all_to_all | solution.py:32
  30.8 22.1 %collective-permute-start.2 = (bf16[256,256]{1,0:T(8,128)(2,1)S(1)}, bf16[256,256]{1,0:T(8,128)(2,1)S(1)}, u32[]{:S(2)}, u32[]{:S(2)}) collective-permute-start(bf16[256,256]{1,0:T(8,128)(2,1)S(1)} %bitcast.28), channel_id=1, source_target_pairs={{0,1},{1,0},{2,3},{3,2},{4,5},{5,4},{6,7},{7,6},{8,9},{9,8},{10,11... | collective-permute-start | bytes 393224 | tf_op jit(solution)/shard_map/ppermute | solution.py:23
  46.5 21.4 %all-to-all-start.1 = ((bf16[16,64,512]{2,1,0:T(8,128)(2,1)}), bf16[16,64,512]{2,1,0:T(8,128)(2,1)S(1)}, u32[]{:S(2)}, u32[]{:S(2)}) async-start(bf16[16,64,512]{2,1,0:T(8,128)(2,1)} %shard_map.96), calls=%async_computation.1 | async-start | bytes 2097152 | tf_op jit(solution)/shard_map/all_to_all | solution.py:32
  52.9 3.4 %collective-permute-start.4 = (bf16[256,512]{1,0:T(8,128)(2,1)S(1)}, bf16[256,512]{1,0:T(8,128)(2,1)S(1)}, u32[]{:S(2)}, u32[]{:S(2)}) collective-permute-start(bf16[256,512]{1,0:T(8,128)(2,1)S(1)} %pad_maximum_fusion), channel_id=1, source_target_pairs={{0,2},{2,0},{4,6},{6,4},{8,10},{10,8},{12,14},{14,12},{16,18},{18,... | collective-permute-start | bytes 786440 | tf_op jit(solution)/shard_map/ppermute | solution.py:37
  68.0 19.4 %all-to-all-start.3 = ((bf16[16,64,512]{2,1,0:T(8,128)(2,1)}), bf16[16,64,512]{2,1,0:T(8,128)(2,1)S(1)}, u32[]{:S(2)}, u32[]{:S(2)}) async-start(bf16[16,64,512]{2,1,0:T(8,128)(2,1)} %bitcast.34), calls=%async_computation.3 | async-start | bytes 2097152 | tf_op jit(solution)/shard_map/all_to_all | solution.py:32
  72.4 1.0 copy-start.2
  73.4 3.4 %collective-permute-start.1 = (bf16[256,512]{1,0:T(8,128)(2,1)S(1)}, bf16[256,512]{1,0:T(8,128)(2,1)S(1)}, u32[]{:S(2)}, u32[]{:S(2)}) collective-permute-start(bf16[256,512]{1,0:T(8,128)(2,1)S(1)} %fusion.3), channel_id=1, source_target_pairs={{0,2},{2,0},{4,6},{6,4},{8,10},{10,8},{12,14},{14,12},{16,18},{18,... | collective-permute-start | bytes 786440 | tf_op jit(solution)/shard_map/ppermute | solution.py:37
  87.4 1.0 copy-start
  91.6 55.7 %collective-permute-start.5 = (bf16[64,8192]{1,0:T(8,128)(2,1)}, bf16[64,8192]{1,0:T(8,128)(2,1)S(1)}, u32[]{:S(2)}, u32[]{:S(2)}) collective-permute-start(bf16[64,8192]{1,0:T(8,128)(2,1)} %shard_map.97), channel_id=1, source_target_pairs={{64,0},{128,64},{192,128},{256,192},{320,256},{384,320},{448,384},... | collective-permute-start | bytes 3145736 | tf_op jit(solution)/shard_map/ppermute | solution.py:19
  95.0 38.9 %collective-permute-start.3 = (bf16[272,256]{1,0:T(8,128)(2,1)S(1)}, bf16[272,256]{1,0:T(8,128)(2,1)S(1)}, u32[]{:S(2)}, u32[]{:S(2)}) collective-permute-start(bf16[272,256]{1,0:T(8,128)(2,1)S(1)} %pad_maximum_fusion.1), channel_id=1, source_target_pairs={{0,1},{1,0},{2,3},{3,2},{4,5},{5,4},{6,7},{7,6},{8,9},{9,8},{10,11... | collective-permute-start | bytes 417800 | tf_op jit(solution)/shard_map/ppermute | solution.py:23
  134.5 12.8 %all-to-all-start.2 = ((f32[32,1,256]{2,1,0:T(1,128)}), f32[32,1,256]{2,1,0:T(1,128)S(1)}, u32[]{:S(2)}, u32[]{:S(2)}) async-start(f32[32,1,256]{2,1,0:T(1,128)} %broadcast_in_dim.19), calls=%async_computation.2 | async-start | bytes 65536 | tf_op jit(solution)/shard_map/all_to_all | solution.py:211

commit v8 on v7

--- a/solution.py
+++ b/solution.py
@@ -32,6 +32,12 @@
     return lax.all_to_all(value, "dp", split, joined, axis_index_groups=same_core())
 
 
+def gathered(value):
+    count = lax.axis_size("dp") // 2
+    copies = jnp.broadcast_to(value[None], (count,) + value.shape)
+    return exchanged(copies, 0, 0)
+
+
 def other_core(value):
     count = lax.axis_size("dp")
     return lax.ppermute(value, "dp", [(source, source ^ 1) for source in range(count)])
@@ -45,23 +51,6 @@
 
 def whole(memory=pltpu.VMEM):
     return pl.BlockSpec(memory_space=memory)
-
-
-def spread_kernel(kept_ref, given_ref, copies_ref):
-    columns = kept_ref.shape[1]
-    for place in range(copies_ref.shape[0]):
-        copies_ref[place, :, :columns] = kept_ref[...]
-        copies_ref[place, :, columns:] = given_ref[...]
-
-
-def spread(kept, given, count):
-    length, columns = kept.shape
-    return pl.pallas_call(
-        spread_kernel,
-        out_shape=jax.ShapeDtypeStruct((count, length, 2 * columns), kept.dtype),
-        in_specs=[whole(), whole()],
-        out_specs=whole(),
-    )(kept, given)
 
 
 def norm_kernel(hidden_ref, normed_ref):
@@ -177,12 +166,12 @@
     normed = normed_blocks(hidden_in[0], n_chip)
     normed_columns = exchanged(normed, 0, 0).reshape(n_chip * own_rows, 2 * chunk)
     kept, given = attend(half, query_vectors[0], key_vectors[0], grad_attn[0], positions)
-    own_values = spread(kept, swapped(given), n_chip)
+    own_value = jnp.concatenate([kept, swapped(given)], axis=1)
     device_weight = jnp.concatenate([local_weight, swapped(local_weight)], axis=1)
     full_weight = by_core(core, device_weight, other_core(device_weight))
     chip_gain = lax.dynamic_slice_in_dim(norm_gain[0], chip * 2 * chunk, 2 * chunk, 0)
     own_gain = lax.dynamic_slice_in_dim(norm_gain[0], here * chunk, chunk, 0)
-    group_value = exchanged(own_values, 0, 0).reshape(n_chip * own_rows, 2 * own_columns)
+    group_value = gathered(own_value).reshape(n_chip * own_rows, 2 * own_columns)
     grad_columns = (
         jnp.einsum("tk,ck->tc", group_value, full_weight, preferred_element_type=jnp.float32)
         * chip_gain.astype(jnp.float32)

time: 150 us -> 149 us (level)
  Pallas kernels: 10.7 us -> 8.86 us
    pallas_call x1 -> x0, Pallas kernels: 1.84 us -> none  [spread(): pl.pallas_call(spread_kernel, out_shape=jax.ShapeDtypeStruct((count, leng...]
    unnamed x10 -> x8, local copies, waits for them, and re-layouts: 4.14 us -> 3.52 us
where the time goes in v8:
time: 149 us; the launch traced here: 148 us
  starting transfers between devices  67 us (45%)
  waiting for transfers between devices  59.5 us (40%)
  Pallas kernels  8.86 us (6%)
  local copies, waits for them, and re-layouts  5.28 us (4%)
  other arithmetic  4.31 us (3%)
  matrix products  2.49 us (2%)
    ppermute x3, starting transfers between devices, swapped(): return lax.ppermute(value, 'tensor', [(0, 1), (1, 0)])  37.4 us
    ppermute x3, waiting for transfers between devices, swapped(): return lax.ppermute(value, 'tensor', [(0, 1), (1, 0)])  30.5 us
    all_to_all x3, waiting for transfers between devices, exchanged(): lax.all_to_all(value, 'dp', split, joined, axis_index_groups=same_core())  20.1 us
    all_to_all x3, starting transfers between devices, exchanged(): lax.all_to_all(value, 'dp', split, joined, axis_index_groups=same_core())  17.1 us
    all_to_all x1, waiting for transfers between devices, layer(): lax.all_to_all(jnp.broadcast_to(home_sum[None], (n_dp, chunk)), 'dp', 0, 0)  6.63 us
    all_to_all x1, starting transfers between devices, layer(): lax.all_to_all(jnp.broadcast_to(home_sum[None], (n_dp, chunk)), 'dp', 0, 0)  5.34 us
    ppermute x2, starting transfers between devices, other_core(): lax.ppermute(value, 'dp', [(source, source ^ 1) for source in range(count)])  3.84 us
    unnamed x8, local copies, waits for them, and re-layouts  3.52 us
  transfers between devices with their start and end apart: 10, of which 8 were waited for; matrix products, arithmetic and copies ran while one was open for 5% of the time, Pallas kernels for 2%

profile of v8, /device:TPU:32, one launch (start us, length us, event | category | flops | bytes accessed | tf_op | source)
XLA Modules:
  0.0 148.3 jit_solution(11914011578791634919)
XLA Ops:
  0.6 3.1 %shard_map.94 = (bf16[64,256]{1,0:T(8,128)(2,1)}, bf16[64,256]{1,0:T(8,128)(2,1)}) custom-call(s32[1]{0:T(128)} %bitcast.half_ref, bf16[128,2048]{1,0:T(8,128)(2,1)} %bitcast.35, bf16[128,256]{1,0:T(8,128)(2,1)} %bitcast.38, bf16[128,2048]{1,0:T(8,128)(2,1)} %bitcast.36, s32[1,128]{1,0:T(1,128)} %position_ref.1), custom_call_target="tpu_custom_call" | custom-call | tf_op jit(solution)/shard_map/pallas_call | solution.py:117
  3.8 14.8 %collective-permute-start = (bf16[64,256]{1,0:T(8,128)(2,1)}, bf16[64,256]{1,0:T(8,128)(2,1)S(1)}, u32[]{:S(2)}, u32[]{:S(2)}) collective-permute-start(bf16[64,256]{1,0:T(8,128)(2,1)} %get-tuple-element.6), channel_id=1, source_target_pairs={{0,1},{1,0},{2,3},{3,2},{4,5},{5,4},{6,7},{7,6},{8,9},{9,8},{10,11... | collective-permute-start | bytes 98312 | tf_op jit(solution)/shard_map/ppermute | solution.py:23
  18.6 2.5 %collective-permute-done = bf16[64,256]{1,0:T(8,128)(2,1)S(1)} collective-permute-done((bf16[64,256]{1,0:T(8,128)(2,1)}, bf16[64,256]{1,0:T(8,128)(2,1)S(1)}, u32[]{:S(2)}, u32[]{:S(2)}) %collective-permute-start) | collective-permute-done | bytes 32800 | tf_op jit(solution)/shard_map/ppermute | solution.py:23
  21.1 0.8 pad_maximum_fusion.2
  21.9 1.1 broadcast_in_dim.11
  23.0 0.0 copy-start.1
  23.0 7.2 %all-to-all-start = ((bf16[16,64,512]{2,1,0:T(8,128)(2,1)}), bf16[16,64,512]{2,1,0:T(8,128)(2,1)S(1)}, u32[]{:S(2)}, u32[]{:S(2)}) async-start(bf16[16,64,512]{2,1,0:T(8,128)(2,1)} %broadcast_in_dim.11), calls=%async_computation | async-start | bytes 2097152 | tf_op jit(solution)/shard_map/all_to_all | solution.py:32
  30.1 0.0 copy-done.1
  30.2 12.3 %collective-permute-start.2 = (bf16[256,256]{1,0:T(8,128)(2,1)S(1)}, bf16[256,256]{1,0:T(8,128)(2,1)S(1)}, u32[]{:S(2)}, u32[]{:S(2)}) collective-permute-start(bf16[256,256]{1,0:T(8,128)(2,1)S(1)} %bitcast.28), channel_id=1, source_target_pairs={{0,1},{1,0},{2,3},{3,2},{4,5},{5,4},{6,7},{7,6},{8,9},{9,8},{10,11... | collective-permute-start | bytes 393224 | tf_op jit(solution)/shard_map/ppermute | solution.py:23
  42.5 2.5 %shard_map.95 = bf16[16,64,512]{2,1,0:T(8,128)(2,1)} custom-call(bf16[64,8192]{1,0:T(8,128)(2,1)} %bitcast.26), custom_call_target="tpu_custom_call" | custom-call | tf_op jit(solution)/shard_map/pallas_call | solution.py:73
  45.0 0.9 all-to-all-done
  45.9 6.3 %all-to-all-start.1 = ((bf16[16,64,512]{2,1,0:T(8,128)(2,1)}), bf16[16,64,512]{2,1,0:T(8,128)(2,1)S(1)}, u32[]{:S(2)}, u32[]{:S(2)}) async-start(bf16[16,64,512]{2,1,0:T(8,128)(2,1)} %shard_map.95), calls=%async_computation.1 | async-start | bytes 2097152 | tf_op jit(solution)/shard_map/all_to_all | solution.py:32
  52.2 0.0 collective-permute-done.2
  52.3 1.9 %collective-permute-start.4 = (bf16[256,512]{1,0:T(8,128)(2,1)S(1)}, bf16[256,512]{1,0:T(8,128)(2,1)S(1)}, u32[]{:S(2)}, u32[]{:S(2)}) collective-permute-start(bf16[256,512]{1,0:T(8,128)(2,1)S(1)} %pad_maximum_fusion), channel_id=1, source_target_pairs={{0,2},{2,0},{4,6},{6,4},{8,10},{10,8},{12,14},{14,12},{16,18},{18,... | collective-permute-start | bytes 786440 | tf_op jit(solution)/shard_map/ppermute | solution.py:43
  54.2 0.7 dynamic-slice_convert_fusion.1
  54.9 0.8 collective-permute-done.4
  55.7 0.1 broadcast_select_fusion.1
  55.8 1.7 %multiply_convert_fusion = bf16[1024,512]{1,0:T(8,128)(2,1)} fusion(bf16[1024,512]{1,0:T(8,128)(2,1)S(1)} %bitcast.32, f32[512]{0:T(512)S(1)} %bitcast.43, bf16[256,512]{1,0:T(8,128)(2,1)S(1)} %get-tuple-element.10, bf16[256,512]{1,0:T(8,128)(2,1)S(1)} %get-tuple-element.9), kind=kOutput, calls=%fused_computation | convolution fusion | flops 538968064 | bytes 2623488 | tf_op jit(solution)/shard_map/tk,ck->tc/dot_general | solution.py:176
  57.5 9.8 %all-to-all-done.1 = bf16[16,64,512]{2,1,0:T(8,128)(2,1)S(1)} async-done(((bf16[16,64,512]{2,1,0:T(8,128)(2,1)}), bf16[16,64,512]{2,1,0:T(8,128)(2,1)S(1)}, u32[]{:S(2)}, u32[]{:S(2)}) %all-to-all-start.1) | async-done | bytes 1048608 | tf_op jit(solution)/shard_map/all_to_all | solution.py:32
  67.4 3.7 %all-to-all-start.3 = ((bf16[16,64,512]{2,1,0:T(8,128)(2,1)}), bf16[16,64,512]{2,1,0:T(8,128)(2,1)S(1)}, u32[]{:S(2)}, u32[]{:S(2)}) async-start(bf16[16,64,512]{2,1,0:T(8,128)(2,1)} %bitcast.34), calls=%async_computation.3 | async-start | bytes 2097152 | tf_op jit(solution)/shard_map/all_to_all | solution.py:32
  71.0 0.8 convolution_bitcast_fusion
  71.8 0.0 copy-start.2
  71.8 1.0 copy-done.2
  72.8 1.9 %collective-permute-start.1 = (bf16[256,512]{1,0:T(8,128)(2,1)S(1)}, bf16[256,512]{1,0:T(8,128)(2,1)S(1)}, u32[]{:S(2)}, u32[]{:S(2)}) collective-permute-start(bf16[256,512]{1,0:T(8,128)(2,1)S(1)} %fusion.3), channel_id=1, source_target_pairs={{0,2},{2,0},{4,6},{6,4},{8,10},{10,8},{12,14},{14,12},{16,18},{18,... | collective-permute-start | bytes 786440 | tf_op jit(solution)/shard_map/ppermute | solution.py:43
  74.7 1.5 %collective-permute-done.1 = bf16[256,512]{1,0:T(8,128)(2,1)S(1)} collective-permute-done((bf16[256,512]{1,0:T(8,128)(2,1)S(1)}, bf16[256,512]{1,0:T(8,128)(2,1)S(1)}, u32[]{:S(2)}, u32[]{:S(2)}) %collective-permute-start.1) | collective-permute-done | bytes 262176 | tf_op jit(solution)/shard_map/ppermute | solution.py:43
  76.2 1.2 multiply_reduce_fusion
  77.5 9.3 %all-to-all-done.3.grad_ref = bf16[16,64,512]{2,1,0:T(8,128)(2,1)S(1)} async-done(((bf16[16,64,512]{2,1,0:T(8,128)(2,1)}), bf16[16,64,512]{2,1,0:T(8,128)(2,1)S(1)}, u32[]{:S(2)}, u32[]{:S(2)}) %all-to-all-start.3) | async-done | bytes 1048608 | tf_op jit(solution)/shard_map/all_to_all | solution.py:32
  86.8 0.0 copy-start
  86.8 1.0 copy-done
  87.8 3.2 %shard_map.96 = bf16[64,8192]{1,0:T(8,128)(2,1)} custom-call(bf16[16,64,512]{2,1,0:T(8,128)(2,1)} %copy-done, bf16[64,8192]{1,0:T(8,128)(2,1)} %bitcast.27), custom_call_target="tpu_custom_call" | custom-call | tf_op jit(solution)/shard_map/pallas_call | solution.py:147
  91.0 3.3 %collective-permute-start.5 = (bf16[64,8192]{1,0:T(8,128)(2,1)}, bf16[64,8192]{1,0:T(8,128)(2,1)S(1)}, u32[]{:S(2)}, u32[]{:S(2)}) collective-permute-start(bf16[64,8192]{1,0:T(8,128)(2,1)} %shard_map.96), channel_id=1, source_target_pairs={{64,0},{128,64},{192,128},{256,192},{320,256},{384,320},{448,384},... | collective-permute-start | bytes 3145736 | tf_op jit(solution)/shard_map/ppermute | solution.py:19
  94.4 10.2 %collective-permute-start.3 = (bf16[272,256]{1,0:T(8,128)(2,1)S(1)}, bf16[272,256]{1,0:T(8,128)(2,1)S(1)}, u32[]{:S(2)}, u32[]{:S(2)}) collective-permute-start(bf16[272,256]{1,0:T(8,128)(2,1)S(1)} %pad_maximum_fusion.1), channel_id=1, source_target_pairs={{0,1},{1,0},{2,3},{3,2},{4,5},{5,4},{6,7},{7,6},{8,9},{9,8},{10,11... | collective-permute-start | bytes 417800 | tf_op jit(solution)/shard_map/ppermute | solution.py:23
  104.6 0.7 dynamic-slice_convert_fusion.2
  105.3 28.0 %collective-permute-done.3 = bf16[272,256]{1,0:T(8,128)(2,1)S(1)} collective-permute-done((bf16[272,256]{1,0:T(8,128)(2,1)S(1)}, bf16[272,256]{1,0:T(8,128)(2,1)S(1)}, u32[]{:S(2)}, u32[]{:S(2)}) %collective-permute-start.3) | collective-permute-done | bytes 139296 | tf_op jit(solution)/shard_map/ppermute | solution.py:23
  133.3 0.6 broadcast_in_dim.26
  133.9 5.3 %all-to-all-start.2 = ((f32[32,1,256]{2,1,0:T(1,128)}), f32[32,1,256]{2,1,0:T(1,128)S(1)}, u32[]{:S(2)}, u32[]{:S(2)}) async-start(f32[32,1,256]{2,1,0:T(1,128)} %broadcast_in_dim.26), calls=%async_computation.2 | async-start | bytes 65536 | tf_op jit(solution)/shard_map/all_to_all | solution.py:200
  139.3 0.8 fusion.5
  140.1 6.6 %all-to-all-done.2 = f32[32,1,256]{2,1,0:T(1,128)S(1)} async-done(((f32[32,1,256]{2,1,0:T(1,128)}), f32[32,1,256]{2,1,0:T(1,128)S(1)}, u32[]{:S(2)}, u32[]{:S(2)}) %all-to-all-start.2) | async-done | bytes 32800 | tf_op jit(solution)/shard_map/all_to_all | solution.py:200
  146.7 0.0 collective-permute-done.5
  146.7 0.6 copy.12
  147.3 1.0 copy.13
  (8 shorter events, 0.1 us)
Async XLA Ops:
  3.8 17.4 %collective-permute-start = (bf16[64,256]{1,0:T(8,128)(2,1)}, bf16[64,256]{1,0:T(8,128)(2,1)S(1)}, u32[]{:S(2)}, u32[]{:S(2)}) collective-permute-start(bf16[64,256]{1,0:T(8,128)(2,1)} %get-tuple-element.6), channel_id=1, source_target_pairs={{0,1},{1,0},{2,3},{3,2},{4,5},{5,4},{6,7},{7,6},{8,9},{9,8},{10,11... | collective-permute-start | bytes 98312 | tf_op jit(solution)/shard_map/ppermute | solution.py:23
  23.0 7.2 %copy-start.1 = (bf16[1,256,256]{2,1,0:T(8,128)(2,1)S(1)}, bf16[1,256,256]{2,1,0:T(8,128)(2,1)}, u32[]{:S(2)}) copy-start(bf16[1,256,256]{2,1,0:T(8,128)(2,1)} %param.9) | copy-start | bytes 393220
  23.0 23.0 %all-to-all-start = ((bf16[16,64,512]{2,1,0:T(8,128)(2,1)}), bf16[16,64,512]{2,1,0:T(8,128)(2,1)S(1)}, u32[]{:S(2)}, u32[]{:S(2)}) async-start(bf16[16,64,512]{2,1,0:T(8,128)(2,1)} %broadcast_in_dim.11), calls=%async_computation | async-start | bytes 2097152 | tf_op jit(solution)/shard_map/all_to_all | solution.py:32
  30.2 22.1 %collective-permute-start.2 = (bf16[256,256]{1,0:T(8,128)(2,1)S(1)}, bf16[256,256]{1,0:T(8,128)(2,1)S(1)}, u32[]{:S(2)}, u32[]{:S(2)}) collective-permute-start(bf16[256,256]{1,0:T(8,128)(2,1)S(1)} %bitcast.28), channel_id=1, source_target_pairs={{0,1},{1,0},{2,3},{3,2},{4,5},{5,4},{6,7},{7,6},{8,9},{9,8},{10,11... | collective-permute-start | bytes 393224 | tf_op jit(solution)/shard_map/ppermute | solution.py:23
  45.9 21.4 %all-to-all-start.1 = ((bf16[16,64,512]{2,1,0:T(8,128)(2,1)}), bf16[16,64,512]{2,1,0:T(8,128)(2,1)S(1)}, u32[]{:S(2)}, u32[]{:S(2)}) async-start(bf16[16,64,512]{2,1,0:T(8,128)(2,1)} %shard_map.95), calls=%async_computation.1 | async-start | bytes 2097152 | tf_op jit(solution)/shard_map/all_to_all | solution.py:32
  52.3 3.4 %collective-permute-start.4 = (bf16[256,512]{1,0:T(8,128)(2,1)S(1)}, bf16[256,512]{1,0:T(8,128)(2,1)S(1)}, u32[]{:S(2)}, u32[]{:S(2)}) collective-permute-start(bf16[256,512]{1,0:T(8,128)(2,1)S(1)} %pad_maximum_fusion), channel_id=1, source_target_pairs={{0,2},{2,0},{4,6},{6,4},{8,10},{10,8},{12,14},{14,12},{16,18},{18,... | collective-permute-start | bytes 786440 | tf_op jit(solution)/shard_map/ppermute | solution.py:43
  67.4 19.4 %all-to-all-start.3 = ((bf16[16,64,512]{2,1,0:T(8,128)(2,1)}), bf16[16,64,512]{2,1,0:T(8,128)(2,1)S(1)}, u32[]{:S(2)}, u32[]{:S(2)}) async-start(bf16[16,64,512]{2,1,0:T(8,128)(2,1)} %bitcast.34), calls=%async_computation.3 | async-start | bytes 2097152 | tf_op jit(solution)/shard_map/all_to_all | solution.py:32
  71.8 1.0 copy-start.2
  72.8 3.4 %collective-permute-start.1 = (bf16[256,512]{1,0:T(8,128)(2,1)S(1)}, bf16[256,512]{1,0:T(8,128)(2,1)S(1)}, u32[]{:S(2)}, u32[]{:S(2)}) collective-permute-start(bf16[256,512]{1,0:T(8,128)(2,1)S(1)} %fusion.3), channel_id=1, source_target_pairs={{0,2},{2,0},{4,6},{6,4},{8,10},{10,8},{12,14},{14,12},{16,18},{18,... | collective-permute-start | bytes 786440 | tf_op jit(solution)/shard_map/ppermute | solution.py:43
  86.8 1.0 copy-start
  91.0 55.7 %collective-permute-start.5 = (bf16[64,8192]{1,0:T(8,128)(2,1)}, bf16[64,8192]{1,0:T(8,128)(2,1)S(1)}, u32[]{:S(2)}, u32[]{:S(2)}) collective-permute-start(bf16[64,8192]{1,0:T(8,128)(2,1)} %shard_map.96), channel_id=1, source_target_pairs={{64,0},{128,64},{192,128},{256,192},{320,256},{384,320},{448,384},... | collective-permute-start | bytes 3145736 | tf_op jit(solution)/shard_map/ppermute | solution.py:19
  94.4 38.9 %collective-permute-start.3 = (bf16[272,256]{1,0:T(8,128)(2,1)S(1)}, bf16[272,256]{1,0:T(8,128)(2,1)S(1)}, u32[]{:S(2)}, u32[]{:S(2)}) collective-permute-start(bf16[272,256]{1,0:T(8,128)(2,1)S(1)} %pad_maximum_fusion.1), channel_id=1, source_target_pairs={{0,1},{1,0},{2,3},{3,2},{4,5},{5,4},{6,7},{7,6},{8,9},{9,8},{10,11... | collective-permute-start | bytes 417800 | tf_op jit(solution)/shard_map/ppermute | solution.py:23
  133.9 12.8 %all-to-all-start.2 = ((f32[32,1,256]{2,1,0:T(1,128)}), f32[32,1,256]{2,1,0:T(1,128)S(1)}, u32[]{:S(2)}, u32[]{:S(2)}) async-start(f32[32,1,256]{2,1,0:T(1,128)} %broadcast_in_dim.26), calls=%async_computation.2 | async-start | bytes 65536 | tf_op jit(solution)/shard_map/all_to_all | solution.py:200
